TPU v7x, 32 devices: a whole 2x2x4 slice. The times are simulated.
32 devices in a mesh: rows: 8 (over y, x, core), depth: 4 (over z).
Axes of the slice: x: 2, y: 2, z: 4, core: 2. Of those that a mesh axis runs over, the one named last changes fastest.
Arguments:
- left_factors: bfloat16 [8, 8, 2048, 128], P('rows', 'depth'), may hold values from -0.125 to 0.125
- right_factors: bfloat16 [8, 8, 2048, 128], P('rows', 'depth'), may hold values from -0.125 to 0.125
- probe_matrix: bfloat16 [2048, 128], replicated, may hold values from -6 to 6
- tile_list: int32 [8, 4], replicated, may hold values from 0 to 7, all different within a row
Outputs:
- basis: float32 [8, 4, 2048, 128], P('rows', None, 'depth')
- chol_factor: float32 [8, 4, 128, 128], P('rows')
Inputs may be any that keep to these rules, and one draw needn't show every extreme that they name: `tile_list`: each row holds 4 different tile rows, and every tile row is named by some row.
All inputs are finite; a program needn't handle non-finite values.
Results may differ from a plain program's by a relative error of at most 0.0058.
Values may be sent and summed in bfloat16 or wider, within the bound.
No kernel may reach another device: no remote copies, remote signals or barrier semaphores. Data moves between devices by JAX's collectives and lax.ppermute only.
A program may use at most 64 MiB of HBM per device.

v0:
```python
import functools
import math

import jax
import jax.numpy as jnp
from jax import lax
from jax.experimental import pallas as pl
from jax.experimental.pallas import tpu as pltpu
from jax.sharding import PartitionSpec as P


HIGHEST = lax.Precision.HIGHEST
BLOCK = 16
GRANT = 12 << 20
VMEM = pl.BlockSpec(memory_space=pltpu.VMEM)
ANY = pl.BlockSpec(memory_space=pl.ANY)
SMEM = pl.BlockSpec(memory_space=pltpu.SMEM)


def swap(x, axis, bits, size):
    return lax.ppermute(x, axis, [(i, i ^ bits) for i in range(size)])


def bits_of(size):
    return [1 << b for b in range(size.bit_length() - 1)]


def gather_rows(halves, axis, size):
    known = {0: halves}
    bits = bits_of(size)
    pairs = bits[len(bits) % 2:]
    late = 0
    for a, b in zip(pairs[::2], pairs[1::2]):
        fresh = {}
        for o, (low, high) in known.items():
            a_low, a_high = swap(low, axis, a, size), swap(high, axis, a, size)
            b_low, b_high = swap(low, axis, b, size), swap(high, axis, b, size)
            fresh[o ^ a] = (a_low, a_high)
            fresh[o ^ b] = (b_low, b_high)
            fresh[o ^ a ^ b] = (swap(b_low, axis, a, size), swap(a_high, axis, b, size))
        known.update(fresh)
        late = a ^ b
    return known, [o for o in known if late and o & late == late]


def gather_depth(x, axis, size):
    known = {0: x}
    for b in reversed(bits_of(size)):
        fresh = {}
        for o, v in known.items():
            fresh[o ^ b] = swap(v, axis, b, size)
        known.update(fresh)
    return known


def fetch(pairs, sems):
    copies = [pltpu.make_async_copy(src, dst, sems.at[n]) for n, (src, dst) in enumerate(pairs)]
    for copy in copies:
        copy.start()
    return copies


def first_kernel(panels, left_ref, right_ref, probe_ref, *refs):
    outs, (probe_buf, left_buf, right_buf, sems) = refs[:2 * panels], refs[2 * panels:]
    sources = [(probe_ref, probe_buf)]
    for p in range(panels):
        sources += [(left_ref.at[0, p], left_buf.at[p]), (right_ref.at[0, p], right_buf.at[p])]
    copies = fetch(sources, sems)
    copies[0].wait()
    probe_turned = probe_buf[...].T
    for p in range(panels):
        copies[1 + 2 * p].wait()
        image = jnp.dot(
            probe_turned, left_buf[p], preferred_element_type=jnp.float32
        ).astype(jnp.bfloat16)
        copies[2 + 2 * p].wait()
        half = outs[0].shape[0]
        for h in range(2):
            outs[2 * p + h][...] = lax.dot_general(
                right_buf[p, h * half:(h + 1) * half], image, (((1,), (1,)), ((), ())),
                preferred_element_type=jnp.float32,
            ).astype(jnp.bfloat16)


def turn_kernel(right_ref, turned_ref):
    for p in range(turned_ref.shape[0]):
        turned_ref[p] = right_ref[0, p].T


def couple(turned_refs, panel, blocks):
    half = blocks[0][0].shape[0]
    total = None
    for h in range(2):
        left = [ref[panel, :, h * half:(h + 1) * half] for ref in turned_refs]
        left = jnp.concatenate(left, axis=0) if len(left) > 1 else left[0]
        right = [block[h][...] for block in blocks]
        right = jnp.concatenate(right, axis=1) if len(right) > 1 else right[0]
        term = jnp.dot(left, right, preferred_element_type=jnp.float32)
        total = term if total is None else total + term
    return total.astype(jnp.bfloat16)


def early_kernel(panel, sides, count, *refs):
    turned_refs, block_refs, outs = refs[:sides], refs[sides:-sides], refs[-sides:]
    rank, width = outs[0].shape[1:]
    for first in range(0, count, 2):
        blocks = range(first, min(first + 2, count))
        found = couple(turned_refs, panel, [block_refs[2 * n:2 * n + 2] for n in blocks])
        for i, n in enumerate(blocks):
            for s in range(sides):
                outs[s][n] = found[s * rank:(s + 1) * rank, i * width:(i + 1) * width]


def late_kernel(panel, early, late, wanted_ref, turned_ref, *refs):
    sides, count = len(early), len(late)
    early_refs, block_refs = refs[:sides], refs[sides:sides + 2 * count]
    out_ref, every_ref = refs[sides + 2 * count:]
    for s, offsets in enumerate(early):
        for n, o in enumerate(offsets):
            every_ref[o] = early_refs[s][n]
    width = every_ref.shape[2]
    for first in range(0, count, 2):
        blocks = range(first, min(first + 2, count))
        found = couple([turned_ref], panel, [block_refs[2 * n:2 * n + 2] for n in blocks])
        for i, n in enumerate(blocks):
            every_ref[late[n]] = found[:, i * width:(i + 1) * width]
    for t in range(out_ref.shape[1] // width):
        out_ref[:, t * width:(t + 1) * width] = every_ref[wanted_ref[t]]


def partial_sketch(panel, left_refs, coupling_refs):
    total = None
    step = 2 if len(left_refs) % 2 == 0 else 1
    for o in range(0, len(left_refs), step):
        left = jnp.concatenate([left_refs[o + i][panel] for i in range(step)], axis=1)
        coupling = jnp.concatenate([coupling_refs[o + i][...] for i in range(step)], axis=0)
        term = jnp.dot(left, coupling, preferred_element_type=jnp.float32)
        total = term if total is None else total + term
    return total


def part_kernel(count, panel, *refs):
    total = partial_sketch(panel, refs[:count], refs[count:2 * count])
    if len(refs) > 2 * count + 1:
        total = total + refs[2 * count][...]
    refs[-1][...] = total


def sketch_kernel(count, panel, *refs):
    sketch_ref, gram_ref = refs[-2:]
    total = partial_sketch(panel, refs[:count], refs[count:2 * count])
    if len(refs) > 2 * count + 2:
        total = total + refs[2 * count][...]
    listed, packed, width = gram_ref.shape
    half = width // 2
    lane = lax.broadcasted_iota(jnp.int32, (half, width), 1)
    row = lax.broadcasted_iota(jnp.int32, (half, width), 0)
    for t in range(listed):
        tile = total[:, t * width:(t + 1) * width]
        sketch_ref[t] = tile
        gram = lax.dot_general(
            tile, tile, (((0,), (0,)), ((), ())), precision=HIGHEST,
            preferred_element_type=jnp.float32,
        )
        lower = gram[half:]
        gram_ref[t, :half] = jnp.where(lane < row, pltpu.roll(lower, half, axis=1), gram[:half])
        diagonal = jnp.sum(jnp.where(lane == row + half, lower, 0.0), axis=0, keepdims=True)
        gram_ref[t, half:] = jnp.broadcast_to(diagonal, (packed - half, width))


def unpacked(packed, half):
    width = packed.shape[1]
    lane = lax.broadcasted_iota(jnp.int32, (half, width), 1)
    row = lax.broadcasted_iota(jnp.int32, (half, width), 0)
    upper = packed[:half]
    moved = pltpu.roll(upper, half, axis=1)
    diagonal = jnp.broadcast_to(packed[half:half + 1], (half, width))
    strict = jnp.concatenate(
        [jnp.where(lane > row, upper, 0.0),
         jnp.where((lane >= half) & (lane < row + half), moved, 0.0)], axis=0)
    center = jnp.concatenate(
        [jnp.where(lane == row, upper, 0.0),
         jnp.where(lane == row + half, diagonal, 0.0)], axis=0)
    return strict + strict.T + center


def eliminate(panel, first, lane, sub):
    cols = [
        jnp.broadcast_to(panel[:, first + j:first + j + 1], panel.shape) for j in range(BLOCK)
    ]
    upper = jnp.zeros_like(panel)
    inverse = jnp.zeros_like(panel)
    pivots = jnp.zeros_like(panel)
    for j in range(BLOCK):
        k = first + j
        pivot = jnp.broadcast_to(cols[j][j:j + 1, :], panel.shape)
        recip = 1.0 / pivot
        root = lax.rsqrt(pivot)
        factor = jnp.where(sub > j, cols[j] * recip, 0.0)
        for c in range(j + 1, BLOCK):
            cols[c] = cols[c] - factor * jnp.broadcast_to(cols[c][j:j + 1, :], panel.shape)
        row = jnp.broadcast_to(panel[j:j + 1, :], panel.shape)
        here = sub == j
        upper = jnp.where(here & (lane >= k), row * root, upper)
        row = jnp.where(lane == k, 1.0, row)
        inverse = jnp.where(here & (lane <= k), row * root, inverse)
        pivots = jnp.where(here, recip, pivots)
        panel = jnp.where((lane == k) & (sub >= j), jnp.where(here, 1.0, 0.0), panel)
        panel = panel - factor * row
    below = jnp.where(lane >= first + BLOCK, panel * pivots, 0.0)
    panel = jnp.where((lane < first + BLOCK) & (lane > first + sub), 0.0, panel)
    return panel, below, upper, inverse


def factor_kernel(scale, own_ref, other_ref, sketch_ref, basis_ref, chol_ref, work_ref, upper_ref, inverse_ref):
    listed, width, _ = work_ref.shape
    for t in range(listed):
        work_ref[t] = unpacked(own_ref[t] + other_ref[t], width // 2)
    lane = lax.broadcasted_iota(jnp.int32, (BLOCK, width), 1)
    sub = lax.broadcasted_iota(jnp.int32, (BLOCK, width), 0)
    for first in range(0, width, BLOCK):
        last = first + BLOCK
        done = [eliminate(work_ref[t, first:last, :], first, lane, sub) for t in range(listed)]
        for t in range(listed):
            rows, below, upper, inverse = done[t]
            upper_ref[t, first:last, :] = upper
            inverse_ref[t, first:last, :] = inverse * scale
            if last < width:
                at = lax.broadcasted_iota(jnp.int32, (width - last, width), 1)
                old = work_ref[t, last:, :]
                old = jnp.where((at >= first) & (at < last), 0.0, old)
                update = lax.dot_general(
                    below, rows, (((0,), (0,)), ((), ())), precision=HIGHEST,
                    preferred_element_type=jnp.float32,
                )
                work_ref[t, last:, :] = old - update[last:, :]
    for t in range(listed):
        chol_ref[t] = upper_ref[t].T * (1.0 / scale)
        basis_ref[t] = lax.dot_general(
            sketch_ref[t], inverse_ref[t], (((1,), (1,)), ((), ())), precision=HIGHEST,
            preferred_element_type=jnp.float32,
        )


def call(kernel, shapes, *args, in_specs=None, leave=False, **more):
    specs = in_specs or [VMEM] * len(args)
    args = [
        pltpu.with_memory_space_constraint(x, pltpu.VMEM) if spec is VMEM else x
        for x, spec in zip(args, specs)
    ]
    if not leave:
        shapes = jax.tree.map(lambda s: pltpu.VMEM(s.shape, s.dtype), shapes)
    out = VMEM if not isinstance(shapes, tuple) else (VMEM,) * len(shapes)
    params = pltpu.CompilerParams(vmem_limit_bytes=GRANT)
    return pl.pallas_call(
        kernel, out_shape=shapes, in_specs=specs, out_specs=out, compiler_params=params, **more
    )(*args)


def on_device(rows_size, depth_size, left_factors, right_factors, probe_matrix, tile_list):
    _, panels, tile_size, rank_size = left_factors.shape
    listed = tile_list.shape[1]
    width = probe_matrix.shape[1]
    scale = math.sqrt(float(tile_size))
    me = lax.axis_index("rows")
    level = lax.axis_index("depth")
    part = tile_size // depth_size
    half = tile_size // 2
    bf16, f32 = jnp.bfloat16, jnp.float32
    shape = jax.ShapeDtypeStruct

    single = len(bits_of(rows_size)) % 2
    halves = call(
        functools.partial(first_kernel, panels), (shape((half, width), bf16),) * (2 * panels),
        left_factors, right_factors, probe_matrix, in_specs=[ANY] * 3,
        scratch_shapes=[
            pltpu.VMEM((tile_size, width), bf16),
            pltpu.VMEM((panels, tile_size, rank_size), bf16),
            pltpu.VMEM((panels, tile_size, rank_size), bf16),
            pltpu.SemaphoreType.DMA((1 + 2 * panels,)),
        ],
    )
    turned = [call(
        turn_kernel, shape((panels, rank_size, tile_size), bf16), right_factors,
        in_specs=[pl.BlockSpec(right_factors.shape)],
    )]
    if single:
        turned.append(swap(turned[0], "rows", 1, rows_size))
    found, late = [], []
    for p in range(panels):
        blocks, last = gather_rows(halves[2 * p:2 * p + 2], "rows", rows_size)
        found.append(blocks)
        late.append(last)

    blocks = left_factors[0].reshape(panels, depth_size, part, rank_size)
    lefts = []
    for o in range(depth_size):
        block = lax.dynamic_index_in_dim(blocks, level ^ o, 1, keepdims=False)
        lefts.append(swap(block, "depth", o, depth_size) if o else block)

    wanted = lax.dynamic_index_in_dim(tile_list, me, 0, keepdims=False) ^ me
    gathered = []
    for p in range(panels):
        last = late[p]
        early = [o for o in found[p] if o not in last]
        sides = 1 + single
        args = [h for o in early for h in found[p][o]]
        first = call(
            functools.partial(early_kernel, p, sides, len(early)),
            (shape((len(early), rank_size, width), bf16),) * sides,
            *turned, *args,
        )
        coupled, offsets = [first[0]], [early]
        if single:
            coupled.append(swap(first[1], "rows", 1, rows_size))
            offsets.append([o ^ 1 for o in early])
        rest = [h for o in last for h in found[p][o]]
        if single:
            rest += [swap(h, "rows", 1, rows_size) for h in rest]
            last = last + [o ^ 1 for o in last]
        coupling = call(
            functools.partial(late_kernel, p, offsets, last),
            shape((rank_size, listed * width), bf16),
            wanted, turned[0], *coupled, *rest,
            in_specs=[SMEM] + [VMEM] * (1 + len(coupled) + len(rest)),
            scratch_shapes=[pltpu.VMEM((rows_size, rank_size, width), bf16)],
        )
        every = gather_depth(coupling, "depth", depth_size)
        gathered.append([every[o] for o in range(depth_size)])

    total = []
    for p in range(panels - 1):
        total = [call(
            functools.partial(part_kernel, depth_size, p),
            shape((part, listed * width), f32), *lefts, *gathered[p], *total,
        )]
    packed = width // 2 + 8
    sketch, gram = call(
        functools.partial(sketch_kernel, depth_size, panels - 1),
        (shape((listed, part, width), f32), shape((listed, packed, width), f32)),
        *lefts, *gathered[-1], *total,
    )
    other = jnp.zeros_like(gram)
    for b in bits_of(depth_size):
        gram = gram + other
        other = swap(gram, "depth", b, depth_size)
    basis, chol_factor = call(
        functools.partial(factor_kernel, scale),
        (shape((listed, part, width), f32), shape((listed, width, width), f32)),
        gram, other, sketch, leave=True,
        scratch_shapes=[pltpu.VMEM((listed, width, width), f32)] * 3,
    )
    return (basis[None], chol_factor[None])


def solution(mesh):
    in_specs = (P("rows", "depth", None, None), P("rows", "depth", None, None), P(), P())
    out_specs = (P("rows", None, "depth", None), P("rows", None, None, None))

    def body(*args):
        return on_device(mesh.shape["rows"], mesh.shape["depth"], *args)

    return jax.shard_map(body, mesh=mesh, in_specs=in_specs, out_specs=out_specs, check_vma=False)
```

profile of v0, /device:TPU:0, one launch (start us, length us, event | category | flops | bytes accessed | tf_op | source)
XLA Modules:
  0.0 121.8 jit_solution(16185681144935728926)
XLA Ops:
  0.6 1.3 %copy-done.1 = bf16[1,2,2048,128]{3,2,1,0:T(8,128)(2,1)S(1)} copy-done((bf16[1,2,2048,128]{3,2,1,0:T(8,128)(2,1)S(1)}, bf16[1,2,2048,128]{3,2,1,0:T(8,128)(2,1)}, u32[]{:S(2)}) %copy-start.1) | copy-done | bytes 1048600
  2.3 0.6 collective-permute-start.3
  2.8 0.4 copy-done.2
  3.2 1.0 copy-done.3
  4.3 1.6 %shard_map.60 = (bf16[1024,128]{1,0:T(8,128)(2,1)S(1)}, bf16[1024,128]{1,0:T(8,128)(2,1)S(1)}, bf16[1024,128]{1,0:T(8,128)(2,1)S(1)}, bf16[1024,128]{1,0:T(8,128)(2,1)S(1)}) custom-call(bf16[1,2,2048,128]{3,2,1,0:T(8,128)(2,1)S(1)} %copy-done, bf16[1,2,2048,128]{3,2,1,0:T(8,128)(2,1)S(1)} %copy-done.2, bf16[2048,128]{1,0:T(8,128)(2,1)S(1)} %copy-done.3), custom_call_target="tpu_custom_call" | custom-call | tf_op jit(solution)/shard_map/pallas_call | solution.py:255
  5.9 3.0 %collective-permute-start.4 = (bf16[1024,128]{1,0:T(8,128)(2,1)S(1)}, bf16[1024,128]{1,0:T(8,128)(2,1)S(1)}, u32[]{:S(2)}, u32[]{:S(2)}) collective-permute-start(bf16[1024,128]{1,0:T(8,128)(2,1)S(1)} %get-tuple-element.14.refs_2_), channel_id=1, source_target_pairs={{0,8},{4,12},{8,0},{12,4},{16,24},{20,28},{24,16},{28,20},{1,9},{5... | collective-permute-start | bytes 786440 | tf_op jit(solution)/shard_map/ppermute | solution.py:21
  9.0 2.0 %collective-permute-start.6 = (bf16[1024,128]{1,0:T(8,128)(2,1)S(1)}, bf16[1024,128]{1,0:T(8,128)(2,1)}, u32[]{:S(2)}, u32[]{:S(2)}) collective-permute-start(bf16[1024,128]{1,0:T(8,128)(2,1)S(1)} %get-tuple-element.14.refs_2_), channel_id=1, source_target_pairs={{0,16},{4,20},{8,24},{12,28},{16,0},{20,4},{24,8},{28,12},{1,17},{... | collective-permute-start | bytes 786440 | tf_op jit(solution)/shard_map/ppermute | solution.py:21
  11.0 0.7 copy-done.4
  11.7 4.3 %collective-permute-done.4.refs_4_ = bf16[1024,128]{1,0:T(8,128)(2,1)S(1)} collective-permute-done((bf16[1024,128]{1,0:T(8,128)(2,1)S(1)}, bf16[1024,128]{1,0:T(8,128)(2,1)S(1)}, u32[]{:S(2)}, u32[]{:S(2)}) %collective-permute-start.4) | collective-permute-done | bytes 262176 | tf_op jit(solution)/shard_map/ppermute | solution.py:21
  16.1 0.7 copy-done.8
  16.8 2.0 %collective-permute-start.17 = (bf16[1024,128]{1,0:T(8,128)(2,1)S(1)}, bf16[1024,128]{1,0:T(8,128)(2,1)S(1)}, u32[]{:S(2)}, u32[]{:S(2)}) collective-permute-start(bf16[1024,128]{1,0:T(8,128)(2,1)S(1)} %get-tuple-element.19.refs_3_), channel_id=1, source_target_pairs={{0,8},{4,12},{8,0},{12,4},{16,24},{20,28},{24,16},{28,20},{1,9},{5... | collective-permute-start | bytes 786440 | tf_op jit(solution)/shard_map/ppermute | solution.py:21
  18.8 3.0 %collective-permute-done.5.refs_5_ = bf16[1024,128]{1,0:T(8,128)(2,1)} collective-permute-done((bf16[1024,128]{1,0:T(8,128)(2,1)S(1)}, bf16[1024,128]{1,0:T(8,128)(2,1)}, u32[]{:S(2)}, u32[]{:S(2)}) %collective-permute-start.5) | collective-permute-done | bytes 262176 | tf_op jit(solution)/shard_map/ppermute | solution.py:21
  21.8 2.0 %collective-permute-start.16 = (bf16[1024,128]{1,0:T(8,128)(2,1)S(1)}, bf16[1024,128]{1,0:T(8,128)(2,1)S(1)}, u32[]{:S(2)}, u32[]{:S(2)}) collective-permute-start(bf16[1024,128]{1,0:T(8,128)(2,1)S(1)} %get-tuple-element.18.refs_2_), channel_id=1, source_target_pairs={{0,8},{4,12},{8,0},{12,4},{16,24},{20,28},{24,16},{28,20},{1,9},{5... | collective-permute-start | bytes 786440 | tf_op jit(solution)/shard_map/ppermute | solution.py:21
  23.8 0.7 copy-done.10
  24.5 1.5 %collective-permute-start.19 = (bf16[1024,128]{1,0:T(8,128)(2,1)S(1)}, bf16[1024,128]{1,0:T(8,128)(2,1)S(1)}, u32[]{:S(2)}, u32[]{:S(2)}) collective-permute-start(bf16[1024,128]{1,0:T(8,128)(2,1)S(1)} %get-tuple-element.19.refs_3_), channel_id=1, source_target_pairs={{0,16},{4,20},{8,24},{12,28},{16,0},{20,4},{24,8},{28,12},{1,17},{... | collective-permute-start | bytes 786440 | tf_op jit(solution)/shard_map/ppermute | solution.py:21
  26.0 0.7 copy-done.12
  26.7 0.5 collective-permute-start.21
  27.3 0.7 copy-done.14
  28.0 1.4 %collective-permute-start.22 = (bf16[1024,128]{1,0:T(8,128)(2,1)S(1)}, bf16[1024,128]{1,0:T(8,128)(2,1)}, u32[]{:S(2)}, u32[]{:S(2)}) collective-permute-start(bf16[1024,128]{1,0:T(8,128)(2,1)S(1)} %collective-permute-done.17.refs_5_), channel_id=1, source_target_pairs={{0,16},{4,20},{8,24},{12,28},{16,0},{20,4},{24,8},{28,12},{1,17},{... | collective-permute-start | bytes 786440 | tf_op jit(solution)/shard_map/ppermute | solution.py:21
  29.3 0.7 copy-done.16
  30.0 2.9 %collective-permute-done.16.refs_4_ = bf16[1024,128]{1,0:T(8,128)(2,1)S(1)} collective-permute-done((bf16[1024,128]{1,0:T(8,128)(2,1)S(1)}, bf16[1024,128]{1,0:T(8,128)(2,1)S(1)}, u32[]{:S(2)}, u32[]{:S(2)}) %collective-permute-start.16) | collective-permute-done | bytes 262176 | tf_op jit(solution)/shard_map/ppermute | solution.py:21
  32.9 0.7 copy-done.18
  33.6 2.0 %collective-permute-start.9 = (bf16[1024,128]{1,0:T(8,128)(2,1)}, bf16[1024,128]{1,0:T(8,128)(2,1)}, u32[]{:S(2)}, u32[]{:S(2)}) collective-permute-start(bf16[1024,128]{1,0:T(8,128)(2,1)} %collective-permute-done.6.refs_6_), channel_id=1, source_target_pairs={{0,8},{4,12},{8,0},{12,4},{16,24},{20,28},{24,16},{28,20},{1,9},{5... | collective-permute-start | bytes 786440 | tf_op jit(solution)/shard_map/ppermute | solution.py:21
  35.6 0.7 copy-done.20
  36.4 1.5 %collective-permute-start.10 = (bf16[1024,128]{1,0:T(8,128)(2,1)}, bf16[1024,128]{1,0:T(8,128)(2,1)}, u32[]{:S(2)}, u32[]{:S(2)}) collective-permute-start(bf16[1024,128]{1,0:T(8,128)(2,1)} %collective-permute-done.5.refs_5_), channel_id=1, source_target_pairs={{0,16},{4,20},{8,24},{12,28},{16,0},{20,4},{24,8},{28,12},{1,17},{... | collective-permute-start | bytes 786440 | tf_op jit(solution)/shard_map/ppermute | solution.py:21
  37.9 0.8 collective-permute-done.21.refs_2_
  38.6 2.0 %collective-permute-start.7 = (bf16[1024,128]{1,0:T(8,128)(2,1)S(1)}, bf16[1024,128]{1,0:T(8,128)(2,1)}, u32[]{:S(2)}, u32[]{:S(2)}) collective-permute-start(bf16[1024,128]{1,0:T(8,128)(2,1)S(1)} %get-tuple-element.15.refs_3_), channel_id=1, source_target_pairs={{0,16},{4,20},{8,24},{12,28},{16,0},{20,4},{24,8},{28,12},{1,17},{... | collective-permute-start | bytes 786440 | tf_op jit(solution)/shard_map/ppermute | solution.py:21
  40.7 0.7 copy-done.6
  41.4 0.5 collective-permute-start.24
  41.9 0.9 copy-done.11
  42.9 0.9 copy-done.13
  43.8 0.9 copy-done.15
  44.8 0.9 copy-done.17
  45.7 0.9 copy-done.19
  46.7 0.9 copy-done.21
  47.6 0.7 shard_map.63
  48.5 0.4 collective-permute-start.12
  49.0 0.9 dynamic-slice_bitcast_fusion
  49.9 1.6 %collective-permute-start = (bf16[2,512,128]{2,1,0:T(8,128)(2,1)}, bf16[2,512,128]{2,1,0:T(8,128)(2,1)S(1)}, u32[]{:S(2)}, u32[]{:S(2)}) collective-permute-start(bf16[2,512,128]{2,1,0:T(8,128)(2,1)} %get-tuple-element.28), channel_id=1, source_target_pairs={{0,1},{1,0},{2,3},{3,2},{4,5},{5,4},{6,7},{7,6},{8,9},{9,8},{10,11... | collective-permute-start | bytes 786440 | tf_op jit(solution)/shard_map/ppermute | solution.py:21
  51.5 2.6 %collective-permute-start.1 = (bf16[2,512,128]{2,1,0:T(8,128)(2,1)}, bf16[2,512,128]{2,1,0:T(8,128)(2,1)S(1)}, u32[]{:S(2)}, u32[]{:S(2)}) collective-permute-start(bf16[2,512,128]{2,1,0:T(8,128)(2,1)} %get-tuple-element.27), channel_id=1, source_target_pairs={{0,2},{1,3},{2,0},{3,1},{4,6},{5,7},{6,4},{7,5},{8,10},{9,11},{10,... | collective-permute-start | bytes 786440 | tf_op jit(solution)/shard_map/ppermute | solution.py:21
  54.1 2.4 %shard_map.61 = (bf16[3,128,128]{2,1,0:T(8,128)(2,1)S(1)}, bf16[3,128,128]{2,1,0:T(8,128)(2,1)}) custom-call(bf16[2,128,2048]{2,1,0:T(8,128)(2,1)S(1)} %shard_map.59.refs_0_.turned_ref, bf16[2,128,2048]{2,1,0:T(8,128)(2,1)S(1)} %collective-permute-done.3.refs_1_, bf16[1024,128]{1,0:T(8,128)(2,1)S(1)} %copy-done.5, bf16[1024,128]{1,0:T(8,128)(2,1)S(1)} %copy-done.7, ...), custom_call_target="tpu_custom_call" | custom-call | tf_op jit(solution)/shard_map/pallas_call | solution.py:255
  56.5 0.6 copy-done.24
  57.2 0.6 copy-done.22
  57.8 0.7 copy-done.27
  58.7 0.9 copy-done.23
  59.6 1.6 %shard_map.64.refs_4_ = bf16[128,512]{1,0:T(8,128)(2,1)S(1)} custom-call(s32[4]{0:T(128)S(1)} %xor_reduce_fusion.wanted_ref, bf16[2,128,2048]{2,1,0:T(8,128)(2,1)S(1)} %shard_map.59.refs_0_.turned_ref, bf16[3,128,128]{2,1,0:T(8,128)(2,1)S(1)} %get-tuple-element.20.refs_0_, bf16[3,128,128]{2,1,0:T(8,128)(2,1)S(1)} %copy-done.23, ...), custom_call_target="tpu_custom_call" | custom-call | tf_op jit(solution)/shard_map/pallas_call | solution.py:255
  61.2 0.4 collective-permute-start.2
  61.6 1.6 %collective-permute-start.26 = (bf16[128,512]{1,0:T(8,128)(2,1)S(1)}, bf16[128,512]{1,0:T(8,128)(2,1)S(1)}, u32[]{:S(2)}, u32[]{:S(2)}) collective-permute-start(bf16[128,512]{1,0:T(8,128)(2,1)S(1)} %shard_map.64.refs_4_), channel_id=1, source_target_pairs={{0,2},{1,3},{2,0},{3,1},{4,6},{5,7},{6,4},{7,5},{8,10},{9,11},{10,... | collective-permute-start | bytes 393224 | tf_op jit(solution)/shard_map/ppermute | solution.py:21
  63.1 1.5 %shard_map.62.refs_4_ = bf16[128,512]{1,0:T(8,128)(2,1)S(1)} custom-call(s32[4]{0:T(128)S(1)} %xor_reduce_fusion.wanted_ref, bf16[2,128,2048]{2,1,0:T(8,128)(2,1)S(1)} %shard_map.59.refs_0_.turned_ref, bf16[3,128,128]{2,1,0:T(8,128)(2,1)S(1)} %copy-done.25, bf16[3,128,128]{2,1,0:T(8,128)(2,1)S(1)} %collective-permute-done.8.refs_1_, ...), custom_call_target="tpu_custom_call" | custom-call | tf_op jit(solution)/shard_map/pallas_call | solution.py:255
  64.7 1.4 %collective-permute-start.14 = (bf16[128,512]{1,0:T(8,128)(2,1)S(1)}, bf16[128,512]{1,0:T(8,128)(2,1)S(1)}, u32[]{:S(2)}, u32[]{:S(2)}) collective-permute-start(bf16[128,512]{1,0:T(8,128)(2,1)S(1)} %shard_map.62.refs_4_), channel_id=1, source_target_pairs={{0,2},{1,3},{2,0},{3,1},{4,6},{5,7},{6,4},{7,5},{8,10},{9,11},{10,... | collective-permute-start | bytes 393224 | tf_op jit(solution)/shard_map/ppermute | solution.py:21
  66.1 1.2 %collective-permute-start.25 = (bf16[128,512]{1,0:T(8,128)(2,1)S(1)}, bf16[128,512]{1,0:T(8,128)(2,1)S(1)}, u32[]{:S(2)}, u32[]{:S(2)}) collective-permute-start(bf16[128,512]{1,0:T(8,128)(2,1)S(1)} %shard_map.64.refs_4_), channel_id=1, source_target_pairs={{0,1},{1,0},{2,3},{3,2},{4,5},{5,4},{6,7},{7,6},{8,9},{9,8},{10,11... | collective-permute-start | bytes 393224 | tf_op jit(solution)/shard_map/ppermute | solution.py:21
  67.3 19.1 %collective-permute-done.26.refs_6_ = bf16[128,512]{1,0:T(8,128)(2,1)S(1)} collective-permute-done((bf16[128,512]{1,0:T(8,128)(2,1)S(1)}, bf16[128,512]{1,0:T(8,128)(2,1)S(1)}, u32[]{:S(2)}, u32[]{:S(2)}) %collective-permute-start.26) | collective-permute-done | bytes 131104 | tf_op jit(solution)/shard_map/ppermute | solution.py:21
  86.4 0.4 collective-permute-start.27
  86.8 1.7 %collective-permute-start.13 = (bf16[128,512]{1,0:T(8,128)(2,1)S(1)}, bf16[128,512]{1,0:T(8,128)(2,1)S(1)}, u32[]{:S(2)}, u32[]{:S(2)}) collective-permute-start(bf16[128,512]{1,0:T(8,128)(2,1)S(1)} %shard_map.62.refs_4_), channel_id=1, source_target_pairs={{0,1},{1,0},{2,3},{3,2},{4,5},{5,4},{6,7},{7,6},{8,9},{9,8},{10,11... | collective-permute-start | bytes 393224 | tf_op jit(solution)/shard_map/ppermute | solution.py:21
  88.4 0.7 collective-permute-done.14.refs_6_
  89.1 3.6 %collective-permute-done.27.refs_7_ = bf16[128,512]{1,0:T(8,128)(2,1)S(1)} collective-permute-done((bf16[128,512]{1,0:T(8,128)(2,1)S(1)}, bf16[128,512]{1,0:T(8,128)(2,1)S(1)}, u32[]{:S(2)}, u32[]{:S(2)}) %collective-permute-start.27) | collective-permute-done | bytes 131104 | tf_op jit(solution)/shard_map/ppermute | solution.py:21
  92.8 0.4 shard_map.65.refs_8_
  93.2 2.4 %collective-permute-done.13.refs_5_ = bf16[128,512]{1,0:T(8,128)(2,1)S(1)} collective-permute-done((bf16[128,512]{1,0:T(8,128)(2,1)S(1)}, bf16[128,512]{1,0:T(8,128)(2,1)S(1)}, u32[]{:S(2)}, u32[]{:S(2)}) %collective-permute-start.13) | collective-permute-done | bytes 131104 | tf_op jit(solution)/shard_map/ppermute | solution.py:21
  95.6 2.0 %collective-permute-done.15.refs_7_ = bf16[128,512]{1,0:T(8,128)(2,1)S(1)} collective-permute-done((bf16[128,512]{1,0:T(8,128)(2,1)S(1)}, bf16[128,512]{1,0:T(8,128)(2,1)S(1)}, u32[]{:S(2)}, u32[]{:S(2)}) %collective-permute-start.15) | collective-permute-done | bytes 131104 | tf_op jit(solution)/shard_map/ppermute | solution.py:21
  97.5 1.5 %shard_map.66 = (f32[4,512,128]{2,1,0:T(8,128)S(1)}, f32[4,72,128]{2,1,0:T(8,128)S(1)}) custom-call(bf16[2,512,128]{2,1,0:T(8,128)(2,1)S(1)} %get-tuple-element.29.refs_0_, bf16[2,512,128]{2,1,0:T(8,128)(2,1)S(1)} %collective-permute-done.refs_1_, bf16[2,512,128]{2,1,0:T(8,128)(2,1)S(1)} %collective-permute-done.1.refs_2_, ...), custom_call_target="tpu_custom_call" | custom-call | tf_op jit(solution)/shard_map/pallas_call | solution.py:255
  99.2 5.1 %collective-permute-done.28 = f32[4,72,128]{2,1,0:T(8,128)S(1)} collective-permute-done((f32[4,72,128]{2,1,0:T(8,128)S(1)}, f32[4,72,128]{2,1,0:T(8,128)S(1)}, u32[]{:S(2)}, u32[]{:S(2)}) %collective-permute-start.28) | collective-permute-done | bytes 147488 | tf_op jit(solution)/shard_map/ppermute | solution.py:21
  104.3 1.1 collective-permute-start.29
  105.4 6.9 %collective-permute-done.29.other_ref = f32[4,72,128]{2,1,0:T(8,128)S(1)} collective-permute-done((f32[4,72,128]{2,1,0:T(8,128)S(1)}, f32[4,72,128]{2,1,0:T(8,128)S(1)}, u32[]{:S(2)}, u32[]{:S(2)}) %collective-permute-start.29) | collective-permute-done | bytes 147488 | tf_op jit(solution)/shard_map/ppermute | solution.py:21
  112.3 9.5 %shard_map.67 = (f32[4,512,128]{2,1,0:T(8,128)}, f32[4,128,128]{2,1,0:T(8,128)}) custom-call(f32[4,72,128]{2,1,0:T(8,128)S(1)} %add.25.own_ref, f32[4,72,128]{2,1,0:T(8,128)S(1)} %collective-permute-done.29.other_ref, f32[4,512,128]{2,1,0:T(8,128)S(1)} %get-tuple-element.23.sketch_ref), custom_call_target="tpu_custom_call" | custom-call | tf_op jit(solution)/shard_map/pallas_call | solution.py:255
  (64 shorter events, 1.1 us)
Async XLA Ops:
  0.6 2.2 %copy-start = (bf16[1,2,2048,128]{3,2,1,0:T(8,128)(2,1)S(1)}, bf16[1,2,2048,128]{3,2,1,0:T(8,128)(2,1)}, u32[]{:S(2)}) copy-start(bf16[1,2,2048,128]{3,2,1,0:T(8,128)(2,1)} %left_ref.1) | copy-start | bytes 3145732
  0.6 1.3 %copy-start.1 = (bf16[1,2,2048,128]{3,2,1,0:T(8,128)(2,1)S(1)}, bf16[1,2,2048,128]{3,2,1,0:T(8,128)(2,1)}, u32[]{:S(2)}) copy-start(bf16[1,2,2048,128]{3,2,1,0:T(8,128)(2,1)} %right_ref.3) | copy-start | bytes 3145732
  2.0 1.3 %copy-start.2 = (bf16[1,2,2048,128]{3,2,1,0:T(8,128)(2,1)S(1)}, bf16[1,2,2048,128]{3,2,1,0:T(8,128)(2,1)}, u32[]{:S(2)}) copy-start(bf16[1,2,2048,128]{3,2,1,0:T(8,128)(2,1)} %right_ref.3) | copy-start | bytes 3145732
  2.3 39.1 %collective-permute-start.3 = (bf16[2,128,2048]{2,1,0:T(8,128)(2,1)S(1)}, bf16[2,128,2048]{2,1,0:T(8,128)(2,1)S(1)}, u32[]{:S(2)}, u32[]{:S(2)}) collective-permute-start(bf16[2,128,2048]{2,1,0:T(8,128)(2,1)S(1)} %shard_map.59.refs_0_.turned_ref), channel_id=1, source_target_pairs={{0,4},{4,0},{8,12},{12,8},{16,20},{20,16},{24,28},{28,24},{1,5},{5... | collective-permute-start | bytes 3145736 | tf_op jit(solution)/shard_map/ppermute | solution.py:21
  3.2 1.0 copy-start.3
  5.9 10.2 %collective-permute-start.4 = (bf16[1024,128]{1,0:T(8,128)(2,1)S(1)}, bf16[1024,128]{1,0:T(8,128)(2,1)S(1)}, u32[]{:S(2)}, u32[]{:S(2)}) collective-permute-start(bf16[1024,128]{1,0:T(8,128)(2,1)S(1)} %get-tuple-element.14.refs_2_), channel_id=1, source_target_pairs={{0,8},{4,12},{8,0},{12,4},{16,24},{20,28},{24,16},{28,20},{1,9},{5... | collective-permute-start | bytes 786440 | tf_op jit(solution)/shard_map/ppermute | solution.py:21
  8.9 12.9 %collective-permute-start.5 = (bf16[1024,128]{1,0:T(8,128)(2,1)S(1)}, bf16[1024,128]{1,0:T(8,128)(2,1)}, u32[]{:S(2)}, u32[]{:S(2)}) collective-permute-start(bf16[1024,128]{1,0:T(8,128)(2,1)S(1)} %get-tuple-element.15.refs_3_), channel_id=1, source_target_pairs={{0,8},{4,12},{8,0},{12,4},{16,24},{20,28},{24,16},{28,20},{1,9},{5... | collective-permute-start | bytes 786440 | tf_op jit(solution)/shard_map/ppermute | solution.py:21
  9.0 15.5 %collective-permute-start.6 = (bf16[1024,128]{1,0:T(8,128)(2,1)S(1)}, bf16[1024,128]{1,0:T(8,128)(2,1)}, u32[]{:S(2)}, u32[]{:S(2)}) collective-permute-start(bf16[1024,128]{1,0:T(8,128)(2,1)S(1)} %get-tuple-element.14.refs_2_), channel_id=1, source_target_pairs={{0,16},{4,20},{8,24},{12,28},{16,0},{20,4},{24,8},{28,12},{1,17},{... | collective-permute-start | bytes 786440 | tf_op jit(solution)/shard_map/ppermute | solution.py:21
  11.0 0.7 copy-start.4
  11.7 15.1 %collective-permute-start.18 = (bf16[1024,128]{1,0:T(8,128)(2,1)S(1)}, bf16[1024,128]{1,0:T(8,128)(2,1)S(1)}, u32[]{:S(2)}, u32[]{:S(2)}) collective-permute-start(bf16[1024,128]{1,0:T(8,128)(2,1)S(1)} %get-tuple-element.18.refs_2_), channel_id=1, source_target_pairs={{0,16},{4,20},{8,24},{12,28},{16,0},{20,4},{24,8},{28,12},{1,17},{... | collective-permute-start | bytes 786440 | tf_op jit(solution)/shard_map/ppermute | solution.py:21
  16.1 0.7 copy-start.8
  16.8 11.2 %collective-permute-start.17 = (bf16[1024,128]{1,0:T(8,128)(2,1)S(1)}, bf16[1024,128]{1,0:T(8,128)(2,1)S(1)}, u32[]{:S(2)}, u32[]{:S(2)}) collective-permute-start(bf16[1024,128]{1,0:T(8,128)(2,1)S(1)} %get-tuple-element.19.refs_3_), channel_id=1, source_target_pairs={{0,8},{4,12},{8,0},{12,4},{16,24},{20,28},{24,16},{28,20},{1,9},{5... | collective-permute-start | bytes 786440 | tf_op jit(solution)/shard_map/ppermute | solution.py:21
  21.8 11.1 %collective-permute-start.16 = (bf16[1024,128]{1,0:T(8,128)(2,1)S(1)}, bf16[1024,128]{1,0:T(8,128)(2,1)S(1)}, u32[]{:S(2)}, u32[]{:S(2)}) collective-permute-start(bf16[1024,128]{1,0:T(8,128)(2,1)S(1)} %get-tuple-element.18.refs_2_), channel_id=1, source_target_pairs={{0,8},{4,12},{8,0},{12,4},{16,24},{20,28},{24,16},{28,20},{1,9},{5... | collective-permute-start | bytes 786440 | tf_op jit(solution)/shard_map/ppermute | solution.py:21
  23.8 0.7 copy-start.10
  24.5 11.1 %collective-permute-start.19 = (bf16[1024,128]{1,0:T(8,128)(2,1)S(1)}, bf16[1024,128]{1,0:T(8,128)(2,1)S(1)}, u32[]{:S(2)}, u32[]{:S(2)}) collective-permute-start(bf16[1024,128]{1,0:T(8,128)(2,1)S(1)} %get-tuple-element.19.refs_3_), channel_id=1, source_target_pairs={{0,16},{4,20},{8,24},{12,28},{16,0},{20,4},{24,8},{28,12},{1,17},{... | collective-permute-start | bytes 786440 | tf_op jit(solution)/shard_map/ppermute | solution.py:21
  26.0 0.7 copy-start.12
  26.7 11.9 %collective-permute-start.21 = (bf16[1024,128]{1,0:T(8,128)(2,1)S(1)}, bf16[1024,128]{1,0:T(8,128)(2,1)}, u32[]{:S(2)}, u32[]{:S(2)}) collective-permute-start(bf16[1024,128]{1,0:T(8,128)(2,1)S(1)} %collective-permute-done.18.refs_6_), channel_id=1, source_target_pairs={{0,8},{4,12},{8,0},{12,4},{16,24},{20,28},{24,16},{28,20},{1,9},{5... | collective-permute-start | bytes 786440 | tf_op jit(solution)/shard_map/ppermute | solution.py:21
  27.3 0.7 copy-start.14
  28.0 13.4 %collective-permute-start.22 = (bf16[1024,128]{1,0:T(8,128)(2,1)S(1)}, bf16[1024,128]{1,0:T(8,128)(2,1)}, u32[]{:S(2)}, u32[]{:S(2)}) collective-permute-start(bf16[1024,128]{1,0:T(8,128)(2,1)S(1)} %collective-permute-done.17.refs_5_), channel_id=1, source_target_pairs={{0,16},{4,20},{8,24},{12,28},{16,0},{20,4},{24,8},{28,12},{1,17},{... | collective-permute-start | bytes 786440 | tf_op jit(solution)/shard_map/ppermute | solution.py:21
  29.3 0.7 copy-start.16
  32.9 0.7 copy-start.18
  33.6 14.7 %collective-permute-start.9 = (bf16[1024,128]{1,0:T(8,128)(2,1)}, bf16[1024,128]{1,0:T(8,128)(2,1)}, u32[]{:S(2)}, u32[]{:S(2)}) collective-permute-start(bf16[1024,128]{1,0:T(8,128)(2,1)} %collective-permute-done.6.refs_6_), channel_id=1, source_target_pairs={{0,8},{4,12},{8,0},{12,4},{16,24},{20,28},{24,16},{28,20},{1,9},{5... | collective-permute-start | bytes 786440 | tf_op jit(solution)/shard_map/ppermute | solution.py:21
  35.6 0.7 copy-start.20
  36.4 12.1 %collective-permute-start.10 = (bf16[1024,128]{1,0:T(8,128)(2,1)}, bf16[1024,128]{1,0:T(8,128)(2,1)}, u32[]{:S(2)}, u32[]{:S(2)}) collective-permute-start(bf16[1024,128]{1,0:T(8,128)(2,1)} %collective-permute-done.5.refs_5_), channel_id=1, source_target_pairs={{0,16},{4,20},{8,24},{12,28},{16,0},{20,4},{24,8},{28,12},{1,17},{... | collective-permute-start | bytes 786440 | tf_op jit(solution)/shard_map/ppermute | solution.py:21
  38.6 10.3 %collective-permute-start.7 = (bf16[1024,128]{1,0:T(8,128)(2,1)S(1)}, bf16[1024,128]{1,0:T(8,128)(2,1)}, u32[]{:S(2)}, u32[]{:S(2)}) collective-permute-start(bf16[1024,128]{1,0:T(8,128)(2,1)S(1)} %get-tuple-element.15.refs_3_), channel_id=1, source_target_pairs={{0,16},{4,20},{8,24},{12,28},{16,0},{20,4},{24,8},{28,12},{1,17},{... | collective-permute-start | bytes 786440 | tf_op jit(solution)/shard_map/ppermute | solution.py:21
  40.7 0.7 copy-start.6
  41.4 8.5 %collective-permute-start.23 = (bf16[1024,128]{1,0:T(8,128)(2,1)}, bf16[1024,128]{1,0:T(8,128)(2,1)}, u32[]{:S(2)}, u32[]{:S(2)}) collective-permute-start(bf16[1024,128]{1,0:T(8,128)(2,1)} %collective-permute-done.21.refs_2_), channel_id=1, source_target_pairs={{0,4},{4,0},{8,12},{12,8},{16,20},{20,16},{24,28},{28,24},{1,5},{5... | collective-permute-start | bytes 786440 | tf_op jit(solution)/shard_map/ppermute | solution.py:21
  41.4 10.1 %collective-permute-start.24 = (bf16[1024,128]{1,0:T(8,128)(2,1)}, bf16[1024,128]{1,0:T(8,128)(2,1)}, u32[]{:S(2)}, u32[]{:S(2)}) collective-permute-start(bf16[1024,128]{1,0:T(8,128)(2,1)} %collective-permute-done.22.refs_3_), channel_id=1, source_target_pairs={{0,4},{4,0},{8,12},{12,8},{16,20},{20,16},{24,28},{28,24},{1,5},{5... | collective-permute-start | bytes 786440 | tf_op jit(solution)/shard_map/ppermute | solution.py:21
  41.9 0.9 copy-start.11
  42.9 0.9 copy-start.13
  43.8 0.9 copy-start.15
  44.8 0.9 copy-start.17
  45.7 0.9 copy-start.19
  46.7 0.9 copy-start.21
  48.3 12.8 %collective-permute-start.11 = (bf16[1024,128]{1,0:T(8,128)(2,1)}, bf16[1024,128]{1,0:T(8,128)(2,1)}, u32[]{:S(2)}, u32[]{:S(2)}) collective-permute-start(bf16[1024,128]{1,0:T(8,128)(2,1)} %collective-permute-done.9.refs_2_), channel_id=1, source_target_pairs={{0,4},{4,0},{8,12},{12,8},{16,20},{20,16},{24,28},{28,24},{1,5},{5... | collective-permute-start | bytes 786440 | tf_op jit(solution)/shard_map/ppermute | solution.py:21
  48.5 13.1 %collective-permute-start.12 = (bf16[1024,128]{1,0:T(8,128)(2,1)}, bf16[1024,128]{1,0:T(8,128)(2,1)}, u32[]{:S(2)}, u32[]{:S(2)}) collective-permute-start(bf16[1024,128]{1,0:T(8,128)(2,1)} %collective-permute-done.10.refs_3_), channel_id=1, source_target_pairs={{0,4},{4,0},{8,12},{12,8},{16,20},{20,16},{24,28},{28,24},{1,5},{5... | collective-permute-start | bytes 786440 | tf_op jit(solution)/shard_map/ppermute | solution.py:21
  48.9 8.2 %collective-permute-start.20 = (bf16[3,128,128]{2,1,0:T(8,128)(2,1)S(1)}, bf16[3,128,128]{2,1,0:T(8,128)(2,1)S(1)}, u32[]{:S(2)}, u32[]{:S(2)}) collective-permute-start(bf16[3,128,128]{2,1,0:T(8,128)(2,1)S(1)} %get-tuple-element.21), channel_id=1, source_target_pairs={{0,4},{4,0},{8,12},{12,8},{16,20},{20,16},{24,28},{28,24},{1,5},{5... | collective-permute-start | bytes 294920 | tf_op jit(solution)/shard_map/ppermute | solution.py:21
  49.0 5.1 %copy-start.5 = (bf16[1024,128]{1,0:T(8,128)(2,1)S(1)}, bf16[1024,128]{1,0:T(8,128)(2,1)}, u32[]{:S(2)}) copy-start(bf16[1024,128]{1,0:T(8,128)(2,1)} %copy-done.4) | copy-start | bytes 786436
  49.0 5.1 %copy-start.7 = (bf16[1024,128]{1,0:T(8,128)(2,1)S(1)}, bf16[1024,128]{1,0:T(8,128)(2,1)}, u32[]{:S(2)}) copy-start(bf16[1024,128]{1,0:T(8,128)(2,1)} %copy-done.6) | copy-start | bytes 786436
  49.0 5.1 %copy-start.9 = (bf16[1024,128]{1,0:T(8,128)(2,1)S(1)}, bf16[1024,128]{1,0:T(8,128)(2,1)}, u32[]{:S(2)}) copy-start(bf16[1024,128]{1,0:T(8,128)(2,1)} %copy-done.8) | copy-start | bytes 786436
  49.9 16.2 %collective-permute-start = (bf16[2,512,128]{2,1,0:T(8,128)(2,1)}, bf16[2,512,128]{2,1,0:T(8,128)(2,1)S(1)}, u32[]{:S(2)}, u32[]{:S(2)}) collective-permute-start(bf16[2,512,128]{2,1,0:T(8,128)(2,1)} %get-tuple-element.28), channel_id=1, source_target_pairs={{0,1},{1,0},{2,3},{3,2},{4,5},{5,4},{6,7},{7,6},{8,9},{9,8},{10,11... | collective-permute-start | bytes 786440 | tf_op jit(solution)/shard_map/ppermute | solution.py:21
  51.5 35.3 %collective-permute-start.1 = (bf16[2,512,128]{2,1,0:T(8,128)(2,1)}, bf16[2,512,128]{2,1,0:T(8,128)(2,1)S(1)}, u32[]{:S(2)}, u32[]{:S(2)}) collective-permute-start(bf16[2,512,128]{2,1,0:T(8,128)(2,1)} %get-tuple-element.27), channel_id=1, source_target_pairs={{0,2},{1,3},{2,0},{3,1},{4,6},{5,7},{6,4},{7,5},{8,10},{9,11},{10,... | collective-permute-start | bytes 786440 | tf_op jit(solution)/shard_map/ppermute | solution.py:21
  56.5 0.6 copy-start.24
  57.2 0.6 copy-start.22
  57.8 5.4 %collective-permute-start.8 = (bf16[3,128,128]{2,1,0:T(8,128)(2,1)}, bf16[3,128,128]{2,1,0:T(8,128)(2,1)S(1)}, u32[]{:S(2)}, u32[]{:S(2)}) collective-permute-start(bf16[3,128,128]{2,1,0:T(8,128)(2,1)} %get-tuple-element.17), channel_id=1, source_target_pairs={{0,4},{4,0},{8,12},{12,8},{16,20},{20,16},{24,28},{28,24},{1,5},{5... | collective-permute-start | bytes 294920 | tf_op jit(solution)/shard_map/ppermute | solution.py:21
  57.8 0.7 copy-start.27
  58.7 0.9 copy-start.23
  59.6 1.6 %copy-start.26 = (bf16[2,512,128]{2,1,0:T(8,128)(2,1)S(1)}, bf16[2,512,128]{2,1,0:T(8,128)(2,1)}, u32[]{:S(2)}) copy-start(bf16[2,512,128]{2,1,0:T(8,128)(2,1)} %get-tuple-element.26) | copy-start | bytes 786436
  59.6 3.6 %copy-start.25 = (bf16[3,128,128]{2,1,0:T(8,128)(2,1)S(1)}, bf16[3,128,128]{2,1,0:T(8,128)(2,1)}, u32[]{:S(2)}) copy-start(bf16[3,128,128]{2,1,0:T(8,128)(2,1)} %copy-done.24) | copy-start | bytes 294916
  61.2 28.0 %collective-permute-start.2 = (bf16[2,512,128]{2,1,0:T(8,128)(2,1)S(1)}, bf16[2,512,128]{2,1,0:T(8,128)(2,1)S(1)}, u32[]{:S(2)}, u32[]{:S(2)}) collective-permute-start(bf16[2,512,128]{2,1,0:T(8,128)(2,1)S(1)} %copy-done.26), channel_id=1, source_target_pairs={{0,3},{1,2},{2,1},{3,0},{4,7},{5,6},{6,5},{7,4},{8,11},{9,10},{10,... | collective-permute-start | bytes 786440 | tf_op jit(solution)/shard_map/ppermute | solution.py:21
  61.6 24.8 %collective-permute-start.26 = (bf16[128,512]{1,0:T(8,128)(2,1)S(1)}, bf16[128,512]{1,0:T(8,128)(2,1)S(1)}, u32[]{:S(2)}, u32[]{:S(2)}) collective-permute-start(bf16[128,512]{1,0:T(8,128)(2,1)S(1)} %shard_map.64.refs_4_), channel_id=1, source_target_pairs={{0,2},{1,3},{2,0},{3,1},{4,6},{5,7},{6,4},{7,5},{8,10},{9,11},{10,... | collective-permute-start | bytes 393224 | tf_op jit(solution)/shard_map/ppermute | solution.py:21
  64.7 24.4 %collective-permute-start.14 = (bf16[128,512]{1,0:T(8,128)(2,1)S(1)}, bf16[128,512]{1,0:T(8,128)(2,1)S(1)}, u32[]{:S(2)}, u32[]{:S(2)}) collective-permute-start(bf16[128,512]{1,0:T(8,128)(2,1)S(1)} %shard_map.62.refs_4_), channel_id=1, source_target_pairs={{0,2},{1,3},{2,0},{3,1},{4,6},{5,7},{6,4},{7,5},{8,10},{9,11},{10,... | collective-permute-start | bytes 393224 | tf_op jit(solution)/shard_map/ppermute | solution.py:21
  66.1 23.0 %collective-permute-start.25 = (bf16[128,512]{1,0:T(8,128)(2,1)S(1)}, bf16[128,512]{1,0:T(8,128)(2,1)S(1)}, u32[]{:S(2)}, u32[]{:S(2)}) collective-permute-start(bf16[128,512]{1,0:T(8,128)(2,1)S(1)} %shard_map.64.refs_4_), channel_id=1, source_target_pairs={{0,1},{1,0},{2,3},{3,2},{4,5},{5,4},{6,7},{7,6},{8,9},{9,8},{10,11... | collective-permute-start | bytes 393224 | tf_op jit(solution)/shard_map/ppermute | solution.py:21
  86.4 6.4 %collective-permute-start.27 = (bf16[128,512]{1,0:T(8,128)(2,1)S(1)}, bf16[128,512]{1,0:T(8,128)(2,1)S(1)}, u32[]{:S(2)}, u32[]{:S(2)}) collective-permute-start(bf16[128,512]{1,0:T(8,128)(2,1)S(1)} %collective-permute-done.26.refs_6_), channel_id=1, source_target_pairs={{0,1},{1,0},{2,3},{3,2},{4,5},{5,4},{6,7},{7,6},{8,9},{9,8},{10,11... | collective-permute-start | bytes 393224 | tf_op jit(solution)/shard_map/ppermute | solution.py:21
  86.8 8.8 %collective-permute-start.13 = (bf16[128,512]{1,0:T(8,128)(2,1)S(1)}, bf16[128,512]{1,0:T(8,128)(2,1)S(1)}, u32[]{:S(2)}, u32[]{:S(2)}) collective-permute-start(bf16[128,512]{1,0:T(8,128)(2,1)S(1)} %shard_map.62.refs_4_), channel_id=1, source_target_pairs={{0,1},{1,0},{2,3},{3,2},{4,5},{5,4},{6,7},{7,6},{8,9},{9,8},{10,11... | collective-permute-start | bytes 393224 | tf_op jit(solution)/shard_map/ppermute | solution.py:21
  89.1 8.4 %collective-permute-start.15 = (bf16[128,512]{1,0:T(8,128)(2,1)S(1)}, bf16[128,512]{1,0:T(8,128)(2,1)S(1)}, u32[]{:S(2)}, u32[]{:S(2)}) collective-permute-start(bf16[128,512]{1,0:T(8,128)(2,1)S(1)} %collective-permute-done.14.refs_6_), channel_id=1, source_target_pairs={{0,1},{1,0},{2,3},{3,2},{4,5},{5,4},{6,7},{7,6},{8,9},{9,8},{10,11... | collective-permute-start | bytes 393224 | tf_op jit(solution)/shard_map/ppermute | solution.py:21
  99.1 5.2 %collective-permute-start.28 = (f32[4,72,128]{2,1,0:T(8,128)S(1)}, f32[4,72,128]{2,1,0:T(8,128)S(1)}, u32[]{:S(2)}, u32[]{:S(2)}) collective-permute-start(f32[4,72,128]{2,1,0:T(8,128)S(1)} %get-tuple-element.22), channel_id=1, source_target_pairs={{0,1},{1,0},{2,3},{3,2},{4,5},{5,4},{6,7},{7,6},{8,9},{9,8},{10,11... | collective-permute-start | bytes 442376 | tf_op jit(solution)/shard_map/ppermute | solution.py:21
  104.3 8.0 %collective-permute-start.29 = (f32[4,72,128]{2,1,0:T(8,128)S(1)}, f32[4,72,128]{2,1,0:T(8,128)S(1)}, u32[]{:S(2)}, u32[]{:S(2)}) collective-permute-start(f32[4,72,128]{2,1,0:T(8,128)S(1)} %add.25.own_ref), channel_id=1, source_target_pairs={{0,2},{1,3},{2,0},{3,1},{4,6},{5,7},{6,4},{7,5},{8,10},{9,11},{10,... | collective-permute-start | bytes 442376 | tf_op jit(solution)/shard_map/ppermute | solution.py:21
where the time goes:
time: 122 us
  waiting for transfers between devices  50.7 us (42%)
  starting transfers between devices  31.9 us (26%)
  Pallas kernels  19.6 us (16%)
  local copies, waits for them, and re-layouts  18.5 us (15%)
    ppermute x30, waiting for transfers between devices, swap(): return lax.ppermute(x, axis, [(i, i ^ bits) for i in range(size)])  50.7 us
    ppermute x30, starting transfers between devices, swap(): return lax.ppermute(x, axis, [(i, i ^ bits) for i in range(size)])  31.9 us
    pallas_call x9, Pallas kernels, call(): pl.pallas_call(kernel, out_shape=shapes, in_specs=specs, out_specs=out, c...  19.6 us
    unnamed x56, local copies, waits for them, and re-layouts  17.6 us
  transfers between devices with their start and end apart: 30, of which 11 were waited for; matrix products, arithmetic and copies ran while one was open for 1% of the time, Pallas kernels for 7%

commit v1 on v0

--- a/solution.py
+++ b/solution.py
@@ -13,7 +13,7 @@
 BLOCK = 16
 GRANT = 12 << 20
 VMEM = pl.BlockSpec(memory_space=pltpu.VMEM)
-ANY = pl.BlockSpec(memory_space=pl.ANY)
+HBM = pl.BlockSpec(memory_space=pltpu.HBM)
 SMEM = pl.BlockSpec(memory_space=pltpu.SMEM)
 
 
@@ -33,8 +33,8 @@
     for a, b in zip(pairs[::2], pairs[1::2]):
         fresh = {}
         for o, (low, high) in known.items():
-            a_low, a_high = swap(low, axis, a, size), swap(high, axis, a, size)
-            b_low, b_high = swap(low, axis, b, size), swap(high, axis, b, size)
+            a_high, b_low = swap(high, axis, a, size), swap(low, axis, b, size)
+            a_low, b_high = swap(low, axis, a, size), swap(high, axis, b, size)
             fresh[o ^ a] = (a_low, a_high)
             fresh[o ^ b] = (b_low, b_high)
             fresh[o ^ a ^ b] = (swap(b_low, axis, a, size), swap(a_high, axis, b, size))
@@ -60,31 +60,37 @@
     return copies
 
 
-def first_kernel(panels, left_ref, right_ref, probe_ref, *refs):
-    outs, (probe_buf, left_buf, right_buf, sems) = refs[:2 * panels], refs[2 * panels:]
-    sources = [(probe_ref, probe_buf)]
+def rows_of(probe_turned, left, right, low_ref, high_ref):
+    image = jnp.dot(probe_turned, left[...], preferred_element_type=jnp.float32)
+    image = image.astype(jnp.bfloat16)
+    half = low_ref.shape[0]
+    for h, ref in enumerate((low_ref, high_ref)):
+        ref[...] = lax.dot_general(
+            right[h * half:(h + 1) * half], image, (((1,), (1,)), ((), ())),
+            preferred_element_type=jnp.float32,
+        ).astype(jnp.bfloat16)
+
+
+def first_kernel(left_ref, right_ref, probe_ref, low_ref, high_ref, probe_buf, left_buf, right_buf, sems):
+    copies = fetch(
+        [(probe_ref, probe_buf), (left_ref.at[0, 0], left_buf), (right_ref.at[0, 0], right_buf)], sems
+    )
+    for copy in copies:
+        copy.wait()
+    rows_of(probe_buf[...].T, left_buf, right_buf, low_ref, high_ref)
+
+
+def second_kernel(count, level_ref, left_ref, right_ref, probe_ref, *outs):
+    panels = left_ref.shape[1]
+    turned_ref, block_refs = outs[2 * panels - 2], outs[2 * panels - 1:]
+    probe_turned = probe_ref[...].T
+    for p in range(1, panels):
+        rows_of(probe_turned, left_ref.at[0, p], right_ref.at[0, p], *outs[2 * p - 2:2 * p])
+    part = left_ref.shape[2] // count
     for p in range(panels):
-        sources += [(left_ref.at[0, p], left_buf.at[p]), (right_ref.at[0, p], right_buf.at[p])]
-    copies = fetch(sources, sems)
-    copies[0].wait()
-    probe_turned = probe_buf[...].T
-    for p in range(panels):
-        copies[1 + 2 * p].wait()
-        image = jnp.dot(
-            probe_turned, left_buf[p], preferred_element_type=jnp.float32
-        ).astype(jnp.bfloat16)
-        copies[2 + 2 * p].wait()
-        half = outs[0].shape[0]
-        for h in range(2):
-            outs[2 * p + h][...] = lax.dot_general(
-                right_buf[p, h * half:(h + 1) * half], image, (((1,), (1,)), ((), ())),
-                preferred_element_type=jnp.float32,
-            ).astype(jnp.bfloat16)
-
-
-def turn_kernel(right_ref, turned_ref):
-    for p in range(turned_ref.shape[0]):
         turned_ref[p] = right_ref[0, p].T
+        for o, ref in enumerate(block_refs):
+            ref[p] = left_ref[0, p, pl.ds(pl.multiple_of((level_ref[0] ^ o) * part, part), part), :]
 
 
 def couple(turned_refs, panel, blocks):
@@ -188,28 +194,38 @@
     cols = [
         jnp.broadcast_to(panel[:, first + j:first + j + 1], panel.shape) for j in range(BLOCK)
     ]
-    upper = jnp.zeros_like(panel)
-    inverse = jnp.zeros_like(panel)
     pivots = jnp.zeros_like(panel)
+    recips = jnp.zeros_like(panel)
     for j in range(BLOCK):
         k = first + j
         pivot = jnp.broadcast_to(cols[j][j:j + 1, :], panel.shape)
         recip = 1.0 / pivot
-        root = lax.rsqrt(pivot)
         factor = jnp.where(sub > j, cols[j] * recip, 0.0)
         for c in range(j + 1, BLOCK):
             cols[c] = cols[c] - factor * jnp.broadcast_to(cols[c][j:j + 1, :], panel.shape)
-        row = jnp.broadcast_to(panel[j:j + 1, :], panel.shape)
         here = sub == j
-        upper = jnp.where(here & (lane >= k), row * root, upper)
-        row = jnp.where(lane == k, 1.0, row)
-        inverse = jnp.where(here & (lane <= k), row * root, inverse)
-        pivots = jnp.where(here, recip, pivots)
+        pivots = jnp.where(here, pivot, pivots)
+        recips = jnp.where(here, recip, recips)
+        row = jnp.where(lane == k, 1.0, jnp.broadcast_to(panel[j:j + 1, :], panel.shape))
         panel = jnp.where((lane == k) & (sub >= j), jnp.where(here, 1.0, 0.0), panel)
         panel = panel - factor * row
-    below = jnp.where(lane >= first + BLOCK, panel * pivots, 0.0)
-    panel = jnp.where((lane < first + BLOCK) & (lane > first + sub), 0.0, panel)
-    return panel, below, upper, inverse
+    return panel, pivots, recips
+
+
+def split(x):
+    high = x.astype(jnp.bfloat16)
+    rest = x - high.astype(jnp.float32)
+    mid = rest.astype(jnp.bfloat16)
+    return high, mid, (rest - mid.astype(jnp.float32)).astype(jnp.bfloat16)
+
+
+def outer(a, b):
+    (ah, am, al), (bh, bm, bl) = split(a), split(b)
+    return lax.dot_general(
+        jnp.concatenate([al, ah, am, ah, am, ah], axis=0),
+        jnp.concatenate([bh, bl, bm, bm, bh, bh], axis=0),
+        (((0,), (0,)), ((), ())), preferred_element_type=jnp.float32,
+    )
 
 
 def factor_kernel(scale, own_ref, other_ref, sketch_ref, basis_ref, chol_ref, work_ref, upper_ref, inverse_ref):
@@ -222,18 +238,22 @@
         last = first + BLOCK
         done = [eliminate(work_ref[t, first:last, :], first, lane, sub) for t in range(listed)]
         for t in range(listed):
-            rows, below, upper, inverse = done[t]
-            upper_ref[t, first:last, :] = upper
-            inverse_ref[t, first:last, :] = inverse * scale
+            panel, pivots, recips = done[t]
+            root = lax.rsqrt(pivots)
+            diagonal = lane == first + sub
+            upper_ref[t, first:last, :] = jnp.where(
+                lane > first + sub, panel * root, jnp.where(diagonal, pivots * root, 0.0)
+            )
+            inverse_ref[t, first:last, :] = jnp.where(
+                lane <= first + sub, panel * (root * scale), 0.0
+            )
             if last < width:
                 at = lax.broadcasted_iota(jnp.int32, (width - last, width), 1)
                 old = work_ref[t, last:, :]
                 old = jnp.where((at >= first) & (at < last), 0.0, old)
-                update = lax.dot_general(
-                    below, rows, (((0,), (0,)), ((), ())), precision=HIGHEST,
-                    preferred_element_type=jnp.float32,
-                )
-                work_ref[t, last:, :] = old - update[last:, :]
+                below = jnp.where(lane >= last, panel * recips, 0.0)
+                rows = jnp.where((lane < last) & (lane > first + sub), 0.0, panel)
+                work_ref[t, last:, :] = old - outer(below, rows)[last:, :]
     for t in range(listed):
         chol_ref[t] = upper_ref[t].T * (1.0 / scale)
         basis_ref[t] = lax.dot_general(
@@ -245,7 +265,7 @@
 def call(kernel, shapes, *args, in_specs=None, leave=False, **more):
     specs = in_specs or [VMEM] * len(args)
     args = [
-        pltpu.with_memory_space_constraint(x, pltpu.VMEM) if spec is VMEM else x
+        x if spec is SMEM else pltpu.with_memory_space_constraint(x, spec.memory_space)
         for x, spec in zip(args, specs)
     ]
     if not leave:
@@ -271,32 +291,33 @@
 
     single = len(bits_of(rows_size)) % 2
     halves = call(
-        functools.partial(first_kernel, panels), (shape((half, width), bf16),) * (2 * panels),
-        left_factors, right_factors, probe_matrix, in_specs=[ANY] * 3,
+        first_kernel, (shape((half, width), bf16),) * 2,
+        left_factors, right_factors, probe_matrix, in_specs=[HBM] * 3,
         scratch_shapes=[
             pltpu.VMEM((tile_size, width), bf16),
-            pltpu.VMEM((panels, tile_size, rank_size), bf16),
-            pltpu.VMEM((panels, tile_size, rank_size), bf16),
-            pltpu.SemaphoreType.DMA((1 + 2 * panels,)),
+            pltpu.VMEM((tile_size, rank_size), bf16),
+            pltpu.VMEM((tile_size, rank_size), bf16),
+            pltpu.SemaphoreType.DMA((3,)),
         ],
     )
-    turned = [call(
-        turn_kernel, shape((panels, rank_size, tile_size), bf16), right_factors,
-        in_specs=[pl.BlockSpec(right_factors.shape)],
-    )]
+    second = call(
+        functools.partial(second_kernel, depth_size),
+        (shape((half, width), bf16),) * (2 * panels - 2)
+        + (shape((panels, rank_size, tile_size), bf16),)
+        + (shape((panels, part, rank_size), bf16),) * depth_size,
+        level[None], left_factors, right_factors, probe_matrix, in_specs=[SMEM] + [VMEM] * 3,
+    )
+    halves = list(halves) + list(second[:2 * panels - 2])
+    turned, blocks = [second[2 * panels - 2]], second[2 * panels - 1:]
     if single:
         turned.append(swap(turned[0], "rows", 1, rows_size))
     found, late = [], []
     for p in range(panels):
-        blocks, last = gather_rows(halves[2 * p:2 * p + 2], "rows", rows_size)
-        found.append(blocks)
+        reached, last = gather_rows(halves[2 * p:2 * p + 2], "rows", rows_size)
+        found.append(reached)
         late.append(last)
 
-    blocks = left_factors[0].reshape(panels, depth_size, part, rank_size)
-    lefts = []
-    for o in range(depth_size):
-        block = lax.dynamic_index_in_dim(blocks, level ^ o, 1, keepdims=False)
-        lefts.append(swap(block, "depth", o, depth_size) if o else block)
+    lefts = [swap(x, "depth", o, depth_size) if o else x for o, x in enumerate(blocks)]
 
     wanted = lax.dynamic_index_in_dim(tile_list, me, 0, keepdims=False) ^ me
     gathered = []

time: 122 us -> 123 us (level)
  waiting for transfers between devices: 50.7 us -> 63.4 us
  local copies, waits for them, and re-layouts: 18.5 us -> 9.71 us
  Pallas kernels: 19.6 us -> 17.5 us
    ppermute x30, waiting for transfers between devices: 50.7 us -> 63.4 us  [swap(): return lax.ppermute(x, axis, [(i, i ^ bits) for i in range(size)])]
    unnamed x56 -> x28, local copies, waits for them, and re-layouts: 17.6 us -> 9.71 us
    pallas_call x9, Pallas kernels: 19.6 us -> 17.5 us  [call(): pl.pallas_call(kernel, out_shape=shapes, in_specs=specs, out_specs=out, c...]
  transfers between devices with their start and end apart: 30 -> 30, of which waited for: 11 -> 15; matrix products, arithmetic and copies ran while one was open for 1% -> 0% of each run, Pallas kernels for 7% -> 5%
where the time goes in v1:
time: 123 us
  waiting for transfers between devices  63.4 us (52%)
  starting transfers between devices  31.3 us (25%)
  Pallas kernels  17.5 us (14%)
  local copies, waits for them, and re-layouts  9.71 us (8%)
    ppermute x30, waiting for transfers between devices, swap(): return lax.ppermute(x, axis, [(i, i ^ bits) for i in range(size)])  63.4 us
    ppermute x30, starting transfers between devices, swap(): return lax.ppermute(x, axis, [(i, i ^ bits) for i in range(size)])  31.3 us
    pallas_call x9, Pallas kernels, call(): pl.pallas_call(kernel, out_shape=shapes, in_specs=specs, out_specs=out, c...  17.5 us
    unnamed x28, local copies, waits for them, and re-layouts  9.71 us
  transfers between devices with their start and end apart: 30, of which 15 were waited for; matrix products, arithmetic and copies ran while one was open for 0% of the time, Pallas kernels for 5%

profile of v1, /device:TPU:0, one launch (start us, length us, event | category | flops | bytes accessed | tf_op | source)
XLA Modules:
  0.0 122.8 jit_solution(10310145978615072868)
XLA Ops:
  0.6 0.0 copy-start
  0.6 1.2 copy-done
  1.9 1.2 copy-done.1
  3.1 1.0 copy-done.2
  4.1 1.4 %shard_map.59 = (bf16[1024,128]{1,0:T(8,128)(2,1)S(1)}, bf16[1024,128]{1,0:T(8,128)(2,1)S(1)}, bf16[2,128,2048]{2,1,0:T(8,128)(2,1)S(1)}, bf16[2,512,128]{2,1,0:...) custom-call(s32[1]{0:T(128)} %bitcast.level_ref, ...), custom_call_target="tpu_custom_call" | custom-call | tf_op jit(solution)/shard_map/pallas_call | solution.py:275
  5.5 0.7 copy-done.11
  6.2 0.5 collective-permute-start.3
  6.7 2.5 %collective-permute-start.4 = (bf16[1024,128]{1,0:T(8,128)(2,1)S(1)}, bf16[1024,128]{1,0:T(8,128)(2,1)S(1)}, u32[]{:S(2)}, u32[]{:S(2)}) collective-permute-start(bf16[1024,128]{1,0:T(8,128)(2,1)S(1)} %get-tuple-element.24.refs_2_), channel_id=1, source_target_pairs={{0,8},{4,12},{8,0},{12,4},{16,24},{20,28},{24,16},{28,20},{1,9},{5... | collective-permute-start | bytes 786440 | tf_op jit(solution)/shard_map/ppermute | solution.py:21
  9.2 0.0 collective-permute-start.5
  9.2 2.0 %collective-permute-start.6 = (bf16[1024,128]{1,0:T(8,128)(2,1)S(1)}, bf16[1024,128]{1,0:T(8,128)(2,1)S(1)}, u32[]{:S(2)}, u32[]{:S(2)}) collective-permute-start(bf16[1024,128]{1,0:T(8,128)(2,1)S(1)} %get-tuple-element.24.refs_2_), channel_id=1, source_target_pairs={{0,16},{4,20},{8,24},{12,28},{16,0},{20,4},{24,8},{28,12},{1,17},{... | collective-permute-start | bytes 786440 | tf_op jit(solution)/shard_map/ppermute | solution.py:21
  11.3 2.0 %shard_map.62 = (bf16[1024,128]{1,0:T(8,128)(2,1)S(1)}, bf16[1024,128]{1,0:T(8,128)(2,1)S(1)}) custom-call(bf16[1,2,2048,128]{3,2,1,0:T(8,128)(2,1)} %left_ref.3, bf16[1,2,2048,128]{3,2,1,0:T(8,128)(2,1)} %right_ref.3, bf16[2048,128]{1,0:T(8,128)(2,1)} %probe_ref.3), custom_call_target="tpu_custom_call" | custom-call | tf_op jit(solution)/shard_map/pallas_call | solution.py:275
  13.3 1.6 %collective-permute-start.16 = (bf16[1024,128]{1,0:T(8,128)(2,1)S(1)}, bf16[1024,128]{1,0:T(8,128)(2,1)S(1)}, u32[]{:S(2)}, u32[]{:S(2)}) collective-permute-start(bf16[1024,128]{1,0:T(8,128)(2,1)S(1)} %get-tuple-element.28.refs_2_), channel_id=1, source_target_pairs={{0,8},{4,12},{8,0},{12,4},{16,24},{20,28},{24,16},{28,20},{1,9},{5... | collective-permute-start | bytes 786440 | tf_op jit(solution)/shard_map/ppermute | solution.py:21
  14.8 1.5 %collective-permute-done.4.refs_4_ = bf16[1024,128]{1,0:T(8,128)(2,1)S(1)} collective-permute-done((bf16[1024,128]{1,0:T(8,128)(2,1)S(1)}, bf16[1024,128]{1,0:T(8,128)(2,1)S(1)}, u32[]{:S(2)}, u32[]{:S(2)}) %collective-permute-start.4) | collective-permute-done | bytes 262176 | tf_op jit(solution)/shard_map/ppermute | solution.py:21
  16.4 2.1 %collective-permute-start.18 = (bf16[1024,128]{1,0:T(8,128)(2,1)S(1)}, bf16[1024,128]{1,0:T(8,128)(2,1)S(1)}, u32[]{:S(2)}, u32[]{:S(2)}) collective-permute-start(bf16[1024,128]{1,0:T(8,128)(2,1)S(1)} %get-tuple-element.28.refs_2_), channel_id=1, source_target_pairs={{0,16},{4,20},{8,24},{12,28},{16,0},{20,4},{24,8},{28,12},{1,17},{... | collective-permute-start | bytes 786440 | tf_op jit(solution)/shard_map/ppermute | solution.py:21
  18.4 3.6 %collective-permute-done.5.refs_5_ = bf16[1024,128]{1,0:T(8,128)(2,1)S(1)} collective-permute-done((bf16[1024,128]{1,0:T(8,128)(2,1)S(1)}, bf16[1024,128]{1,0:T(8,128)(2,1)S(1)}, u32[]{:S(2)}, u32[]{:S(2)}) %collective-permute-start.5) | collective-permute-done | bytes 262176 | tf_op jit(solution)/shard_map/ppermute | solution.py:21
  22.0 2.0 %collective-permute-start.17 = (bf16[1024,128]{1,0:T(8,128)(2,1)S(1)}, bf16[1024,128]{1,0:T(8,128)(2,1)S(1)}, u32[]{:S(2)}, u32[]{:S(2)}) collective-permute-start(bf16[1024,128]{1,0:T(8,128)(2,1)S(1)} %get-tuple-element.29.refs_3_), channel_id=1, source_target_pairs={{0,8},{4,12},{8,0},{12,4},{16,24},{20,28},{24,16},{28,20},{1,9},{5... | collective-permute-start | bytes 786440 | tf_op jit(solution)/shard_map/ppermute | solution.py:21
  24.0 0.0 collective-permute-done.6.refs_6_
  24.0 1.5 %collective-permute-start.19 = (bf16[1024,128]{1,0:T(8,128)(2,1)S(1)}, bf16[1024,128]{1,0:T(8,128)(2,1)S(1)}, u32[]{:S(2)}, u32[]{:S(2)}) collective-permute-start(bf16[1024,128]{1,0:T(8,128)(2,1)S(1)} %get-tuple-element.29.refs_3_), channel_id=1, source_target_pairs={{0,16},{4,20},{8,24},{12,28},{16,0},{20,4},{24,8},{28,12},{1,17},{... | collective-permute-start | bytes 786440 | tf_op jit(solution)/shard_map/ppermute | solution.py:21
  25.5 2.1 %collective-permute-done.16.refs_4_ = bf16[1024,128]{1,0:T(8,128)(2,1)S(1)} collective-permute-done((bf16[1024,128]{1,0:T(8,128)(2,1)S(1)}, bf16[1024,128]{1,0:T(8,128)(2,1)S(1)}, u32[]{:S(2)}, u32[]{:S(2)}) %collective-permute-start.16) | collective-permute-done | bytes 262176 | tf_op jit(solution)/shard_map/ppermute | solution.py:21
  27.6 2.0 %collective-permute-start.9 = (bf16[1024,128]{1,0:T(8,128)(2,1)S(1)}, bf16[1024,128]{1,0:T(8,128)(2,1)S(1)}, u32[]{:S(2)}, u32[]{:S(2)}) collective-permute-start(bf16[1024,128]{1,0:T(8,128)(2,1)S(1)} %collective-permute-done.6.refs_6_), channel_id=1, source_target_pairs={{0,8},{4,12},{8,0},{12,4},{16,24},{20,28},{24,16},{28,20},{1,9},{5... | collective-permute-start | bytes 786440 | tf_op jit(solution)/shard_map/ppermute | solution.py:21
  29.6 0.0 collective-permute-start.21
  29.7 3.6 %collective-permute-done.17.refs_5_ = bf16[1024,128]{1,0:T(8,128)(2,1)S(1)} collective-permute-done((bf16[1024,128]{1,0:T(8,128)(2,1)S(1)}, bf16[1024,128]{1,0:T(8,128)(2,1)S(1)}, u32[]{:S(2)}, u32[]{:S(2)}) %collective-permute-start.17) | collective-permute-done | bytes 262176 | tf_op jit(solution)/shard_map/ppermute | solution.py:21
  33.2 2.1 %collective-permute-start.22 = (bf16[1024,128]{1,0:T(8,128)(2,1)S(1)}, bf16[1024,128]{1,0:T(8,128)(2,1)S(1)}, u32[]{:S(2)}, u32[]{:S(2)}) collective-permute-start(bf16[1024,128]{1,0:T(8,128)(2,1)S(1)} %collective-permute-done.17.refs_5_), channel_id=1, source_target_pairs={{0,16},{4,20},{8,24},{12,28},{16,0},{20,4},{24,8},{28,12},{1,17},{... | collective-permute-start | bytes 786440 | tf_op jit(solution)/shard_map/ppermute | solution.py:21
  35.3 0.0 collective-permute-done.19.refs_7_
  35.3 0.0 collective-permute-start.10
  35.3 3.5 %collective-permute-done.9.refs_2_ = bf16[1024,128]{1,0:T(8,128)(2,1)S(1)} collective-permute-done((bf16[1024,128]{1,0:T(8,128)(2,1)S(1)}, bf16[1024,128]{1,0:T(8,128)(2,1)S(1)}, u32[]{:S(2)}, u32[]{:S(2)}) %collective-permute-start.9) | collective-permute-done | bytes 262176 | tf_op jit(solution)/shard_map/ppermute | solution.py:21
  38.8 2.1 %collective-permute-start.7 = (bf16[1024,128]{1,0:T(8,128)(2,1)S(1)}, bf16[1024,128]{1,0:T(8,128)(2,1)S(1)}, u32[]{:S(2)}, u32[]{:S(2)}) collective-permute-start(bf16[1024,128]{1,0:T(8,128)(2,1)S(1)} %get-tuple-element.25.refs_3_), channel_id=1, source_target_pairs={{0,16},{4,20},{8,24},{12,28},{16,0},{20,4},{24,8},{28,12},{1,17},{... | collective-permute-start | bytes 786440 | tf_op jit(solution)/shard_map/ppermute | solution.py:21
  40.9 3.4 %collective-permute-done.21.refs_2_ = bf16[1024,128]{1,0:T(8,128)(2,1)S(1)} collective-permute-done((bf16[1024,128]{1,0:T(8,128)(2,1)S(1)}, bf16[1024,128]{1,0:T(8,128)(2,1)S(1)}, u32[]{:S(2)}, u32[]{:S(2)}) %collective-permute-start.21) | collective-permute-done | bytes 262176 | tf_op jit(solution)/shard_map/ppermute | solution.py:21
  44.3 0.5 collective-permute-start.24
  44.8 3.3 %collective-permute-done.10.refs_3_ = bf16[1024,128]{1,0:T(8,128)(2,1)S(1)} collective-permute-done((bf16[1024,128]{1,0:T(8,128)(2,1)S(1)}, bf16[1024,128]{1,0:T(8,128)(2,1)S(1)}, u32[]{:S(2)}, u32[]{:S(2)}) %collective-permute-start.10) | collective-permute-done | bytes 262176 | tf_op jit(solution)/shard_map/ppermute | solution.py:21
  48.1 0.5 collective-permute-start.12
  48.6 0.7 shard_map.63
  49.3 3.1 %collective-permute-done.7.refs_7_ = bf16[1024,128]{1,0:T(8,128)(2,1)S(1)} collective-permute-done((bf16[1024,128]{1,0:T(8,128)(2,1)S(1)}, bf16[1024,128]{1,0:T(8,128)(2,1)S(1)}, u32[]{:S(2)}, u32[]{:S(2)}) %collective-permute-start.7) | collective-permute-done | bytes 262176 | tf_op jit(solution)/shard_map/ppermute | solution.py:21
  52.4 1.6 %collective-permute-start = (bf16[2,512,128]{2,1,0:T(8,128)(2,1)}, bf16[2,512,128]{2,1,0:T(8,128)(2,1)S(1)}, u32[]{:S(2)}, u32[]{:S(2)}) collective-permute-start(bf16[2,512,128]{2,1,0:T(8,128)(2,1)} %get-tuple-element.20), channel_id=1, source_target_pairs={{0,1},{1,0},{2,3},{3,2},{4,5},{5,4},{6,7},{7,6},{8,9},{9,8},{10,11... | collective-permute-start | bytes 786440 | tf_op jit(solution)/shard_map/ppermute | solution.py:21
  54.1 0.7 copy-done.5
  54.8 2.6 %collective-permute-start.1 = (bf16[2,512,128]{2,1,0:T(8,128)(2,1)}, bf16[2,512,128]{2,1,0:T(8,128)(2,1)S(1)}, u32[]{:S(2)}, u32[]{:S(2)}) collective-permute-start(bf16[2,512,128]{2,1,0:T(8,128)(2,1)} %get-tuple-element.21), channel_id=1, source_target_pairs={{0,2},{1,3},{2,0},{3,1},{4,6},{5,7},{6,4},{7,5},{8,10},{9,11},{10,... | collective-permute-start | bytes 786440 | tf_op jit(solution)/shard_map/ppermute | solution.py:21
  57.4 1.3 %shard_map.60 = (bf16[3,128,128]{2,1,0:T(8,128)(2,1)S(1)}, bf16[3,128,128]{2,1,0:T(8,128)(2,1)}) custom-call(bf16[2,128,2048]{2,1,0:T(8,128)(2,1)S(1)} %get-tuple-element.23.refs_0_.turned_ref, bf16[2,128,2048]{2,1,0:T(8,128)(2,1)S(1)} %collective-permute-done.3.refs_1_, bf16[1024,128]{1,0:T(8,128)(2,1)S(1)} %get-tuple-element.24.refs_2_, ...), custom_call_target="tpu_custom_call" | custom-call | tf_op jit(solution)/shard_map/pallas_call | solution.py:275
  58.7 0.6 copy-done.7
  59.3 0.6 copy-done.9
  60.0 0.7 copy-done.13
  60.6 0.2 xor_reduce_fusion.wanted_ref
  60.8 0.9 copy-done.4
  61.8 0.9 copy-done.6
  62.7 0.9 copy-done.10
  63.6 0.9 shard_map.64.refs_4_
  64.5 0.1 copy-done.12
  64.6 0.3 collective-permute-start.2
  64.8 1.7 %collective-permute-start.26 = (bf16[128,512]{1,0:T(8,128)(2,1)S(1)}, bf16[128,512]{1,0:T(8,128)(2,1)S(1)}, u32[]{:S(2)}, u32[]{:S(2)}) collective-permute-start(bf16[128,512]{1,0:T(8,128)(2,1)S(1)} %shard_map.64.refs_4_), channel_id=1, source_target_pairs={{0,2},{1,3},{2,0},{3,1},{4,6},{5,7},{6,4},{7,5},{8,10},{9,11},{10,... | collective-permute-start | bytes 393224 | tf_op jit(solution)/shard_map/ppermute | solution.py:21
  66.5 1.2 %shard_map.61.refs_4_ = bf16[128,512]{1,0:T(8,128)(2,1)S(1)} custom-call(s32[4]{0:T(128)S(1)} %xor_reduce_fusion.wanted_ref, bf16[2,128,2048]{2,1,0:T(8,128)(2,1)S(1)} %get-tuple-element.23.refs_0_.turned_ref, bf16[3,128,128]{2,1,0:T(8,128)(2,1)S(1)} %copy-done.8, bf16[3,128,128]{2,1,0:T(8,128)(2,1)} %collective-permute-done.8.refs_1_, ...), custom_call_target="tpu_custom_call" | custom-call | tf_op jit(solution)/shard_map/pallas_call | solution.py:275
  67.8 1.3 %collective-permute-start.14 = (bf16[128,512]{1,0:T(8,128)(2,1)S(1)}, bf16[128,512]{1,0:T(8,128)(2,1)S(1)}, u32[]{:S(2)}, u32[]{:S(2)}) collective-permute-start(bf16[128,512]{1,0:T(8,128)(2,1)S(1)} %shard_map.61.refs_4_), channel_id=1, source_target_pairs={{0,2},{1,3},{2,0},{3,1},{4,6},{5,7},{6,4},{7,5},{8,10},{9,11},{10,... | collective-permute-start | bytes 393224 | tf_op jit(solution)/shard_map/ppermute | solution.py:21
  69.1 1.3 %collective-permute-start.25 = (bf16[128,512]{1,0:T(8,128)(2,1)S(1)}, bf16[128,512]{1,0:T(8,128)(2,1)S(1)}, u32[]{:S(2)}, u32[]{:S(2)}) collective-permute-start(bf16[128,512]{1,0:T(8,128)(2,1)S(1)} %shard_map.64.refs_4_), channel_id=1, source_target_pairs={{0,1},{1,0},{2,3},{3,2},{4,5},{5,4},{6,7},{7,6},{8,9},{9,8},{10,11... | collective-permute-start | bytes 393224 | tf_op jit(solution)/shard_map/ppermute | solution.py:21
  70.4 20.0 %collective-permute-done.26.refs_6_ = bf16[128,512]{1,0:T(8,128)(2,1)S(1)} collective-permute-done((bf16[128,512]{1,0:T(8,128)(2,1)S(1)}, bf16[128,512]{1,0:T(8,128)(2,1)S(1)}, u32[]{:S(2)}, u32[]{:S(2)}) %collective-permute-start.26) | collective-permute-done | bytes 131104 | tf_op jit(solution)/shard_map/ppermute | solution.py:21
  90.4 2.0 %collective-permute-start.13 = (bf16[128,512]{1,0:T(8,128)(2,1)S(1)}, bf16[128,512]{1,0:T(8,128)(2,1)S(1)}, u32[]{:S(2)}, u32[]{:S(2)}) collective-permute-start(bf16[128,512]{1,0:T(8,128)(2,1)S(1)} %shard_map.61.refs_4_), channel_id=1, source_target_pairs={{0,1},{1,0},{2,3},{3,2},{4,5},{5,4},{6,7},{7,6},{8,9},{9,8},{10,11... | collective-permute-start | bytes 393224 | tf_op jit(solution)/shard_map/ppermute | solution.py:21
  92.5 0.1 collective-permute-done.14.refs_6_
  92.5 4.3 %collective-permute-done.27.refs_7_ = bf16[128,512]{1,0:T(8,128)(2,1)S(1)} collective-permute-done((bf16[128,512]{1,0:T(8,128)(2,1)S(1)}, bf16[128,512]{1,0:T(8,128)(2,1)S(1)}, u32[]{:S(2)}, u32[]{:S(2)}) %collective-permute-start.27) | collective-permute-done | bytes 131104 | tf_op jit(solution)/shard_map/ppermute | solution.py:21
  96.8 0.4 shard_map.65.refs_8_
  97.2 2.2 %collective-permute-done.13.refs_5_ = bf16[128,512]{1,0:T(8,128)(2,1)S(1)} collective-permute-done((bf16[128,512]{1,0:T(8,128)(2,1)S(1)}, bf16[128,512]{1,0:T(8,128)(2,1)S(1)}, u32[]{:S(2)}, u32[]{:S(2)}) %collective-permute-start.13) | collective-permute-done | bytes 131104 | tf_op jit(solution)/shard_map/ppermute | solution.py:21
  99.4 1.4 %collective-permute-done.15.refs_7_ = bf16[128,512]{1,0:T(8,128)(2,1)S(1)} collective-permute-done((bf16[128,512]{1,0:T(8,128)(2,1)S(1)}, bf16[128,512]{1,0:T(8,128)(2,1)S(1)}, u32[]{:S(2)}, u32[]{:S(2)}) %collective-permute-start.15) | collective-permute-done | bytes 131104 | tf_op jit(solution)/shard_map/ppermute | solution.py:21
  100.9 1.5 %shard_map.66 = (f32[4,512,128]{2,1,0:T(8,128)S(1)}, f32[4,72,128]{2,1,0:T(8,128)S(1)}) custom-call(bf16[2,512,128]{2,1,0:T(8,128)(2,1)S(1)} %get-tuple-element.19.refs_0_, bf16[2,512,128]{2,1,0:T(8,128)(2,1)S(1)} %collective-permute-done.refs_1_, bf16[2,512,128]{2,1,0:T(8,128)(2,1)S(1)} %collective-permute-done.1.refs_2_, ...), custom_call_target="tpu_custom_call" | custom-call | tf_op jit(solution)/shard_map/pallas_call | solution.py:275
  102.4 0.1 collective-permute-start.28
  102.5 5.1 %collective-permute-done.28 = f32[4,72,128]{2,1,0:T(8,128)S(1)} collective-permute-done((f32[4,72,128]{2,1,0:T(8,128)S(1)}, f32[4,72,128]{2,1,0:T(8,128)S(1)}, u32[]{:S(2)}, u32[]{:S(2)}) %collective-permute-start.28) | collective-permute-done | bytes 147488 | tf_op jit(solution)/shard_map/ppermute | solution.py:21
  107.6 1.0 collective-permute-start.29
  108.7 6.2 %collective-permute-done.29.other_ref = f32[4,72,128]{2,1,0:T(8,128)S(1)} collective-permute-done((f32[4,72,128]{2,1,0:T(8,128)S(1)}, f32[4,72,128]{2,1,0:T(8,128)S(1)}, u32[]{:S(2)}, u32[]{:S(2)}) %collective-permute-start.29) | collective-permute-done | bytes 147488 | tf_op jit(solution)/shard_map/ppermute | solution.py:21
  114.8 8.0 %shard_map.67 = (f32[4,512,128]{2,1,0:T(8,128)}, f32[4,128,128]{2,1,0:T(8,128)}) custom-call(f32[4,72,128]{2,1,0:T(8,128)S(1)} %add.8.own_ref, f32[4,72,128]{2,1,0:T(8,128)S(1)} %collective-permute-done.29.other_ref, f32[4,512,128]{2,1,0:T(8,128)S(1)} %get-tuple-element.33.sketch_ref), custom_call_target="tpu_custom_call" | custom-call | tf_op jit(solution)/shard_map/pallas_call | solution.py:275
  (35 shorter events, 0.1 us)
Async XLA Ops:
  0.6 1.2 copy-start
  1.9 1.2 copy-start.1
  3.1 1.0 copy-start.2
  5.5 0.7 copy-start.11
  6.2 41.8 %collective-permute-start.3 = (bf16[2,128,2048]{2,1,0:T(8,128)(2,1)S(1)}, bf16[2,128,2048]{2,1,0:T(8,128)(2,1)S(1)}, u32[]{:S(2)}, u32[]{:S(2)}) collective-permute-start(bf16[2,128,2048]{2,1,0:T(8,128)(2,1)S(1)} %get-tuple-element.23.refs_0_.turned_ref), channel_id=1, source_target_pairs={{0,4},{4,0},{8,12},{12,8},{16,20},{20,16},{24,28},{28,24},{1,5},{5... | collective-permute-start | bytes 3145736 | tf_op jit(solution)/shard_map/ppermute | solution.py:21
  6.7 9.6 %collective-permute-start.4 = (bf16[1024,128]{1,0:T(8,128)(2,1)S(1)}, bf16[1024,128]{1,0:T(8,128)(2,1)S(1)}, u32[]{:S(2)}, u32[]{:S(2)}) collective-permute-start(bf16[1024,128]{1,0:T(8,128)(2,1)S(1)} %get-tuple-element.24.refs_2_), channel_id=1, source_target_pairs={{0,8},{4,12},{8,0},{12,4},{16,24},{20,28},{24,16},{28,20},{1,9},{5... | collective-permute-start | bytes 786440 | tf_op jit(solution)/shard_map/ppermute | solution.py:21
  9.2 12.8 %collective-permute-start.5 = (bf16[1024,128]{1,0:T(8,128)(2,1)S(1)}, bf16[1024,128]{1,0:T(8,128)(2,1)S(1)}, u32[]{:S(2)}, u32[]{:S(2)}) collective-permute-start(bf16[1024,128]{1,0:T(8,128)(2,1)S(1)} %get-tuple-element.25.refs_3_), channel_id=1, source_target_pairs={{0,8},{4,12},{8,0},{12,4},{16,24},{20,28},{24,16},{28,20},{1,9},{5... | collective-permute-start | bytes 786440 | tf_op jit(solution)/shard_map/ppermute | solution.py:21
  9.2 14.8 %collective-permute-start.6 = (bf16[1024,128]{1,0:T(8,128)(2,1)S(1)}, bf16[1024,128]{1,0:T(8,128)(2,1)S(1)}, u32[]{:S(2)}, u32[]{:S(2)}) collective-permute-start(bf16[1024,128]{1,0:T(8,128)(2,1)S(1)} %get-tuple-element.24.refs_2_), channel_id=1, source_target_pairs={{0,16},{4,20},{8,24},{12,28},{16,0},{20,4},{24,8},{28,12},{1,17},{... | collective-permute-start | bytes 786440 | tf_op jit(solution)/shard_map/ppermute | solution.py:21
  13.3 14.3 %collective-permute-start.16 = (bf16[1024,128]{1,0:T(8,128)(2,1)S(1)}, bf16[1024,128]{1,0:T(8,128)(2,1)S(1)}, u32[]{:S(2)}, u32[]{:S(2)}) collective-permute-start(bf16[1024,128]{1,0:T(8,128)(2,1)S(1)} %get-tuple-element.28.refs_2_), channel_id=1, source_target_pairs={{0,8},{4,12},{8,0},{12,4},{16,24},{20,28},{24,16},{28,20},{1,9},{5... | collective-permute-start | bytes 786440 | tf_op jit(solution)/shard_map/ppermute | solution.py:21
  16.4 13.3 %collective-permute-start.18 = (bf16[1024,128]{1,0:T(8,128)(2,1)S(1)}, bf16[1024,128]{1,0:T(8,128)(2,1)S(1)}, u32[]{:S(2)}, u32[]{:S(2)}) collective-permute-start(bf16[1024,128]{1,0:T(8,128)(2,1)S(1)} %get-tuple-element.28.refs_2_), channel_id=1, source_target_pairs={{0,16},{4,20},{8,24},{12,28},{16,0},{20,4},{24,8},{28,12},{1,17},{... | collective-permute-start | bytes 786440 | tf_op jit(solution)/shard_map/ppermute | solution.py:21
  22.0 11.2 %collective-permute-start.17 = (bf16[1024,128]{1,0:T(8,128)(2,1)S(1)}, bf16[1024,128]{1,0:T(8,128)(2,1)S(1)}, u32[]{:S(2)}, u32[]{:S(2)}) collective-permute-start(bf16[1024,128]{1,0:T(8,128)(2,1)S(1)} %get-tuple-element.29.refs_3_), channel_id=1, source_target_pairs={{0,8},{4,12},{8,0},{12,4},{16,24},{20,28},{24,16},{28,20},{1,9},{5... | collective-permute-start | bytes 786440 | tf_op jit(solution)/shard_map/ppermute | solution.py:21
  24.0 11.3 %collective-permute-start.19 = (bf16[1024,128]{1,0:T(8,128)(2,1)S(1)}, bf16[1024,128]{1,0:T(8,128)(2,1)S(1)}, u32[]{:S(2)}, u32[]{:S(2)}) collective-permute-start(bf16[1024,128]{1,0:T(8,128)(2,1)S(1)} %get-tuple-element.29.refs_3_), channel_id=1, source_target_pairs={{0,16},{4,20},{8,24},{12,28},{16,0},{20,4},{24,8},{28,12},{1,17},{... | collective-permute-start | bytes 786440 | tf_op jit(solution)/shard_map/ppermute | solution.py:21
  27.6 11.2 %collective-permute-start.9 = (bf16[1024,128]{1,0:T(8,128)(2,1)S(1)}, bf16[1024,128]{1,0:T(8,128)(2,1)S(1)}, u32[]{:S(2)}, u32[]{:S(2)}) collective-permute-start(bf16[1024,128]{1,0:T(8,128)(2,1)S(1)} %collective-permute-done.6.refs_6_), channel_id=1, source_target_pairs={{0,8},{4,12},{8,0},{12,4},{16,24},{20,28},{24,16},{28,20},{1,9},{5... | collective-permute-start | bytes 786440 | tf_op jit(solution)/shard_map/ppermute | solution.py:21
  29.6 14.6 %collective-permute-start.21 = (bf16[1024,128]{1,0:T(8,128)(2,1)S(1)}, bf16[1024,128]{1,0:T(8,128)(2,1)S(1)}, u32[]{:S(2)}, u32[]{:S(2)}) collective-permute-start(bf16[1024,128]{1,0:T(8,128)(2,1)S(1)} %collective-permute-done.18.refs_6_), channel_id=1, source_target_pairs={{0,8},{4,12},{8,0},{12,4},{16,24},{20,28},{24,16},{28,20},{1,9},{5... | collective-permute-start | bytes 786440 | tf_op jit(solution)/shard_map/ppermute | solution.py:21
  33.2 11.1 %collective-permute-start.22 = (bf16[1024,128]{1,0:T(8,128)(2,1)S(1)}, bf16[1024,128]{1,0:T(8,128)(2,1)S(1)}, u32[]{:S(2)}, u32[]{:S(2)}) collective-permute-start(bf16[1024,128]{1,0:T(8,128)(2,1)S(1)} %collective-permute-done.17.refs_5_), channel_id=1, source_target_pairs={{0,16},{4,20},{8,24},{12,28},{16,0},{20,4},{24,8},{28,12},{1,17},{... | collective-permute-start | bytes 786440 | tf_op jit(solution)/shard_map/ppermute | solution.py:21
  35.3 12.8 %collective-permute-start.10 = (bf16[1024,128]{1,0:T(8,128)(2,1)S(1)}, bf16[1024,128]{1,0:T(8,128)(2,1)S(1)}, u32[]{:S(2)}, u32[]{:S(2)}) collective-permute-start(bf16[1024,128]{1,0:T(8,128)(2,1)S(1)} %collective-permute-done.5.refs_5_), channel_id=1, source_target_pairs={{0,16},{4,20},{8,24},{12,28},{16,0},{20,4},{24,8},{28,12},{1,17},{... | collective-permute-start | bytes 786440 | tf_op jit(solution)/shard_map/ppermute | solution.py:21
  38.8 13.6 %collective-permute-start.7 = (bf16[1024,128]{1,0:T(8,128)(2,1)S(1)}, bf16[1024,128]{1,0:T(8,128)(2,1)S(1)}, u32[]{:S(2)}, u32[]{:S(2)}) collective-permute-start(bf16[1024,128]{1,0:T(8,128)(2,1)S(1)} %get-tuple-element.25.refs_3_), channel_id=1, source_target_pairs={{0,16},{4,20},{8,24},{12,28},{16,0},{20,4},{24,8},{28,12},{1,17},{... | collective-permute-start | bytes 786440 | tf_op jit(solution)/shard_map/ppermute | solution.py:21
  44.3 8.1 %collective-permute-start.23 = (bf16[1024,128]{1,0:T(8,128)(2,1)S(1)}, bf16[1024,128]{1,0:T(8,128)(2,1)S(1)}, u32[]{:S(2)}, u32[]{:S(2)}) collective-permute-start(bf16[1024,128]{1,0:T(8,128)(2,1)S(1)} %collective-permute-done.21.refs_2_), channel_id=1, source_target_pairs={{0,4},{4,0},{8,12},{12,8},{16,20},{20,16},{24,28},{28,24},{1,5},{5... | collective-permute-start | bytes 786440 | tf_op jit(solution)/shard_map/ppermute | solution.py:21
  44.3 9.8 %collective-permute-start.24 = (bf16[1024,128]{1,0:T(8,128)(2,1)S(1)}, bf16[1024,128]{1,0:T(8,128)(2,1)S(1)}, u32[]{:S(2)}, u32[]{:S(2)}) collective-permute-start(bf16[1024,128]{1,0:T(8,128)(2,1)S(1)} %collective-permute-done.22.refs_3_), channel_id=1, source_target_pairs={{0,4},{4,0},{8,12},{12,8},{16,20},{20,16},{24,28},{28,24},{1,5},{5... | collective-permute-start | bytes 786440 | tf_op jit(solution)/shard_map/ppermute | solution.py:21
  48.1 16.5 %collective-permute-start.11 = (bf16[1024,128]{1,0:T(8,128)(2,1)S(1)}, bf16[1024,128]{1,0:T(8,128)(2,1)S(1)}, u32[]{:S(2)}, u32[]{:S(2)}) collective-permute-start(bf16[1024,128]{1,0:T(8,128)(2,1)S(1)} %collective-permute-done.9.refs_2_), channel_id=1, source_target_pairs={{0,4},{4,0},{8,12},{12,8},{16,20},{20,16},{24,28},{28,24},{1,5},{5... | collective-permute-start | bytes 786440 | tf_op jit(solution)/shard_map/ppermute | solution.py:21
  48.1 16.8 %collective-permute-start.12 = (bf16[1024,128]{1,0:T(8,128)(2,1)S(1)}, bf16[1024,128]{1,0:T(8,128)(2,1)S(1)}, u32[]{:S(2)}, u32[]{:S(2)}) collective-permute-start(bf16[1024,128]{1,0:T(8,128)(2,1)S(1)} %collective-permute-done.10.refs_3_), channel_id=1, source_target_pairs={{0,4},{4,0},{8,12},{12,8},{16,20},{20,16},{24,28},{28,24},{1,5},{5... | collective-permute-start | bytes 786440 | tf_op jit(solution)/shard_map/ppermute | solution.py:21
  52.4 6.9 %collective-permute-start.20 = (bf16[3,128,128]{2,1,0:T(8,128)(2,1)S(1)}, bf16[3,128,128]{2,1,0:T(8,128)(2,1)S(1)}, u32[]{:S(2)}, u32[]{:S(2)}) collective-permute-start(bf16[3,128,128]{2,1,0:T(8,128)(2,1)S(1)} %get-tuple-element.31), channel_id=1, source_target_pairs={{0,4},{4,0},{8,12},{12,8},{16,20},{20,16},{24,28},{28,24},{1,5},{5... | collective-permute-start | bytes 294920 | tf_op jit(solution)/shard_map/ppermute | solution.py:21
  52.4 6.3 %copy-start.3 = (bf16[1024,128]{1,0:T(8,128)(2,1)}, bf16[1024,128]{1,0:T(8,128)(2,1)S(1)}, u32[]{:S(2)}) copy-start(bf16[1024,128]{1,0:T(8,128)(2,1)S(1)} %collective-permute-done.23.refs_4_) | copy-start | bytes 786436
  52.4 16.7 %collective-permute-start = (bf16[2,512,128]{2,1,0:T(8,128)(2,1)}, bf16[2,512,128]{2,1,0:T(8,128)(2,1)S(1)}, u32[]{:S(2)}, u32[]{:S(2)}) collective-permute-start(bf16[2,512,128]{2,1,0:T(8,128)(2,1)} %get-tuple-element.20), channel_id=1, source_target_pairs={{0,1},{1,0},{2,3},{3,2},{4,5},{5,4},{6,7},{7,6},{8,9},{9,8},{10,11... | collective-permute-start | bytes 786440 | tf_op jit(solution)/shard_map/ppermute | solution.py:21
  54.0 0.7 copy-start.5
  54.8 35.7 %collective-permute-start.1 = (bf16[2,512,128]{2,1,0:T(8,128)(2,1)}, bf16[2,512,128]{2,1,0:T(8,128)(2,1)S(1)}, u32[]{:S(2)}, u32[]{:S(2)}) collective-permute-start(bf16[2,512,128]{2,1,0:T(8,128)(2,1)} %get-tuple-element.21), channel_id=1, source_target_pairs={{0,2},{1,3},{2,0},{3,1},{4,6},{5,7},{6,4},{7,5},{8,10},{9,11},{10,... | collective-permute-start | bytes 786440 | tf_op jit(solution)/shard_map/ppermute | solution.py:21
  58.7 0.6 copy-start.7
  59.3 0.6 copy-start.9
  60.0 6.6 %collective-permute-start.8 = (bf16[3,128,128]{2,1,0:T(8,128)(2,1)}, bf16[3,128,128]{2,1,0:T(8,128)(2,1)}, u32[]{:S(2)}, u32[]{:S(2)}) collective-permute-start(bf16[3,128,128]{2,1,0:T(8,128)(2,1)} %get-tuple-element.27), channel_id=1, source_target_pairs={{0,4},{4,0},{8,12},{12,8},{16,20},{20,16},{24,28},{28,24},{1,5},{5... | collective-permute-start | bytes 294920 | tf_op jit(solution)/shard_map/ppermute | solution.py:21
  60.0 0.7 copy-start.13
  60.8 1.0 copy-start.4
  61.8 0.9 copy-start.6
  62.7 0.9 copy-start.10
  63.6 0.9 copy-start.12
  63.6 2.9 %copy-start.8 = (bf16[3,128,128]{2,1,0:T(8,128)(2,1)S(1)}, bf16[3,128,128]{2,1,0:T(8,128)(2,1)}, u32[]{:S(2)}) copy-start(bf16[3,128,128]{2,1,0:T(8,128)(2,1)} %copy-done.7) | copy-start | bytes 294916
  64.6 28.0 %collective-permute-start.2 = (bf16[2,512,128]{2,1,0:T(8,128)(2,1)S(1)}, bf16[2,512,128]{2,1,0:T(8,128)(2,1)S(1)}, u32[]{:S(2)}, u32[]{:S(2)}) collective-permute-start(bf16[2,512,128]{2,1,0:T(8,128)(2,1)S(1)} %copy-done.12), channel_id=1, source_target_pairs={{0,3},{1,2},{2,1},{3,0},{4,7},{5,6},{6,5},{7,4},{8,11},{9,10},{10,... | collective-permute-start | bytes 786440 | tf_op jit(solution)/shard_map/ppermute | solution.py:21
  64.8 25.6 %collective-permute-start.26 = (bf16[128,512]{1,0:T(8,128)(2,1)S(1)}, bf16[128,512]{1,0:T(8,128)(2,1)S(1)}, u32[]{:S(2)}, u32[]{:S(2)}) collective-permute-start(bf16[128,512]{1,0:T(8,128)(2,1)S(1)} %shard_map.64.refs_4_), channel_id=1, source_target_pairs={{0,2},{1,3},{2,0},{3,1},{4,6},{5,7},{6,4},{7,5},{8,10},{9,11},{10,... | collective-permute-start | bytes 393224 | tf_op jit(solution)/shard_map/ppermute | solution.py:21
  67.8 24.8 %collective-permute-start.14 = (bf16[128,512]{1,0:T(8,128)(2,1)S(1)}, bf16[128,512]{1,0:T(8,128)(2,1)S(1)}, u32[]{:S(2)}, u32[]{:S(2)}) collective-permute-start(bf16[128,512]{1,0:T(8,128)(2,1)S(1)} %shard_map.61.refs_4_), channel_id=1, source_target_pairs={{0,2},{1,3},{2,0},{3,1},{4,6},{5,7},{6,4},{7,5},{8,10},{9,11},{10,... | collective-permute-start | bytes 393224 | tf_op jit(solution)/shard_map/ppermute | solution.py:21
  69.1 23.4 %collective-permute-start.25 = (bf16[128,512]{1,0:T(8,128)(2,1)S(1)}, bf16[128,512]{1,0:T(8,128)(2,1)S(1)}, u32[]{:S(2)}, u32[]{:S(2)}) collective-permute-start(bf16[128,512]{1,0:T(8,128)(2,1)S(1)} %shard_map.64.refs_4_), channel_id=1, source_target_pairs={{0,1},{1,0},{2,3},{3,2},{4,5},{5,4},{6,7},{7,6},{8,9},{9,8},{10,11... | collective-permute-start | bytes 393224 | tf_op jit(solution)/shard_map/ppermute | solution.py:21
  90.4 6.4 %collective-permute-start.27 = (bf16[128,512]{1,0:T(8,128)(2,1)S(1)}, bf16[128,512]{1,0:T(8,128)(2,1)S(1)}, u32[]{:S(2)}, u32[]{:S(2)}) collective-permute-start(bf16[128,512]{1,0:T(8,128)(2,1)S(1)} %collective-permute-done.26.refs_6_), channel_id=1, source_target_pairs={{0,1},{1,0},{2,3},{3,2},{4,5},{5,4},{6,7},{7,6},{8,9},{9,8},{10,11... | collective-permute-start | bytes 393224 | tf_op jit(solution)/shard_map/ppermute | solution.py:21
  90.4 9.0 %collective-permute-start.13 = (bf16[128,512]{1,0:T(8,128)(2,1)S(1)}, bf16[128,512]{1,0:T(8,128)(2,1)S(1)}, u32[]{:S(2)}, u32[]{:S(2)}) collective-permute-start(bf16[128,512]{1,0:T(8,128)(2,1)S(1)} %shard_map.61.refs_4_), channel_id=1, source_target_pairs={{0,1},{1,0},{2,3},{3,2},{4,5},{5,4},{6,7},{7,6},{8,9},{9,8},{10,11... | collective-permute-start | bytes 393224 | tf_op jit(solution)/shard_map/ppermute | solution.py:21
  92.5 8.3 %collective-permute-start.15 = (bf16[128,512]{1,0:T(8,128)(2,1)S(1)}, bf16[128,512]{1,0:T(8,128)(2,1)S(1)}, u32[]{:S(2)}, u32[]{:S(2)}) collective-permute-start(bf16[128,512]{1,0:T(8,128)(2,1)S(1)} %collective-permute-done.14.refs_6_), channel_id=1, source_target_pairs={{0,1},{1,0},{2,3},{3,2},{4,5},{5,4},{6,7},{7,6},{8,9},{9,8},{10,11... | collective-permute-start | bytes 393224 | tf_op jit(solution)/shard_map/ppermute | solution.py:21
  102.4 5.2 %collective-permute-start.28 = (f32[4,72,128]{2,1,0:T(8,128)S(1)}, f32[4,72,128]{2,1,0:T(8,128)S(1)}, u32[]{:S(2)}, u32[]{:S(2)}) collective-permute-start(f32[4,72,128]{2,1,0:T(8,128)S(1)} %get-tuple-element.32), channel_id=1, source_target_pairs={{0,1},{1,0},{2,3},{3,2},{4,5},{5,4},{6,7},{7,6},{8,9},{9,8},{10,11... | collective-permute-start | bytes 442376 | tf_op jit(solution)/shard_map/ppermute | solution.py:21
  107.6 7.2 %collective-permute-start.29 = (f32[4,72,128]{2,1,0:T(8,128)S(1)}, f32[4,72,128]{2,1,0:T(8,128)S(1)}, u32[]{:S(2)}, u32[]{:S(2)}) collective-permute-start(f32[4,72,128]{2,1,0:T(8,128)S(1)} %add.8.own_ref), channel_id=1, source_target_pairs={{0,2},{1,3},{2,0},{3,1},{4,6},{5,7},{6,4},{7,5},{8,10},{9,11},{10,... | collective-permute-start | bytes 442376 | tf_op jit(solution)/shard_map/ppermute | solution.py:21

commit v2 on v1

--- a/solution.py
+++ b/solution.py
@@ -82,15 +82,18 @@
 
 def second_kernel(count, level_ref, left_ref, right_ref, probe_ref, *outs):
     panels = left_ref.shape[1]
+    outs, (probe_buf, sems) = outs[:-2], outs[-2:]
     turned_ref, block_refs = outs[2 * panels - 2], outs[2 * panels - 1:]
-    probe_turned = probe_ref[...].T
-    for p in range(1, panels):
-        rows_of(probe_turned, left_ref.at[0, p], right_ref.at[0, p], *outs[2 * p - 2:2 * p])
+    (copy,) = fetch([(probe_ref, probe_buf)], sems)
     part = left_ref.shape[2] // count
     for p in range(panels):
         turned_ref[p] = right_ref[0, p].T
         for o, ref in enumerate(block_refs):
             ref[p] = left_ref[0, p, pl.ds(pl.multiple_of((level_ref[0] ^ o) * part, part), part), :]
+    copy.wait()
+    probe_turned = probe_buf[...].T
+    for p in range(1, panels):
+        rows_of(probe_turned, left_ref.at[0, p], right_ref.at[0, p], *outs[2 * p - 2:2 * p])
 
 
 def couple(turned_refs, panel, blocks):
@@ -305,7 +308,9 @@
         (shape((half, width), bf16),) * (2 * panels - 2)
         + (shape((panels, rank_size, tile_size), bf16),)
         + (shape((panels, part, rank_size), bf16),) * depth_size,
-        level[None], left_factors, right_factors, probe_matrix, in_specs=[SMEM] + [VMEM] * 3,
+        level[None], left_factors, right_factors, probe_matrix,
+        in_specs=[SMEM, VMEM, VMEM, HBM],
+        scratch_shapes=[pltpu.VMEM((tile_size, width), bf16), pltpu.SemaphoreType.DMA((1,))],
     )
     halves = list(halves) + list(second[:2 * panels - 2])
     turned, blocks = [second[2 * panels - 2]], second[2 * panels - 1:]

time: 123 us -> 123 us (level)
    unnamed x28 -> x26, local copies, waits for them, and re-layouts: 9.71 us -> 8.68 us
where the time goes in v2:
time: 123 us; the launch traced here: 122 us
  waiting for transfers between devices  63.4 us (52%)
  starting transfers between devices  31.3 us (25%)
  Pallas kernels  18 us (15%)
  local copies, waits for them, and re-layouts  8.68 us (7%)
    ppermute x30, waiting for transfers between devices, swap(): return lax.ppermute(x, axis, [(i, i ^ bits) for i in range(size)])  63.4 us
    ppermute x30, starting transfers between devices, swap(): return lax.ppermute(x, axis, [(i, i ^ bits) for i in range(size)])  31.3 us
    pallas_call x9, Pallas kernels, call(): pl.pallas_call(kernel, out_shape=shapes, in_specs=specs, out_specs=out, c...  18 us
    unnamed x26, local copies, waits for them, and re-layouts  8.68 us
  transfers between devices with their start and end apart: 30, of which 15 were waited for; matrix products, arithmetic and copies ran while one was open for 0% of the time, Pallas kernels for 5%

profile of v2, /device:TPU:0, one launch (start us, length us, event | category | flops | bytes accessed | tf_op | source)
XLA Modules:
  0.0 122.3 jit_solution(16139453096008950155)
XLA Ops:
  0.6 0.0 copy-start
  0.6 1.2 copy-done
  1.9 1.2 copy-done.1
  3.1 2.0 %shard_map.59 = (bf16[1024,128]{1,0:T(8,128)(2,1)S(1)}, bf16[1024,128]{1,0:T(8,128)(2,1)S(1)}, bf16[2,128,2048]{2,1,0:T(8,128)(2,1)S(1)}, bf16[2,512,128]{2,1,0:...) custom-call(s32[1]{0:T(128)} %bitcast.level_ref, ...), custom_call_target="tpu_custom_call" | custom-call | tf_op jit(solution)/shard_map/pallas_call | solution.py:278
  5.1 0.7 copy-done.10
  5.8 0.5 collective-permute-start.3
  6.3 2.5 %collective-permute-start.4 = (bf16[1024,128]{1,0:T(8,128)(2,1)S(1)}, bf16[1024,128]{1,0:T(8,128)(2,1)S(1)}, u32[]{:S(2)}, u32[]{:S(2)}) collective-permute-start(bf16[1024,128]{1,0:T(8,128)(2,1)S(1)} %get-tuple-element.24.refs_2_), channel_id=1, source_target_pairs={{0,8},{4,12},{8,0},{12,4},{16,24},{20,28},{24,16},{28,20},{1,9},{5... | collective-permute-start | bytes 786440 | tf_op jit(solution)/shard_map/ppermute | solution.py:21
  8.7 0.0 collective-permute-start.5
  8.8 2.0 %collective-permute-start.6 = (bf16[1024,128]{1,0:T(8,128)(2,1)S(1)}, bf16[1024,128]{1,0:T(8,128)(2,1)S(1)}, u32[]{:S(2)}, u32[]{:S(2)}) collective-permute-start(bf16[1024,128]{1,0:T(8,128)(2,1)S(1)} %get-tuple-element.24.refs_2_), channel_id=1, source_target_pairs={{0,16},{4,20},{8,24},{12,28},{16,0},{20,4},{24,8},{28,12},{1,17},{... | collective-permute-start | bytes 786440 | tf_op jit(solution)/shard_map/ppermute | solution.py:21
  10.8 2.0 %shard_map.62 = (bf16[1024,128]{1,0:T(8,128)(2,1)S(1)}, bf16[1024,128]{1,0:T(8,128)(2,1)S(1)}) custom-call(bf16[1,2,2048,128]{3,2,1,0:T(8,128)(2,1)} %left_ref.3, bf16[1,2,2048,128]{3,2,1,0:T(8,128)(2,1)} %right_ref.3, bf16[2048,128]{1,0:T(8,128)(2,1)} %probe_ref.3), custom_call_target="tpu_custom_call" | custom-call | tf_op jit(solution)/shard_map/pallas_call | solution.py:278
  12.8 1.6 %collective-permute-start.16 = (bf16[1024,128]{1,0:T(8,128)(2,1)S(1)}, bf16[1024,128]{1,0:T(8,128)(2,1)S(1)}, u32[]{:S(2)}, u32[]{:S(2)}) collective-permute-start(bf16[1024,128]{1,0:T(8,128)(2,1)S(1)} %get-tuple-element.28.refs_2_), channel_id=1, source_target_pairs={{0,8},{4,12},{8,0},{12,4},{16,24},{20,28},{24,16},{28,20},{1,9},{5... | collective-permute-start | bytes 786440 | tf_op jit(solution)/shard_map/ppermute | solution.py:21
  14.4 1.5 %collective-permute-done.4.refs_4_ = bf16[1024,128]{1,0:T(8,128)(2,1)S(1)} collective-permute-done((bf16[1024,128]{1,0:T(8,128)(2,1)S(1)}, bf16[1024,128]{1,0:T(8,128)(2,1)S(1)}, u32[]{:S(2)}, u32[]{:S(2)}) %collective-permute-start.4) | collective-permute-done | bytes 262176 | tf_op jit(solution)/shard_map/ppermute | solution.py:21
  15.9 2.1 %collective-permute-start.18 = (bf16[1024,128]{1,0:T(8,128)(2,1)S(1)}, bf16[1024,128]{1,0:T(8,128)(2,1)S(1)}, u32[]{:S(2)}, u32[]{:S(2)}) collective-permute-start(bf16[1024,128]{1,0:T(8,128)(2,1)S(1)} %get-tuple-element.28.refs_2_), channel_id=1, source_target_pairs={{0,16},{4,20},{8,24},{12,28},{16,0},{20,4},{24,8},{28,12},{1,17},{... | collective-permute-start | bytes 786440 | tf_op jit(solution)/shard_map/ppermute | solution.py:21
  18.0 3.6 %collective-permute-done.5.refs_5_ = bf16[1024,128]{1,0:T(8,128)(2,1)S(1)} collective-permute-done((bf16[1024,128]{1,0:T(8,128)(2,1)S(1)}, bf16[1024,128]{1,0:T(8,128)(2,1)S(1)}, u32[]{:S(2)}, u32[]{:S(2)}) %collective-permute-start.5) | collective-permute-done | bytes 262176 | tf_op jit(solution)/shard_map/ppermute | solution.py:21
  21.5 2.0 %collective-permute-start.17 = (bf16[1024,128]{1,0:T(8,128)(2,1)S(1)}, bf16[1024,128]{1,0:T(8,128)(2,1)S(1)}, u32[]{:S(2)}, u32[]{:S(2)}) collective-permute-start(bf16[1024,128]{1,0:T(8,128)(2,1)S(1)} %get-tuple-element.29.refs_3_), channel_id=1, source_target_pairs={{0,8},{4,12},{8,0},{12,4},{16,24},{20,28},{24,16},{28,20},{1,9},{5... | collective-permute-start | bytes 786440 | tf_op jit(solution)/shard_map/ppermute | solution.py:21
  23.5 0.0 collective-permute-done.6.refs_6_
  23.5 1.5 %collective-permute-start.19 = (bf16[1024,128]{1,0:T(8,128)(2,1)S(1)}, bf16[1024,128]{1,0:T(8,128)(2,1)S(1)}, u32[]{:S(2)}, u32[]{:S(2)}) collective-permute-start(bf16[1024,128]{1,0:T(8,128)(2,1)S(1)} %get-tuple-element.29.refs_3_), channel_id=1, source_target_pairs={{0,16},{4,20},{8,24},{12,28},{16,0},{20,4},{24,8},{28,12},{1,17},{... | collective-permute-start | bytes 786440 | tf_op jit(solution)/shard_map/ppermute | solution.py:21
  25.1 2.1 %collective-permute-done.16.refs_4_ = bf16[1024,128]{1,0:T(8,128)(2,1)S(1)} collective-permute-done((bf16[1024,128]{1,0:T(8,128)(2,1)S(1)}, bf16[1024,128]{1,0:T(8,128)(2,1)S(1)}, u32[]{:S(2)}, u32[]{:S(2)}) %collective-permute-start.16) | collective-permute-done | bytes 262176 | tf_op jit(solution)/shard_map/ppermute | solution.py:21
  27.1 2.0 %collective-permute-start.9 = (bf16[1024,128]{1,0:T(8,128)(2,1)S(1)}, bf16[1024,128]{1,0:T(8,128)(2,1)S(1)}, u32[]{:S(2)}, u32[]{:S(2)}) collective-permute-start(bf16[1024,128]{1,0:T(8,128)(2,1)S(1)} %collective-permute-done.6.refs_6_), channel_id=1, source_target_pairs={{0,8},{4,12},{8,0},{12,4},{16,24},{20,28},{24,16},{28,20},{1,9},{5... | collective-permute-start | bytes 786440 | tf_op jit(solution)/shard_map/ppermute | solution.py:21
  29.2 0.0 collective-permute-start.21
  29.2 3.6 %collective-permute-done.17.refs_5_ = bf16[1024,128]{1,0:T(8,128)(2,1)S(1)} collective-permute-done((bf16[1024,128]{1,0:T(8,128)(2,1)S(1)}, bf16[1024,128]{1,0:T(8,128)(2,1)S(1)}, u32[]{:S(2)}, u32[]{:S(2)}) %collective-permute-start.17) | collective-permute-done | bytes 262176 | tf_op jit(solution)/shard_map/ppermute | solution.py:21
  32.8 2.1 %collective-permute-start.22 = (bf16[1024,128]{1,0:T(8,128)(2,1)S(1)}, bf16[1024,128]{1,0:T(8,128)(2,1)S(1)}, u32[]{:S(2)}, u32[]{:S(2)}) collective-permute-start(bf16[1024,128]{1,0:T(8,128)(2,1)S(1)} %collective-permute-done.17.refs_5_), channel_id=1, source_target_pairs={{0,16},{4,20},{8,24},{12,28},{16,0},{20,4},{24,8},{28,12},{1,17},{... | collective-permute-start | bytes 786440 | tf_op jit(solution)/shard_map/ppermute | solution.py:21
  34.8 0.0 collective-permute-start.10
  34.8 3.5 %collective-permute-done.9.refs_2_ = bf16[1024,128]{1,0:T(8,128)(2,1)S(1)} collective-permute-done((bf16[1024,128]{1,0:T(8,128)(2,1)S(1)}, bf16[1024,128]{1,0:T(8,128)(2,1)S(1)}, u32[]{:S(2)}, u32[]{:S(2)}) %collective-permute-start.9) | collective-permute-done | bytes 262176 | tf_op jit(solution)/shard_map/ppermute | solution.py:21
  38.4 2.1 %collective-permute-start.7 = (bf16[1024,128]{1,0:T(8,128)(2,1)S(1)}, bf16[1024,128]{1,0:T(8,128)(2,1)S(1)}, u32[]{:S(2)}, u32[]{:S(2)}) collective-permute-start(bf16[1024,128]{1,0:T(8,128)(2,1)S(1)} %get-tuple-element.25.refs_3_), channel_id=1, source_target_pairs={{0,16},{4,20},{8,24},{12,28},{16,0},{20,4},{24,8},{28,12},{1,17},{... | collective-permute-start | bytes 786440 | tf_op jit(solution)/shard_map/ppermute | solution.py:21
  40.4 3.4 %collective-permute-done.21.refs_2_ = bf16[1024,128]{1,0:T(8,128)(2,1)S(1)} collective-permute-done((bf16[1024,128]{1,0:T(8,128)(2,1)S(1)}, bf16[1024,128]{1,0:T(8,128)(2,1)S(1)}, u32[]{:S(2)}, u32[]{:S(2)}) %collective-permute-start.21) | collective-permute-done | bytes 262176 | tf_op jit(solution)/shard_map/ppermute | solution.py:21
  43.8 0.5 collective-permute-start.24
  44.3 3.3 %collective-permute-done.10.refs_3_ = bf16[1024,128]{1,0:T(8,128)(2,1)S(1)} collective-permute-done((bf16[1024,128]{1,0:T(8,128)(2,1)S(1)}, bf16[1024,128]{1,0:T(8,128)(2,1)S(1)}, u32[]{:S(2)}, u32[]{:S(2)}) %collective-permute-start.10) | collective-permute-done | bytes 262176 | tf_op jit(solution)/shard_map/ppermute | solution.py:21
  47.6 0.0 collective-permute-start.11
  47.6 0.0 collective-permute-done.3.refs_1_
  47.6 0.5 collective-permute-start.12
  48.1 0.7 shard_map.63
  48.8 3.1 %collective-permute-done.7.refs_7_ = bf16[1024,128]{1,0:T(8,128)(2,1)S(1)} collective-permute-done((bf16[1024,128]{1,0:T(8,128)(2,1)S(1)}, bf16[1024,128]{1,0:T(8,128)(2,1)S(1)}, u32[]{:S(2)}, u32[]{:S(2)}) %collective-permute-start.7) | collective-permute-done | bytes 262176 | tf_op jit(solution)/shard_map/ppermute | solution.py:21
  52.0 1.6 %collective-permute-start = (bf16[2,512,128]{2,1,0:T(8,128)(2,1)}, bf16[2,512,128]{2,1,0:T(8,128)(2,1)S(1)}, u32[]{:S(2)}, u32[]{:S(2)}) collective-permute-start(bf16[2,512,128]{2,1,0:T(8,128)(2,1)} %get-tuple-element.20), channel_id=1, source_target_pairs={{0,1},{1,0},{2,3},{3,2},{4,5},{5,4},{6,7},{7,6},{8,9},{9,8},{10,11... | collective-permute-start | bytes 786440 | tf_op jit(solution)/shard_map/ppermute | solution.py:21
  53.6 0.7 copy-done.4
  54.3 2.6 %collective-permute-start.1 = (bf16[2,512,128]{2,1,0:T(8,128)(2,1)}, bf16[2,512,128]{2,1,0:T(8,128)(2,1)S(1)}, u32[]{:S(2)}, u32[]{:S(2)}) collective-permute-start(bf16[2,512,128]{2,1,0:T(8,128)(2,1)} %get-tuple-element.21), channel_id=1, source_target_pairs={{0,2},{1,3},{2,0},{3,1},{4,6},{5,7},{6,4},{7,5},{8,10},{9,11},{10,... | collective-permute-start | bytes 786440 | tf_op jit(solution)/shard_map/ppermute | solution.py:21
  56.9 1.3 %shard_map.60 = (bf16[3,128,128]{2,1,0:T(8,128)(2,1)S(1)}, bf16[3,128,128]{2,1,0:T(8,128)(2,1)}) custom-call(bf16[2,128,2048]{2,1,0:T(8,128)(2,1)S(1)} %get-tuple-element.23.refs_0_.turned_ref, bf16[2,128,2048]{2,1,0:T(8,128)(2,1)S(1)} %collective-permute-done.3.refs_1_, bf16[1024,128]{1,0:T(8,128)(2,1)S(1)} %get-tuple-element.24.refs_2_, ...), custom_call_target="tpu_custom_call" | custom-call | tf_op jit(solution)/shard_map/pallas_call | solution.py:278
  58.2 0.6 copy-done.6
  58.9 0.6 copy-done.8
  59.5 0.7 copy-done.12
  60.2 0.2 xor_reduce_fusion.wanted_ref
  60.4 0.9 copy-done.3
  61.3 0.9 copy-done.5
  62.3 0.9 copy-done.9
  63.2 0.9 shard_map.64.refs_4_
  64.1 0.1 copy-done.11
  64.1 0.3 collective-permute-start.2
  64.4 1.7 %collective-permute-start.26 = (bf16[128,512]{1,0:T(8,128)(2,1)S(1)}, bf16[128,512]{1,0:T(8,128)(2,1)S(1)}, u32[]{:S(2)}, u32[]{:S(2)}) collective-permute-start(bf16[128,512]{1,0:T(8,128)(2,1)S(1)} %shard_map.64.refs_4_), channel_id=1, source_target_pairs={{0,2},{1,3},{2,0},{3,1},{4,6},{5,7},{6,4},{7,5},{8,10},{9,11},{10,... | collective-permute-start | bytes 393224 | tf_op jit(solution)/shard_map/ppermute | solution.py:21
  66.1 1.2 %shard_map.61.refs_4_ = bf16[128,512]{1,0:T(8,128)(2,1)S(1)} custom-call(s32[4]{0:T(128)S(1)} %xor_reduce_fusion.wanted_ref, bf16[2,128,2048]{2,1,0:T(8,128)(2,1)S(1)} %get-tuple-element.23.refs_0_.turned_ref, bf16[3,128,128]{2,1,0:T(8,128)(2,1)S(1)} %copy-done.7, bf16[3,128,128]{2,1,0:T(8,128)(2,1)} %collective-permute-done.8.refs_1_, ...), custom_call_target="tpu_custom_call" | custom-call | tf_op jit(solution)/shard_map/pallas_call | solution.py:278
  67.3 1.3 %collective-permute-start.14 = (bf16[128,512]{1,0:T(8,128)(2,1)S(1)}, bf16[128,512]{1,0:T(8,128)(2,1)S(1)}, u32[]{:S(2)}, u32[]{:S(2)}) collective-permute-start(bf16[128,512]{1,0:T(8,128)(2,1)S(1)} %shard_map.61.refs_4_), channel_id=1, source_target_pairs={{0,2},{1,3},{2,0},{3,1},{4,6},{5,7},{6,4},{7,5},{8,10},{9,11},{10,... | collective-permute-start | bytes 393224 | tf_op jit(solution)/shard_map/ppermute | solution.py:21
  68.6 1.3 %collective-permute-start.25 = (bf16[128,512]{1,0:T(8,128)(2,1)S(1)}, bf16[128,512]{1,0:T(8,128)(2,1)S(1)}, u32[]{:S(2)}, u32[]{:S(2)}) collective-permute-start(bf16[128,512]{1,0:T(8,128)(2,1)S(1)} %shard_map.64.refs_4_), channel_id=1, source_target_pairs={{0,1},{1,0},{2,3},{3,2},{4,5},{5,4},{6,7},{7,6},{8,9},{9,8},{10,11... | collective-permute-start | bytes 393224 | tf_op jit(solution)/shard_map/ppermute | solution.py:21
  69.9 20.0 %collective-permute-done.26.refs_6_ = bf16[128,512]{1,0:T(8,128)(2,1)S(1)} collective-permute-done((bf16[128,512]{1,0:T(8,128)(2,1)S(1)}, bf16[128,512]{1,0:T(8,128)(2,1)S(1)}, u32[]{:S(2)}, u32[]{:S(2)}) %collective-permute-start.26) | collective-permute-done | bytes 131104 | tf_op jit(solution)/shard_map/ppermute | solution.py:21
  90.0 2.0 %collective-permute-start.13 = (bf16[128,512]{1,0:T(8,128)(2,1)S(1)}, bf16[128,512]{1,0:T(8,128)(2,1)S(1)}, u32[]{:S(2)}, u32[]{:S(2)}) collective-permute-start(bf16[128,512]{1,0:T(8,128)(2,1)S(1)} %shard_map.61.refs_4_), channel_id=1, source_target_pairs={{0,1},{1,0},{2,3},{3,2},{4,5},{5,4},{6,7},{7,6},{8,9},{9,8},{10,11... | collective-permute-start | bytes 393224 | tf_op jit(solution)/shard_map/ppermute | solution.py:21
  92.0 0.1 collective-permute-done.14.refs_6_
  92.1 4.3 %collective-permute-done.27.refs_7_ = bf16[128,512]{1,0:T(8,128)(2,1)S(1)} collective-permute-done((bf16[128,512]{1,0:T(8,128)(2,1)S(1)}, bf16[128,512]{1,0:T(8,128)(2,1)S(1)}, u32[]{:S(2)}, u32[]{:S(2)}) %collective-permute-start.27) | collective-permute-done | bytes 131104 | tf_op jit(solution)/shard_map/ppermute | solution.py:21
  96.3 0.4 shard_map.65.refs_8_
  96.8 2.2 %collective-permute-done.13.refs_5_ = bf16[128,512]{1,0:T(8,128)(2,1)S(1)} collective-permute-done((bf16[128,512]{1,0:T(8,128)(2,1)S(1)}, bf16[128,512]{1,0:T(8,128)(2,1)S(1)}, u32[]{:S(2)}, u32[]{:S(2)}) %collective-permute-start.13) | collective-permute-done | bytes 131104 | tf_op jit(solution)/shard_map/ppermute | solution.py:21
  99.0 1.4 %collective-permute-done.15.refs_7_ = bf16[128,512]{1,0:T(8,128)(2,1)S(1)} collective-permute-done((bf16[128,512]{1,0:T(8,128)(2,1)S(1)}, bf16[128,512]{1,0:T(8,128)(2,1)S(1)}, u32[]{:S(2)}, u32[]{:S(2)}) %collective-permute-start.15) | collective-permute-done | bytes 131104 | tf_op jit(solution)/shard_map/ppermute | solution.py:21
  100.4 1.5 %shard_map.66 = (f32[4,512,128]{2,1,0:T(8,128)S(1)}, f32[4,72,128]{2,1,0:T(8,128)S(1)}) custom-call(bf16[2,512,128]{2,1,0:T(8,128)(2,1)S(1)} %get-tuple-element.19.refs_0_, bf16[2,512,128]{2,1,0:T(8,128)(2,1)S(1)} %collective-permute-done.refs_1_, bf16[2,512,128]{2,1,0:T(8,128)(2,1)S(1)} %collective-permute-done.1.refs_2_, ...), custom_call_target="tpu_custom_call" | custom-call | tf_op jit(solution)/shard_map/pallas_call | solution.py:278
  101.9 0.1 collective-permute-start.28
  102.0 5.1 %collective-permute-done.28 = f32[4,72,128]{2,1,0:T(8,128)S(1)} collective-permute-done((f32[4,72,128]{2,1,0:T(8,128)S(1)}, f32[4,72,128]{2,1,0:T(8,128)S(1)}, u32[]{:S(2)}, u32[]{:S(2)}) %collective-permute-start.28) | collective-permute-done | bytes 147488 | tf_op jit(solution)/shard_map/ppermute | solution.py:21
  107.1 1.0 collective-permute-start.29
  108.2 6.2 %collective-permute-done.29.other_ref = f32[4,72,128]{2,1,0:T(8,128)S(1)} collective-permute-done((f32[4,72,128]{2,1,0:T(8,128)S(1)}, f32[4,72,128]{2,1,0:T(8,128)S(1)}, u32[]{:S(2)}, u32[]{:S(2)}) %collective-permute-start.29) | collective-permute-done | bytes 147488 | tf_op jit(solution)/shard_map/ppermute | solution.py:21
  114.3 8.0 %shard_map.67 = (f32[4,512,128]{2,1,0:T(8,128)}, f32[4,128,128]{2,1,0:T(8,128)}) custom-call(f32[4,72,128]{2,1,0:T(8,128)S(1)} %add.8.own_ref, f32[4,72,128]{2,1,0:T(8,128)S(1)} %collective-permute-done.29.other_ref, f32[4,512,128]{2,1,0:T(8,128)S(1)} %get-tuple-element.33.sketch_ref), custom_call_target="tpu_custom_call" | custom-call | tf_op jit(solution)/shard_map/pallas_call | solution.py:278
  (33 shorter events, 0.1 us)
Async XLA Ops:
  0.6 1.2 %copy-start = (bf16[1,2,2048,128]{3,2,1,0:T(8,128)(2,1)S(1)}, bf16[1,2,2048,128]{3,2,1,0:T(8,128)(2,1)}, u32[]{:S(2)}) copy-start(bf16[1,2,2048,128]{3,2,1,0:T(8,128)(2,1)} %left_ref.3) | copy-start | bytes 3145732
  1.9 1.2 %copy-start.1 = (bf16[1,2,2048,128]{3,2,1,0:T(8,128)(2,1)S(1)}, bf16[1,2,2048,128]{3,2,1,0:T(8,128)(2,1)}, u32[]{:S(2)}) copy-start(bf16[1,2,2048,128]{3,2,1,0:T(8,128)(2,1)} %right_ref.3) | copy-start | bytes 3145732
  5.1 0.7 copy-start.10
  5.8 41.8 %collective-permute-start.3 = (bf16[2,128,2048]{2,1,0:T(8,128)(2,1)S(1)}, bf16[2,128,2048]{2,1,0:T(8,128)(2,1)S(1)}, u32[]{:S(2)}, u32[]{:S(2)}) collective-permute-start(bf16[2,128,2048]{2,1,0:T(8,128)(2,1)S(1)} %get-tuple-element.23.refs_0_.turned_ref), channel_id=1, source_target_pairs={{0,4},{4,0},{8,12},{12,8},{16,20},{20,16},{24,28},{28,24},{1,5},{5... | collective-permute-start | bytes 3145736 | tf_op jit(solution)/shard_map/ppermute | solution.py:21
  6.3 9.6 %collective-permute-start.4 = (bf16[1024,128]{1,0:T(8,128)(2,1)S(1)}, bf16[1024,128]{1,0:T(8,128)(2,1)S(1)}, u32[]{:S(2)}, u32[]{:S(2)}) collective-permute-start(bf16[1024,128]{1,0:T(8,128)(2,1)S(1)} %get-tuple-element.24.refs_2_), channel_id=1, source_target_pairs={{0,8},{4,12},{8,0},{12,4},{16,24},{20,28},{24,16},{28,20},{1,9},{5... | collective-permute-start | bytes 786440 | tf_op jit(solution)/shard_map/ppermute | solution.py:21
  8.7 12.8 %collective-permute-start.5 = (bf16[1024,128]{1,0:T(8,128)(2,1)S(1)}, bf16[1024,128]{1,0:T(8,128)(2,1)S(1)}, u32[]{:S(2)}, u32[]{:S(2)}) collective-permute-start(bf16[1024,128]{1,0:T(8,128)(2,1)S(1)} %get-tuple-element.25.refs_3_), channel_id=1, source_target_pairs={{0,8},{4,12},{8,0},{12,4},{16,24},{20,28},{24,16},{28,20},{1,9},{5... | collective-permute-start | bytes 786440 | tf_op jit(solution)/shard_map/ppermute | solution.py:21
  8.8 14.8 %collective-permute-start.6 = (bf16[1024,128]{1,0:T(8,128)(2,1)S(1)}, bf16[1024,128]{1,0:T(8,128)(2,1)S(1)}, u32[]{:S(2)}, u32[]{:S(2)}) collective-permute-start(bf16[1024,128]{1,0:T(8,128)(2,1)S(1)} %get-tuple-element.24.refs_2_), channel_id=1, source_target_pairs={{0,16},{4,20},{8,24},{12,28},{16,0},{20,4},{24,8},{28,12},{1,17},{... | collective-permute-start | bytes 786440 | tf_op jit(solution)/shard_map/ppermute | solution.py:21
  12.8 14.3 %collective-permute-start.16 = (bf16[1024,128]{1,0:T(8,128)(2,1)S(1)}, bf16[1024,128]{1,0:T(8,128)(2,1)S(1)}, u32[]{:S(2)}, u32[]{:S(2)}) collective-permute-start(bf16[1024,128]{1,0:T(8,128)(2,1)S(1)} %get-tuple-element.28.refs_2_), channel_id=1, source_target_pairs={{0,8},{4,12},{8,0},{12,4},{16,24},{20,28},{24,16},{28,20},{1,9},{5... | collective-permute-start | bytes 786440 | tf_op jit(solution)/shard_map/ppermute | solution.py:21
  15.9 13.3 %collective-permute-start.18 = (bf16[1024,128]{1,0:T(8,128)(2,1)S(1)}, bf16[1024,128]{1,0:T(8,128)(2,1)S(1)}, u32[]{:S(2)}, u32[]{:S(2)}) collective-permute-start(bf16[1024,128]{1,0:T(8,128)(2,1)S(1)} %get-tuple-element.28.refs_2_), channel_id=1, source_target_pairs={{0,16},{4,20},{8,24},{12,28},{16,0},{20,4},{24,8},{28,12},{1,17},{... | collective-permute-start | bytes 786440 | tf_op jit(solution)/shard_map/ppermute | solution.py:21
  21.5 11.2 %collective-permute-start.17 = (bf16[1024,128]{1,0:T(8,128)(2,1)S(1)}, bf16[1024,128]{1,0:T(8,128)(2,1)S(1)}, u32[]{:S(2)}, u32[]{:S(2)}) collective-permute-start(bf16[1024,128]{1,0:T(8,128)(2,1)S(1)} %get-tuple-element.29.refs_3_), channel_id=1, source_target_pairs={{0,8},{4,12},{8,0},{12,4},{16,24},{20,28},{24,16},{28,20},{1,9},{5... | collective-permute-start | bytes 786440 | tf_op jit(solution)/shard_map/ppermute | solution.py:21
  23.5 11.3 %collective-permute-start.19 = (bf16[1024,128]{1,0:T(8,128)(2,1)S(1)}, bf16[1024,128]{1,0:T(8,128)(2,1)S(1)}, u32[]{:S(2)}, u32[]{:S(2)}) collective-permute-start(bf16[1024,128]{1,0:T(8,128)(2,1)S(1)} %get-tuple-element.29.refs_3_), channel_id=1, source_target_pairs={{0,16},{4,20},{8,24},{12,28},{16,0},{20,4},{24,8},{28,12},{1,17},{... | collective-permute-start | bytes 786440 | tf_op jit(solution)/shard_map/ppermute | solution.py:21
  27.1 11.2 %collective-permute-start.9 = (bf16[1024,128]{1,0:T(8,128)(2,1)S(1)}, bf16[1024,128]{1,0:T(8,128)(2,1)S(1)}, u32[]{:S(2)}, u32[]{:S(2)}) collective-permute-start(bf16[1024,128]{1,0:T(8,128)(2,1)S(1)} %collective-permute-done.6.refs_6_), channel_id=1, source_target_pairs={{0,8},{4,12},{8,0},{12,4},{16,24},{20,28},{24,16},{28,20},{1,9},{5... | collective-permute-start | bytes 786440 | tf_op jit(solution)/shard_map/ppermute | solution.py:21
  29.2 14.6 %collective-permute-start.21 = (bf16[1024,128]{1,0:T(8,128)(2,1)S(1)}, bf16[1024,128]{1,0:T(8,128)(2,1)S(1)}, u32[]{:S(2)}, u32[]{:S(2)}) collective-permute-start(bf16[1024,128]{1,0:T(8,128)(2,1)S(1)} %collective-permute-done.18.refs_6_), channel_id=1, source_target_pairs={{0,8},{4,12},{8,0},{12,4},{16,24},{20,28},{24,16},{28,20},{1,9},{5... | collective-permute-start | bytes 786440 | tf_op jit(solution)/shard_map/ppermute | solution.py:21
  32.8 11.1 %collective-permute-start.22 = (bf16[1024,128]{1,0:T(8,128)(2,1)S(1)}, bf16[1024,128]{1,0:T(8,128)(2,1)S(1)}, u32[]{:S(2)}, u32[]{:S(2)}) collective-permute-start(bf16[1024,128]{1,0:T(8,128)(2,1)S(1)} %collective-permute-done.17.refs_5_), channel_id=1, source_target_pairs={{0,16},{4,20},{8,24},{12,28},{16,0},{20,4},{24,8},{28,12},{1,17},{... | collective-permute-start | bytes 786440 | tf_op jit(solution)/shard_map/ppermute | solution.py:21
  34.8 12.8 %collective-permute-start.10 = (bf16[1024,128]{1,0:T(8,128)(2,1)S(1)}, bf16[1024,128]{1,0:T(8,128)(2,1)S(1)}, u32[]{:S(2)}, u32[]{:S(2)}) collective-permute-start(bf16[1024,128]{1,0:T(8,128)(2,1)S(1)} %collective-permute-done.5.refs_5_), channel_id=1, source_target_pairs={{0,16},{4,20},{8,24},{12,28},{16,0},{20,4},{24,8},{28,12},{1,17},{... | collective-permute-start | bytes 786440 | tf_op jit(solution)/shard_map/ppermute | solution.py:21
  38.4 13.6 %collective-permute-start.7 = (bf16[1024,128]{1,0:T(8,128)(2,1)S(1)}, bf16[1024,128]{1,0:T(8,128)(2,1)S(1)}, u32[]{:S(2)}, u32[]{:S(2)}) collective-permute-start(bf16[1024,128]{1,0:T(8,128)(2,1)S(1)} %get-tuple-element.25.refs_3_), channel_id=1, source_target_pairs={{0,16},{4,20},{8,24},{12,28},{16,0},{20,4},{24,8},{28,12},{1,17},{... | collective-permute-start | bytes 786440 | tf_op jit(solution)/shard_map/ppermute | solution.py:21
  43.8 8.1 %collective-permute-start.23 = (bf16[1024,128]{1,0:T(8,128)(2,1)S(1)}, bf16[1024,128]{1,0:T(8,128)(2,1)S(1)}, u32[]{:S(2)}, u32[]{:S(2)}) collective-permute-start(bf16[1024,128]{1,0:T(8,128)(2,1)S(1)} %collective-permute-done.21.refs_2_), channel_id=1, source_target_pairs={{0,4},{4,0},{8,12},{12,8},{16,20},{20,16},{24,28},{28,24},{1,5},{5... | collective-permute-start | bytes 786440 | tf_op jit(solution)/shard_map/ppermute | solution.py:21
  43.8 9.8 %collective-permute-start.24 = (bf16[1024,128]{1,0:T(8,128)(2,1)S(1)}, bf16[1024,128]{1,0:T(8,128)(2,1)S(1)}, u32[]{:S(2)}, u32[]{:S(2)}) collective-permute-start(bf16[1024,128]{1,0:T(8,128)(2,1)S(1)} %collective-permute-done.22.refs_3_), channel_id=1, source_target_pairs={{0,4},{4,0},{8,12},{12,8},{16,20},{20,16},{24,28},{28,24},{1,5},{5... | collective-permute-start | bytes 786440 | tf_op jit(solution)/shard_map/ppermute | solution.py:21
  47.6 16.5 %collective-permute-start.11 = (bf16[1024,128]{1,0:T(8,128)(2,1)S(1)}, bf16[1024,128]{1,0:T(8,128)(2,1)S(1)}, u32[]{:S(2)}, u32[]{:S(2)}) collective-permute-start(bf16[1024,128]{1,0:T(8,128)(2,1)S(1)} %collective-permute-done.9.refs_2_), channel_id=1, source_target_pairs={{0,4},{4,0},{8,12},{12,8},{16,20},{20,16},{24,28},{28,24},{1,5},{5... | collective-permute-start | bytes 786440 | tf_op jit(solution)/shard_map/ppermute | solution.py:21
  47.6 16.8 %collective-permute-start.12 = (bf16[1024,128]{1,0:T(8,128)(2,1)S(1)}, bf16[1024,128]{1,0:T(8,128)(2,1)S(1)}, u32[]{:S(2)}, u32[]{:S(2)}) collective-permute-start(bf16[1024,128]{1,0:T(8,128)(2,1)S(1)} %collective-permute-done.10.refs_3_), channel_id=1, source_target_pairs={{0,4},{4,0},{8,12},{12,8},{16,20},{20,16},{24,28},{28,24},{1,5},{5... | collective-permute-start | bytes 786440 | tf_op jit(solution)/shard_map/ppermute | solution.py:21
  51.9 6.9 %collective-permute-start.20 = (bf16[3,128,128]{2,1,0:T(8,128)(2,1)S(1)}, bf16[3,128,128]{2,1,0:T(8,128)(2,1)S(1)}, u32[]{:S(2)}, u32[]{:S(2)}) collective-permute-start(bf16[3,128,128]{2,1,0:T(8,128)(2,1)S(1)} %get-tuple-element.31), channel_id=1, source_target_pairs={{0,4},{4,0},{8,12},{12,8},{16,20},{20,16},{24,28},{28,24},{1,5},{5... | collective-permute-start | bytes 294920 | tf_op jit(solution)/shard_map/ppermute | solution.py:21
  52.0 6.3 %copy-start.2 = (bf16[1024,128]{1,0:T(8,128)(2,1)}, bf16[1024,128]{1,0:T(8,128)(2,1)S(1)}, u32[]{:S(2)}) copy-start(bf16[1024,128]{1,0:T(8,128)(2,1)S(1)} %collective-permute-done.23.refs_4_) | copy-start | bytes 786436
  52.0 16.7 %collective-permute-start = (bf16[2,512,128]{2,1,0:T(8,128)(2,1)}, bf16[2,512,128]{2,1,0:T(8,128)(2,1)S(1)}, u32[]{:S(2)}, u32[]{:S(2)}) collective-permute-start(bf16[2,512,128]{2,1,0:T(8,128)(2,1)} %get-tuple-element.20), channel_id=1, source_target_pairs={{0,1},{1,0},{2,3},{3,2},{4,5},{5,4},{6,7},{7,6},{8,9},{9,8},{10,11... | collective-permute-start | bytes 786440 | tf_op jit(solution)/shard_map/ppermute | solution.py:21
  53.6 0.7 copy-start.4
  54.3 35.7 %collective-permute-start.1 = (bf16[2,512,128]{2,1,0:T(8,128)(2,1)}, bf16[2,512,128]{2,1,0:T(8,128)(2,1)S(1)}, u32[]{:S(2)}, u32[]{:S(2)}) collective-permute-start(bf16[2,512,128]{2,1,0:T(8,128)(2,1)} %get-tuple-element.21), channel_id=1, source_target_pairs={{0,2},{1,3},{2,0},{3,1},{4,6},{5,7},{6,4},{7,5},{8,10},{9,11},{10,... | collective-permute-start | bytes 786440 | tf_op jit(solution)/shard_map/ppermute | solution.py:21
  58.2 0.6 copy-start.6
  58.9 0.6 copy-start.8
  59.5 6.6 %collective-permute-start.8 = (bf16[3,128,128]{2,1,0:T(8,128)(2,1)}, bf16[3,128,128]{2,1,0:T(8,128)(2,1)}, u32[]{:S(2)}, u32[]{:S(2)}) collective-permute-start(bf16[3,128,128]{2,1,0:T(8,128)(2,1)} %get-tuple-element.27), channel_id=1, source_target_pairs={{0,4},{4,0},{8,12},{12,8},{16,20},{20,16},{24,28},{28,24},{1,5},{5... | collective-permute-start | bytes 294920 | tf_op jit(solution)/shard_map/ppermute | solution.py:21
  59.5 0.7 copy-start.12
  60.4 1.0 copy-start.3
  61.3 0.9 copy-start.5
  62.3 0.9 copy-start.9
  63.2 0.9 copy-start.11
  63.2 2.9 %copy-start.7 = (bf16[3,128,128]{2,1,0:T(8,128)(2,1)S(1)}, bf16[3,128,128]{2,1,0:T(8,128)(2,1)}, u32[]{:S(2)}) copy-start(bf16[3,128,128]{2,1,0:T(8,128)(2,1)} %copy-done.6) | copy-start | bytes 294916
  64.1 27.9 %collective-permute-start.2 = (bf16[2,512,128]{2,1,0:T(8,128)(2,1)S(1)}, bf16[2,512,128]{2,1,0:T(8,128)(2,1)S(1)}, u32[]{:S(2)}, u32[]{:S(2)}) collective-permute-start(bf16[2,512,128]{2,1,0:T(8,128)(2,1)S(1)} %copy-done.11), channel_id=1, source_target_pairs={{0,3},{1,2},{2,1},{3,0},{4,7},{5,6},{6,5},{7,4},{8,11},{9,10},{10,... | collective-permute-start | bytes 786440 | tf_op jit(solution)/shard_map/ppermute | solution.py:21
  64.4 25.6 %collective-permute-start.26 = (bf16[128,512]{1,0:T(8,128)(2,1)S(1)}, bf16[128,512]{1,0:T(8,128)(2,1)S(1)}, u32[]{:S(2)}, u32[]{:S(2)}) collective-permute-start(bf16[128,512]{1,0:T(8,128)(2,1)S(1)} %shard_map.64.refs_4_), channel_id=1, source_target_pairs={{0,2},{1,3},{2,0},{3,1},{4,6},{5,7},{6,4},{7,5},{8,10},{9,11},{10,... | collective-permute-start | bytes 393224 | tf_op jit(solution)/shard_map/ppermute | solution.py:21
  67.3 24.8 %collective-permute-start.14 = (bf16[128,512]{1,0:T(8,128)(2,1)S(1)}, bf16[128,512]{1,0:T(8,128)(2,1)S(1)}, u32[]{:S(2)}, u32[]{:S(2)}) collective-permute-start(bf16[128,512]{1,0:T(8,128)(2,1)S(1)} %shard_map.61.refs_4_), channel_id=1, source_target_pairs={{0,2},{1,3},{2,0},{3,1},{4,6},{5,7},{6,4},{7,5},{8,10},{9,11},{10,... | collective-permute-start | bytes 393224 | tf_op jit(solution)/shard_map/ppermute | solution.py:21
  68.6 23.4 %collective-permute-start.25 = (bf16[128,512]{1,0:T(8,128)(2,1)S(1)}, bf16[128,512]{1,0:T(8,128)(2,1)S(1)}, u32[]{:S(2)}, u32[]{:S(2)}) collective-permute-start(bf16[128,512]{1,0:T(8,128)(2,1)S(1)} %shard_map.64.refs_4_), channel_id=1, source_target_pairs={{0,1},{1,0},{2,3},{3,2},{4,5},{5,4},{6,7},{7,6},{8,9},{9,8},{10,11... | collective-permute-start | bytes 393224 | tf_op jit(solution)/shard_map/ppermute | solution.py:21
  90.0 6.4 %collective-permute-start.27 = (bf16[128,512]{1,0:T(8,128)(2,1)S(1)}, bf16[128,512]{1,0:T(8,128)(2,1)S(1)}, u32[]{:S(2)}, u32[]{:S(2)}) collective-permute-start(bf16[128,512]{1,0:T(8,128)(2,1)S(1)} %collective-permute-done.26.refs_6_), channel_id=1, source_target_pairs={{0,1},{1,0},{2,3},{3,2},{4,5},{5,4},{6,7},{7,6},{8,9},{9,8},{10,11... | collective-permute-start | bytes 393224 | tf_op jit(solution)/shard_map/ppermute | solution.py:21
  90.0 9.0 %collective-permute-start.13 = (bf16[128,512]{1,0:T(8,128)(2,1)S(1)}, bf16[128,512]{1,0:T(8,128)(2,1)S(1)}, u32[]{:S(2)}, u32[]{:S(2)}) collective-permute-start(bf16[128,512]{1,0:T(8,128)(2,1)S(1)} %shard_map.61.refs_4_), channel_id=1, source_target_pairs={{0,1},{1,0},{2,3},{3,2},{4,5},{5,4},{6,7},{7,6},{8,9},{9,8},{10,11... | collective-permute-start | bytes 393224 | tf_op jit(solution)/shard_map/ppermute | solution.py:21
  92.1 8.3 %collective-permute-start.15 = (bf16[128,512]{1,0:T(8,128)(2,1)S(1)}, bf16[128,512]{1,0:T(8,128)(2,1)S(1)}, u32[]{:S(2)}, u32[]{:S(2)}) collective-permute-start(bf16[128,512]{1,0:T(8,128)(2,1)S(1)} %collective-permute-done.14.refs_6_), channel_id=1, source_target_pairs={{0,1},{1,0},{2,3},{3,2},{4,5},{5,4},{6,7},{7,6},{8,9},{9,8},{10,11... | collective-permute-start | bytes 393224 | tf_op jit(solution)/shard_map/ppermute | solution.py:21
  101.9 5.2 %collective-permute-start.28 = (f32[4,72,128]{2,1,0:T(8,128)S(1)}, f32[4,72,128]{2,1,0:T(8,128)S(1)}, u32[]{:S(2)}, u32[]{:S(2)}) collective-permute-start(f32[4,72,128]{2,1,0:T(8,128)S(1)} %get-tuple-element.32), channel_id=1, source_target_pairs={{0,1},{1,0},{2,3},{3,2},{4,5},{5,4},{6,7},{7,6},{8,9},{9,8},{10,11... | collective-permute-start | bytes 442376 | tf_op jit(solution)/shard_map/ppermute | solution.py:21
  107.1 7.2 %collective-permute-start.29 = (f32[4,72,128]{2,1,0:T(8,128)S(1)}, f32[4,72,128]{2,1,0:T(8,128)S(1)}, u32[]{:S(2)}, u32[]{:S(2)}) collective-permute-start(f32[4,72,128]{2,1,0:T(8,128)S(1)} %add.8.own_ref), channel_id=1, source_target_pairs={{0,2},{1,3},{2,0},{3,1},{4,6},{5,7},{6,4},{7,5},{8,10},{9,11},{10,... | collective-permute-start | bytes 442376 | tf_op jit(solution)/shard_map/ppermute | solution.py:21

commit v3 on v2

--- a/solution.py
+++ b/solution.py
@@ -193,26 +193,61 @@
     return strict + strict.T + center
 
 
-def eliminate(panel, first, lane, sub):
-    cols = [
-        jnp.broadcast_to(panel[:, first + j:first + j + 1], panel.shape) for j in range(BLOCK)
-    ]
-    pivots = jnp.zeros_like(panel)
-    recips = jnp.zeros_like(panel)
-    for j in range(BLOCK):
-        k = first + j
-        pivot = jnp.broadcast_to(cols[j][j:j + 1, :], panel.shape)
+def at_row(x, r):
+    return jnp.broadcast_to(x[r:r + 1, :], x.shape)
+
+
+def eliminate(panels, first, lane, sub):
+    number = len(panels)
+    count, size = panels[0].shape[0] // 8, panels[0].shape[1] // number
+    blocks = [[panel[8 * i:8 * i + 8] for i in range(count)] for panel in panels]
+    cols = []
+    for k in range(first, first + 8 * count):
+        col = []
+        for i in range(count):
+            packed = None
+            for t in range(number):
+                x = jnp.broadcast_to(blocks[t][i][:, k:k + 1], lane.shape)
+                packed = x if packed is None else jnp.where(lane >= t * size, x, packed)
+            col.append(packed)
+        cols.append(col)
+    pivots = [jnp.zeros_like(blocks[0][0])] * count
+    recips = [jnp.zeros_like(blocks[0][0])] * count
+    factors = []
+    for j, col in enumerate(cols):
+        s, r = divmod(j, 8)
+        pivot = at_row(col[s], r)
         recip = 1.0 / pivot
-        factor = jnp.where(sub > j, cols[j] * recip, 0.0)
-        for c in range(j + 1, BLOCK):
-            cols[c] = cols[c] - factor * jnp.broadcast_to(cols[c][j:j + 1, :], panel.shape)
-        here = sub == j
-        pivots = jnp.where(here, pivot, pivots)
-        recips = jnp.where(here, recip, recips)
-        row = jnp.where(lane == k, 1.0, jnp.broadcast_to(panel[j:j + 1, :], panel.shape))
-        panel = jnp.where((lane == k) & (sub >= j), jnp.where(here, 1.0, 0.0), panel)
-        panel = panel - factor * row
-    return panel, pivots, recips
+        factor = {i: col[i] * recip for i in range(s, count)}
+        factor[s] = jnp.where(sub > r, factor[s], 0.0)
+        for other in cols[j + 1:]:
+            top = at_row(other[s], r)
+            for i in range(s, count):
+                other[i] = other[i] - factor[i] * top
+        pivots[s] = jnp.where(sub == r, pivot, pivots[s])
+        recips[s] = jnp.where(sub == r, recip, recips[s])
+        factors.append(factor)
+    done = []
+    for t in range(number):
+        def own(x):
+            return jnp.broadcast_to(x[:, t * size:t * size + 1], x.shape)
+
+        rows = blocks[t]
+        for j, factor in enumerate(factors):
+            s, r = divmod(j, 8)
+            here = lane == first + j
+            row = jnp.where(here, 1.0, at_row(rows[s], r))
+            for i in range(s, count):
+                if i > s:
+                    old = jnp.where(here, 0.0, rows[i])
+                else:
+                    old = jnp.where(here & (sub >= r), jnp.where(sub == r, 1.0, 0.0), rows[i])
+                rows[i] = old - own(factor[i]) * row
+        done.append([
+            jnp.concatenate(parts, axis=0)
+            for parts in (rows, [own(x) for x in pivots], [own(x) for x in recips])
+        ])
+    return done
 
 
 def split(x):
@@ -239,7 +274,9 @@
     sub = lax.broadcasted_iota(jnp.int32, (BLOCK, width), 0)
     for first in range(0, width, BLOCK):
         last = first + BLOCK
-        done = [eliminate(work_ref[t, first:last, :], first, lane, sub) for t in range(listed)]
+        done = eliminate(
+            [work_ref[t, first:last, :] for t in range(listed)], first, lane[:8], sub[:8]
+        )
         for t in range(listed):
             panel, pivots, recips = done[t]
             root = lax.rsqrt(pivots)
@@ -303,12 +340,13 @@
             pltpu.SemaphoreType.DMA((3,)),
         ],
     )
+    *halves, later_left, later_right = lax.optimization_barrier((*halves, left_factors, right_factors))
     second = call(
         functools.partial(second_kernel, depth_size),
         (shape((half, width), bf16),) * (2 * panels - 2)
         + (shape((panels, rank_size, tile_size), bf16),)
         + (shape((panels, part, rank_size), bf16),) * depth_size,
-        level[None], left_factors, right_factors, probe_matrix,
+        level[None], later_left, later_right, probe_matrix,
         in_specs=[SMEM, VMEM, VMEM, HBM],
         scratch_shapes=[pltpu.VMEM((tile_size, width), bf16), pltpu.SemaphoreType.DMA((1,))],
     )

time: 123 us -> 121 us (0.984)
  local copies, waits for them, and re-layouts: 8.68 us -> 6.25 us
  waiting for transfers between devices: 63.4 us -> 65.5 us
    unnamed x26, local copies, waits for them, and re-layouts: 8.68 us -> 6.25 us
    ppermute x30, waiting for transfers between devices: 63.4 us -> 65.5 us  [swap(): return lax.ppermute(x, axis, [(i, i ^ bits) for i in range(size)])]
  transfers between devices with their start and end apart: 30 -> 30, of which waited for: 15 -> 15; matrix products, arithmetic and copies ran while one was open for 0% -> 0% of each run, Pallas kernels for 5% -> 4%
where the time goes in v3:
time: 121 us
  waiting for transfers between devices  65.5 us (54%)
  starting transfers between devices  31.2 us (26%)
  Pallas kernels  17.1 us (14%)
  local copies, waits for them, and re-layouts  6.25 us (5%)
    ppermute x30, waiting for transfers between devices, swap(): return lax.ppermute(x, axis, [(i, i ^ bits) for i in range(size)])  65.5 us
    ppermute x30, starting transfers between devices, swap(): return lax.ppermute(x, axis, [(i, i ^ bits) for i in range(size)])  31.2 us
    pallas_call x9, Pallas kernels, call(): pl.pallas_call(kernel, out_shape=shapes, in_specs=specs, out_specs=out, c...  17.1 us
    unnamed x26, local copies, waits for them, and re-layouts  6.25 us
  transfers between devices with their start and end apart: 30, of which 15 were waited for; matrix products, arithmetic and copies ran while one was open for 0% of the time, Pallas kernels for 4%

profile of v3, /device:TPU:0, one launch (start us, length us, event | category | flops | bytes accessed | tf_op | source)
XLA Modules:
  0.0 121.0 jit_solution(14513701362533973978)
XLA Ops:
  0.7 2.1 %shard_map.59 = (bf16[1024,128]{1,0:T(8,128)(2,1)S(1)}, bf16[1024,128]{1,0:T(8,128)(2,1)S(1)}) custom-call(bf16[1,2,2048,128]{3,2,1,0:T(8,128)(2,1)} %left_ref.2, bf16[1,2,2048,128]{3,2,1,0:T(8,128)(2,1)} %right_ref.2, bf16[2048,128]{1,0:T(8,128)(2,1)} %probe_ref.3), custom_call_target="tpu_custom_call" | custom-call | tf_op jit(solution)/shard_map/pallas_call | solution.py:315
  2.8 2.0 %shard_map.60 = (bf16[1024,128]{1,0:T(8,128)(2,1)S(1)}, bf16[1024,128]{1,0:T(8,128)(2,1)S(1)}, bf16[2,128,2048]{2,1,0:T(8,128)(2,1)S(1)}, bf16[2,512,128]{2,1,0:...) custom-call(s32[1]{0:T(128)} %bitcast.level_ref, ...), custom_call_target="tpu_custom_call" | custom-call | tf_op jit(solution)/shard_map/pallas_call | solution.py:315
  4.8 0.7 copy-done.10
  5.5 0.5 collective-permute-start.3
  6.0 2.5 %collective-permute-start.4 = (bf16[1024,128]{1,0:T(8,128)(2,1)S(1)}, bf16[1024,128]{1,0:T(8,128)(2,1)S(1)}, u32[]{:S(2)}, u32[]{:S(2)}) collective-permute-start(bf16[1024,128]{1,0:T(8,128)(2,1)S(1)} %get-tuple-element.32.refs_2_), channel_id=1, source_target_pairs={{0,8},{4,12},{8,0},{12,4},{16,24},{20,28},{24,16},{28,20},{1,9},{5... | collective-permute-start | bytes 786440 | tf_op jit(solution)/shard_map/ppermute | solution.py:21
  8.5 0.0 collective-permute-start.5
  8.5 2.0 %collective-permute-start.6 = (bf16[1024,128]{1,0:T(8,128)(2,1)S(1)}, bf16[1024,128]{1,0:T(8,128)(2,1)S(1)}, u32[]{:S(2)}, u32[]{:S(2)}) collective-permute-start(bf16[1024,128]{1,0:T(8,128)(2,1)S(1)} %get-tuple-element.32.refs_2_), channel_id=1, source_target_pairs={{0,16},{4,20},{8,24},{12,28},{16,0},{20,4},{24,8},{28,12},{1,17},{... | collective-permute-start | bytes 786440 | tf_op jit(solution)/shard_map/ppermute | solution.py:21
  10.5 1.5 %collective-permute-start.16 = (bf16[1024,128]{1,0:T(8,128)(2,1)S(1)}, bf16[1024,128]{1,0:T(8,128)(2,1)S(1)}, u32[]{:S(2)}, u32[]{:S(2)}) collective-permute-start(bf16[1024,128]{1,0:T(8,128)(2,1)S(1)} %get-tuple-element.36.refs_2_), channel_id=1, source_target_pairs={{0,8},{4,12},{8,0},{12,4},{16,24},{20,28},{24,16},{28,20},{1,9},{5... | collective-permute-start | bytes 786440 | tf_op jit(solution)/shard_map/ppermute | solution.py:21
  12.0 3.6 %collective-permute-done.4.refs_4_ = bf16[1024,128]{1,0:T(8,128)(2,1)S(1)} collective-permute-done((bf16[1024,128]{1,0:T(8,128)(2,1)S(1)}, bf16[1024,128]{1,0:T(8,128)(2,1)S(1)}, u32[]{:S(2)}, u32[]{:S(2)}) %collective-permute-start.4) | collective-permute-done | bytes 262176 | tf_op jit(solution)/shard_map/ppermute | solution.py:21
  15.6 2.0 %collective-permute-start.18 = (bf16[1024,128]{1,0:T(8,128)(2,1)S(1)}, bf16[1024,128]{1,0:T(8,128)(2,1)S(1)}, u32[]{:S(2)}, u32[]{:S(2)}) collective-permute-start(bf16[1024,128]{1,0:T(8,128)(2,1)S(1)} %get-tuple-element.36.refs_2_), channel_id=1, source_target_pairs={{0,16},{4,20},{8,24},{12,28},{16,0},{20,4},{24,8},{28,12},{1,17},{... | collective-permute-start | bytes 786440 | tf_op jit(solution)/shard_map/ppermute | solution.py:21
  17.7 3.6 %collective-permute-done.5.refs_5_ = bf16[1024,128]{1,0:T(8,128)(2,1)S(1)} collective-permute-done((bf16[1024,128]{1,0:T(8,128)(2,1)S(1)}, bf16[1024,128]{1,0:T(8,128)(2,1)S(1)}, u32[]{:S(2)}, u32[]{:S(2)}) %collective-permute-start.5) | collective-permute-done | bytes 262176 | tf_op jit(solution)/shard_map/ppermute | solution.py:21
  21.3 2.0 %collective-permute-start.17 = (bf16[1024,128]{1,0:T(8,128)(2,1)S(1)}, bf16[1024,128]{1,0:T(8,128)(2,1)S(1)}, u32[]{:S(2)}, u32[]{:S(2)}) collective-permute-start(bf16[1024,128]{1,0:T(8,128)(2,1)S(1)} %get-tuple-element.37.refs_3_), channel_id=1, source_target_pairs={{0,8},{4,12},{8,0},{12,4},{16,24},{20,28},{24,16},{28,20},{1,9},{5... | collective-permute-start | bytes 786440 | tf_op jit(solution)/shard_map/ppermute | solution.py:21
  23.3 1.5 %collective-permute-start.19 = (bf16[1024,128]{1,0:T(8,128)(2,1)S(1)}, bf16[1024,128]{1,0:T(8,128)(2,1)S(1)}, u32[]{:S(2)}, u32[]{:S(2)}) collective-permute-start(bf16[1024,128]{1,0:T(8,128)(2,1)S(1)} %get-tuple-element.37.refs_3_), channel_id=1, source_target_pairs={{0,16},{4,20},{8,24},{12,28},{16,0},{20,4},{24,8},{28,12},{1,17},{... | collective-permute-start | bytes 786440 | tf_op jit(solution)/shard_map/ppermute | solution.py:21
  24.8 2.1 %collective-permute-done.16.refs_4_ = bf16[1024,128]{1,0:T(8,128)(2,1)S(1)} collective-permute-done((bf16[1024,128]{1,0:T(8,128)(2,1)S(1)}, bf16[1024,128]{1,0:T(8,128)(2,1)S(1)}, u32[]{:S(2)}, u32[]{:S(2)}) %collective-permute-start.16) | collective-permute-done | bytes 262176 | tf_op jit(solution)/shard_map/ppermute | solution.py:21
  26.9 2.0 %collective-permute-start.9 = (bf16[1024,128]{1,0:T(8,128)(2,1)S(1)}, bf16[1024,128]{1,0:T(8,128)(2,1)S(1)}, u32[]{:S(2)}, u32[]{:S(2)}) collective-permute-start(bf16[1024,128]{1,0:T(8,128)(2,1)S(1)} %collective-permute-done.6.refs_6_), channel_id=1, source_target_pairs={{0,8},{4,12},{8,0},{12,4},{16,24},{20,28},{24,16},{28,20},{1,9},{5... | collective-permute-start | bytes 786440 | tf_op jit(solution)/shard_map/ppermute | solution.py:21
  28.9 0.0 collective-permute-done.18.refs_6_
  28.9 0.0 collective-permute-start.21
  28.9 3.6 %collective-permute-done.17.refs_5_ = bf16[1024,128]{1,0:T(8,128)(2,1)S(1)} collective-permute-done((bf16[1024,128]{1,0:T(8,128)(2,1)S(1)}, bf16[1024,128]{1,0:T(8,128)(2,1)S(1)}, u32[]{:S(2)}, u32[]{:S(2)}) %collective-permute-start.17) | collective-permute-done | bytes 262176 | tf_op jit(solution)/shard_map/ppermute | solution.py:21
  32.5 2.0 %collective-permute-start.22 = (bf16[1024,128]{1,0:T(8,128)(2,1)S(1)}, bf16[1024,128]{1,0:T(8,128)(2,1)S(1)}, u32[]{:S(2)}, u32[]{:S(2)}) collective-permute-start(bf16[1024,128]{1,0:T(8,128)(2,1)S(1)} %collective-permute-done.17.refs_5_), channel_id=1, source_target_pairs={{0,16},{4,20},{8,24},{12,28},{16,0},{20,4},{24,8},{28,12},{1,17},{... | collective-permute-start | bytes 786440 | tf_op jit(solution)/shard_map/ppermute | solution.py:21
  34.5 0.0 collective-permute-done.19.refs_7_
  34.5 0.0 collective-permute-start.10
  34.6 3.5 %collective-permute-done.9.refs_2_ = bf16[1024,128]{1,0:T(8,128)(2,1)S(1)} collective-permute-done((bf16[1024,128]{1,0:T(8,128)(2,1)S(1)}, bf16[1024,128]{1,0:T(8,128)(2,1)S(1)}, u32[]{:S(2)}, u32[]{:S(2)}) %collective-permute-start.9) | collective-permute-done | bytes 262176 | tf_op jit(solution)/shard_map/ppermute | solution.py:21
  38.1 2.0 %collective-permute-start.7 = (bf16[1024,128]{1,0:T(8,128)(2,1)S(1)}, bf16[1024,128]{1,0:T(8,128)(2,1)S(1)}, u32[]{:S(2)}, u32[]{:S(2)}) collective-permute-start(bf16[1024,128]{1,0:T(8,128)(2,1)S(1)} %get-tuple-element.33.refs_3_), channel_id=1, source_target_pairs={{0,16},{4,20},{8,24},{12,28},{16,0},{20,4},{24,8},{28,12},{1,17},{... | collective-permute-start | bytes 786440 | tf_op jit(solution)/shard_map/ppermute | solution.py:21
  40.2 3.4 %collective-permute-done.21.refs_2_ = bf16[1024,128]{1,0:T(8,128)(2,1)S(1)} collective-permute-done((bf16[1024,128]{1,0:T(8,128)(2,1)S(1)}, bf16[1024,128]{1,0:T(8,128)(2,1)S(1)}, u32[]{:S(2)}, u32[]{:S(2)}) %collective-permute-start.21) | collective-permute-done | bytes 262176 | tf_op jit(solution)/shard_map/ppermute | solution.py:21
  43.6 0.0 collective-permute-start.23
  43.6 0.0 collective-permute-done.22.refs_3_
  43.6 0.5 collective-permute-start.24
  44.1 3.2 %collective-permute-done.10.refs_3_ = bf16[1024,128]{1,0:T(8,128)(2,1)S(1)} collective-permute-done((bf16[1024,128]{1,0:T(8,128)(2,1)S(1)}, bf16[1024,128]{1,0:T(8,128)(2,1)S(1)}, u32[]{:S(2)}, u32[]{:S(2)}) %collective-permute-start.10) | collective-permute-done | bytes 262176 | tf_op jit(solution)/shard_map/ppermute | solution.py:21
  47.3 0.5 collective-permute-start.12
  47.8 0.7 shard_map.63
  48.5 3.2 %collective-permute-done.7.refs_7_ = bf16[1024,128]{1,0:T(8,128)(2,1)S(1)} collective-permute-done((bf16[1024,128]{1,0:T(8,128)(2,1)S(1)}, bf16[1024,128]{1,0:T(8,128)(2,1)S(1)}, u32[]{:S(2)}, u32[]{:S(2)}) %collective-permute-start.7) | collective-permute-done | bytes 262176 | tf_op jit(solution)/shard_map/ppermute | solution.py:21
  51.7 1.6 %collective-permute-start = (bf16[2,512,128]{2,1,0:T(8,128)(2,1)}, bf16[2,512,128]{2,1,0:T(8,128)(2,1)S(1)}, u32[]{:S(2)}, u32[]{:S(2)}) collective-permute-start(bf16[2,512,128]{2,1,0:T(8,128)(2,1)} %get-tuple-element.28), channel_id=1, source_target_pairs={{0,1},{1,0},{2,3},{3,2},{4,5},{5,4},{6,7},{7,6},{8,9},{9,8},{10,11... | collective-permute-start | bytes 786440 | tf_op jit(solution)/shard_map/ppermute | solution.py:21
  53.3 0.0 collective-permute-done.24.refs_5_
  53.3 0.7 copy-done.4
  54.0 2.6 %collective-permute-start.1 = (bf16[2,512,128]{2,1,0:T(8,128)(2,1)}, bf16[2,512,128]{2,1,0:T(8,128)(2,1)S(1)}, u32[]{:S(2)}, u32[]{:S(2)}) collective-permute-start(bf16[2,512,128]{2,1,0:T(8,128)(2,1)} %get-tuple-element.29), channel_id=1, source_target_pairs={{0,2},{1,3},{2,0},{3,1},{4,6},{5,7},{6,4},{7,5},{8,10},{9,11},{10,... | collective-permute-start | bytes 786440 | tf_op jit(solution)/shard_map/ppermute | solution.py:21
  56.6 1.3 %shard_map.61 = (bf16[3,128,128]{2,1,0:T(8,128)(2,1)S(1)}, bf16[3,128,128]{2,1,0:T(8,128)(2,1)}) custom-call(bf16[2,128,2048]{2,1,0:T(8,128)(2,1)S(1)} %get-tuple-element.31.refs_0_.turned_ref, bf16[2,128,2048]{2,1,0:T(8,128)(2,1)S(1)} %collective-permute-done.3.refs_1_, bf16[1024,128]{1,0:T(8,128)(2,1)S(1)} %get-tuple-element.32.refs_2_, ...), custom_call_target="tpu_custom_call" | custom-call | tf_op jit(solution)/shard_map/pallas_call | solution.py:315
  58.0 0.6 copy-done.6
  58.6 0.0 collective-permute-done.20.refs_1_
  58.6 0.6 copy-done.8
  59.2 0.7 copy-done.12
  59.9 0.2 xor_reduce_fusion.wanted_ref
  60.1 0.9 copy-done.3
  61.1 0.9 copy-done.5
  62.0 0.9 copy-done.9
  62.9 0.9 shard_map.64.refs_4_
  63.8 0.1 copy-done.11
  63.9 0.3 collective-permute-start.2
  64.1 1.7 %collective-permute-start.26 = (bf16[128,512]{1,0:T(8,128)(2,1)S(1)}, bf16[128,512]{1,0:T(8,128)(2,1)S(1)}, u32[]{:S(2)}, u32[]{:S(2)}) collective-permute-start(bf16[128,512]{1,0:T(8,128)(2,1)S(1)} %shard_map.64.refs_4_), channel_id=1, source_target_pairs={{0,2},{1,3},{2,0},{3,1},{4,6},{5,7},{6,4},{7,5},{8,10},{9,11},{10,... | collective-permute-start | bytes 393224 | tf_op jit(solution)/shard_map/ppermute | solution.py:21
  65.8 1.2 %shard_map.62.refs_4_ = bf16[128,512]{1,0:T(8,128)(2,1)S(1)} custom-call(s32[4]{0:T(128)S(1)} %xor_reduce_fusion.wanted_ref, bf16[2,128,2048]{2,1,0:T(8,128)(2,1)S(1)} %get-tuple-element.31.refs_0_.turned_ref, bf16[3,128,128]{2,1,0:T(8,128)(2,1)S(1)} %copy-done.7, bf16[3,128,128]{2,1,0:T(8,128)(2,1)} %collective-permute-done.8.refs_1_, ...), custom_call_target="tpu_custom_call" | custom-call | tf_op jit(solution)/shard_map/pallas_call | solution.py:315
  67.0 1.3 %collective-permute-start.14 = (bf16[128,512]{1,0:T(8,128)(2,1)S(1)}, bf16[128,512]{1,0:T(8,128)(2,1)S(1)}, u32[]{:S(2)}, u32[]{:S(2)}) collective-permute-start(bf16[128,512]{1,0:T(8,128)(2,1)S(1)} %shard_map.62.refs_4_), channel_id=1, source_target_pairs={{0,2},{1,3},{2,0},{3,1},{4,6},{5,7},{6,4},{7,5},{8,10},{9,11},{10,... | collective-permute-start | bytes 393224 | tf_op jit(solution)/shard_map/ppermute | solution.py:21
  68.4 1.3 %collective-permute-start.25 = (bf16[128,512]{1,0:T(8,128)(2,1)S(1)}, bf16[128,512]{1,0:T(8,128)(2,1)S(1)}, u32[]{:S(2)}, u32[]{:S(2)}) collective-permute-start(bf16[128,512]{1,0:T(8,128)(2,1)S(1)} %shard_map.64.refs_4_), channel_id=1, source_target_pairs={{0,1},{1,0},{2,3},{3,2},{4,5},{5,4},{6,7},{7,6},{8,9},{9,8},{10,11... | collective-permute-start | bytes 393224 | tf_op jit(solution)/shard_map/ppermute | solution.py:21
  69.7 20.0 %collective-permute-done.26.refs_6_ = bf16[128,512]{1,0:T(8,128)(2,1)S(1)} collective-permute-done((bf16[128,512]{1,0:T(8,128)(2,1)S(1)}, bf16[128,512]{1,0:T(8,128)(2,1)S(1)}, u32[]{:S(2)}, u32[]{:S(2)}) %collective-permute-start.26) | collective-permute-done | bytes 131104 | tf_op jit(solution)/shard_map/ppermute | solution.py:21
  89.7 2.0 %collective-permute-start.13 = (bf16[128,512]{1,0:T(8,128)(2,1)S(1)}, bf16[128,512]{1,0:T(8,128)(2,1)S(1)}, u32[]{:S(2)}, u32[]{:S(2)}) collective-permute-start(bf16[128,512]{1,0:T(8,128)(2,1)S(1)} %shard_map.62.refs_4_), channel_id=1, source_target_pairs={{0,1},{1,0},{2,3},{3,2},{4,5},{5,4},{6,7},{7,6},{8,9},{9,8},{10,11... | collective-permute-start | bytes 393224 | tf_op jit(solution)/shard_map/ppermute | solution.py:21
  91.7 0.1 collective-permute-done.14.refs_6_
  91.8 4.3 %collective-permute-done.27.refs_7_ = bf16[128,512]{1,0:T(8,128)(2,1)S(1)} collective-permute-done((bf16[128,512]{1,0:T(8,128)(2,1)S(1)}, bf16[128,512]{1,0:T(8,128)(2,1)S(1)}, u32[]{:S(2)}, u32[]{:S(2)}) %collective-permute-start.27) | collective-permute-done | bytes 131104 | tf_op jit(solution)/shard_map/ppermute | solution.py:21
  96.1 0.4 shard_map.65.refs_8_
  96.5 2.2 %collective-permute-done.13.refs_5_ = bf16[128,512]{1,0:T(8,128)(2,1)S(1)} collective-permute-done((bf16[128,512]{1,0:T(8,128)(2,1)S(1)}, bf16[128,512]{1,0:T(8,128)(2,1)S(1)}, u32[]{:S(2)}, u32[]{:S(2)}) %collective-permute-start.13) | collective-permute-done | bytes 131104 | tf_op jit(solution)/shard_map/ppermute | solution.py:21
  98.7 1.4 %collective-permute-done.15.refs_7_ = bf16[128,512]{1,0:T(8,128)(2,1)S(1)} collective-permute-done((bf16[128,512]{1,0:T(8,128)(2,1)S(1)}, bf16[128,512]{1,0:T(8,128)(2,1)S(1)}, u32[]{:S(2)}, u32[]{:S(2)}) %collective-permute-start.15) | collective-permute-done | bytes 131104 | tf_op jit(solution)/shard_map/ppermute | solution.py:21
  100.1 1.5 %shard_map.66 = (f32[4,512,128]{2,1,0:T(8,128)S(1)}, f32[4,72,128]{2,1,0:T(8,128)S(1)}) custom-call(bf16[2,512,128]{2,1,0:T(8,128)(2,1)S(1)} %get-tuple-element.27.refs_0_, bf16[2,512,128]{2,1,0:T(8,128)(2,1)S(1)} %collective-permute-done.refs_1_, bf16[2,512,128]{2,1,0:T(8,128)(2,1)S(1)} %collective-permute-done.1.refs_2_, ...), custom_call_target="tpu_custom_call" | custom-call | tf_op jit(solution)/shard_map/pallas_call | solution.py:315
  101.7 0.1 collective-permute-start.28
  101.7 5.1 %collective-permute-done.28 = f32[4,72,128]{2,1,0:T(8,128)S(1)} collective-permute-done((f32[4,72,128]{2,1,0:T(8,128)S(1)}, f32[4,72,128]{2,1,0:T(8,128)S(1)}, u32[]{:S(2)}, u32[]{:S(2)}) %collective-permute-start.28) | collective-permute-done | bytes 147488 | tf_op jit(solution)/shard_map/ppermute | solution.py:21
  106.9 1.0 collective-permute-start.29
  107.9 6.2 %collective-permute-done.29.other_ref = f32[4,72,128]{2,1,0:T(8,128)S(1)} collective-permute-done((f32[4,72,128]{2,1,0:T(8,128)S(1)}, f32[4,72,128]{2,1,0:T(8,128)S(1)}, u32[]{:S(2)}, u32[]{:S(2)}) %collective-permute-start.29) | collective-permute-done | bytes 147488 | tf_op jit(solution)/shard_map/ppermute | solution.py:21
  114.1 6.9 %shard_map.67 = (f32[4,512,128]{2,1,0:T(8,128)}, f32[4,128,128]{2,1,0:T(8,128)}) custom-call(f32[4,72,128]{2,1,0:T(8,128)S(1)} %add.8.own_ref, f32[4,72,128]{2,1,0:T(8,128)S(1)} %collective-permute-done.29.other_ref, f32[4,512,128]{2,1,0:T(8,128)S(1)} %get-tuple-element.41.sketch_ref), custom_call_target="tpu_custom_call" | custom-call | tf_op jit(solution)/shard_map/pallas_call | solution.py:315
  (33 shorter events, 0.1 us)
Async XLA Ops:
  0.6 2.2 %copy-start = (bf16[1,2,2048,128]{3,2,1,0:T(8,128)(2,1)S(1)}, bf16[1,2,2048,128]{3,2,1,0:T(8,128)(2,1)}, u32[]{:S(2)}) copy-start(bf16[1,2,2048,128]{3,2,1,0:T(8,128)(2,1)} %left_ref.2) | copy-start | bytes 3145732
  0.6 2.2 %copy-start.1 = (bf16[1,2,2048,128]{3,2,1,0:T(8,128)(2,1)S(1)}, bf16[1,2,2048,128]{3,2,1,0:T(8,128)(2,1)}, u32[]{:S(2)}) copy-start(bf16[1,2,2048,128]{3,2,1,0:T(8,128)(2,1)} %right_ref.2) | copy-start | bytes 3145732
  4.8 0.7 copy-start.10
  5.5 41.8 %collective-permute-start.3 = (bf16[2,128,2048]{2,1,0:T(8,128)(2,1)S(1)}, bf16[2,128,2048]{2,1,0:T(8,128)(2,1)S(1)}, u32[]{:S(2)}, u32[]{:S(2)}) collective-permute-start(bf16[2,128,2048]{2,1,0:T(8,128)(2,1)S(1)} %get-tuple-element.31.refs_0_.turned_ref), channel_id=1, source_target_pairs={{0,4},{4,0},{8,12},{12,8},{16,20},{20,16},{24,28},{28,24},{1,5},{5... | collective-permute-start | bytes 3145736 | tf_op jit(solution)/shard_map/ppermute | solution.py:21
  6.0 9.6 %collective-permute-start.4 = (bf16[1024,128]{1,0:T(8,128)(2,1)S(1)}, bf16[1024,128]{1,0:T(8,128)(2,1)S(1)}, u32[]{:S(2)}, u32[]{:S(2)}) collective-permute-start(bf16[1024,128]{1,0:T(8,128)(2,1)S(1)} %get-tuple-element.32.refs_2_), channel_id=1, source_target_pairs={{0,8},{4,12},{8,0},{12,4},{16,24},{20,28},{24,16},{28,20},{1,9},{5... | collective-permute-start | bytes 786440 | tf_op jit(solution)/shard_map/ppermute | solution.py:21
  8.5 12.8 %collective-permute-start.5 = (bf16[1024,128]{1,0:T(8,128)(2,1)S(1)}, bf16[1024,128]{1,0:T(8,128)(2,1)S(1)}, u32[]{:S(2)}, u32[]{:S(2)}) collective-permute-start(bf16[1024,128]{1,0:T(8,128)(2,1)S(1)} %get-tuple-element.33.refs_3_), channel_id=1, source_target_pairs={{0,8},{4,12},{8,0},{12,4},{16,24},{20,28},{24,16},{28,20},{1,9},{5... | collective-permute-start | bytes 786440 | tf_op jit(solution)/shard_map/ppermute | solution.py:21
  8.5 14.8 %collective-permute-start.6 = (bf16[1024,128]{1,0:T(8,128)(2,1)S(1)}, bf16[1024,128]{1,0:T(8,128)(2,1)S(1)}, u32[]{:S(2)}, u32[]{:S(2)}) collective-permute-start(bf16[1024,128]{1,0:T(8,128)(2,1)S(1)} %get-tuple-element.32.refs_2_), channel_id=1, source_target_pairs={{0,16},{4,20},{8,24},{12,28},{16,0},{20,4},{24,8},{28,12},{1,17},{... | collective-permute-start | bytes 786440 | tf_op jit(solution)/shard_map/ppermute | solution.py:21
  10.5 16.3 %collective-permute-start.16 = (bf16[1024,128]{1,0:T(8,128)(2,1)S(1)}, bf16[1024,128]{1,0:T(8,128)(2,1)S(1)}, u32[]{:S(2)}, u32[]{:S(2)}) collective-permute-start(bf16[1024,128]{1,0:T(8,128)(2,1)S(1)} %get-tuple-element.36.refs_2_), channel_id=1, source_target_pairs={{0,8},{4,12},{8,0},{12,4},{16,24},{20,28},{24,16},{28,20},{1,9},{5... | collective-permute-start | bytes 786440 | tf_op jit(solution)/shard_map/ppermute | solution.py:21
  15.6 13.3 %collective-permute-start.18 = (bf16[1024,128]{1,0:T(8,128)(2,1)S(1)}, bf16[1024,128]{1,0:T(8,128)(2,1)S(1)}, u32[]{:S(2)}, u32[]{:S(2)}) collective-permute-start(bf16[1024,128]{1,0:T(8,128)(2,1)S(1)} %get-tuple-element.36.refs_2_), channel_id=1, source_target_pairs={{0,16},{4,20},{8,24},{12,28},{16,0},{20,4},{24,8},{28,12},{1,17},{... | collective-permute-start | bytes 786440 | tf_op jit(solution)/shard_map/ppermute | solution.py:21
  21.3 11.2 %collective-permute-start.17 = (bf16[1024,128]{1,0:T(8,128)(2,1)S(1)}, bf16[1024,128]{1,0:T(8,128)(2,1)S(1)}, u32[]{:S(2)}, u32[]{:S(2)}) collective-permute-start(bf16[1024,128]{1,0:T(8,128)(2,1)S(1)} %get-tuple-element.37.refs_3_), channel_id=1, source_target_pairs={{0,8},{4,12},{8,0},{12,4},{16,24},{20,28},{24,16},{28,20},{1,9},{5... | collective-permute-start | bytes 786440 | tf_op jit(solution)/shard_map/ppermute | solution.py:21
  23.3 11.3 %collective-permute-start.19 = (bf16[1024,128]{1,0:T(8,128)(2,1)S(1)}, bf16[1024,128]{1,0:T(8,128)(2,1)S(1)}, u32[]{:S(2)}, u32[]{:S(2)}) collective-permute-start(bf16[1024,128]{1,0:T(8,128)(2,1)S(1)} %get-tuple-element.37.refs_3_), channel_id=1, source_target_pairs={{0,16},{4,20},{8,24},{12,28},{16,0},{20,4},{24,8},{28,12},{1,17},{... | collective-permute-start | bytes 786440 | tf_op jit(solution)/shard_map/ppermute | solution.py:21
  26.9 11.2 %collective-permute-start.9 = (bf16[1024,128]{1,0:T(8,128)(2,1)S(1)}, bf16[1024,128]{1,0:T(8,128)(2,1)S(1)}, u32[]{:S(2)}, u32[]{:S(2)}) collective-permute-start(bf16[1024,128]{1,0:T(8,128)(2,1)S(1)} %collective-permute-done.6.refs_6_), channel_id=1, source_target_pairs={{0,8},{4,12},{8,0},{12,4},{16,24},{20,28},{24,16},{28,20},{1,9},{5... | collective-permute-start | bytes 786440 | tf_op jit(solution)/shard_map/ppermute | solution.py:21
  28.9 14.6 %collective-permute-start.21 = (bf16[1024,128]{1,0:T(8,128)(2,1)S(1)}, bf16[1024,128]{1,0:T(8,128)(2,1)S(1)}, u32[]{:S(2)}, u32[]{:S(2)}) collective-permute-start(bf16[1024,128]{1,0:T(8,128)(2,1)S(1)} %collective-permute-done.18.refs_6_), channel_id=1, source_target_pairs={{0,8},{4,12},{8,0},{12,4},{16,24},{20,28},{24,16},{28,20},{1,9},{5... | collective-permute-start | bytes 786440 | tf_op jit(solution)/shard_map/ppermute | solution.py:21
  32.5 11.1 %collective-permute-start.22 = (bf16[1024,128]{1,0:T(8,128)(2,1)S(1)}, bf16[1024,128]{1,0:T(8,128)(2,1)S(1)}, u32[]{:S(2)}, u32[]{:S(2)}) collective-permute-start(bf16[1024,128]{1,0:T(8,128)(2,1)S(1)} %collective-permute-done.17.refs_5_), channel_id=1, source_target_pairs={{0,16},{4,20},{8,24},{12,28},{16,0},{20,4},{24,8},{28,12},{1,17},{... | collective-permute-start | bytes 786440 | tf_op jit(solution)/shard_map/ppermute | solution.py:21
  34.5 12.8 %collective-permute-start.10 = (bf16[1024,128]{1,0:T(8,128)(2,1)S(1)}, bf16[1024,128]{1,0:T(8,128)(2,1)S(1)}, u32[]{:S(2)}, u32[]{:S(2)}) collective-permute-start(bf16[1024,128]{1,0:T(8,128)(2,1)S(1)} %collective-permute-done.5.refs_5_), channel_id=1, source_target_pairs={{0,16},{4,20},{8,24},{12,28},{16,0},{20,4},{24,8},{28,12},{1,17},{... | collective-permute-start | bytes 786440 | tf_op jit(solution)/shard_map/ppermute | solution.py:21
  38.1 13.6 %collective-permute-start.7 = (bf16[1024,128]{1,0:T(8,128)(2,1)S(1)}, bf16[1024,128]{1,0:T(8,128)(2,1)S(1)}, u32[]{:S(2)}, u32[]{:S(2)}) collective-permute-start(bf16[1024,128]{1,0:T(8,128)(2,1)S(1)} %get-tuple-element.33.refs_3_), channel_id=1, source_target_pairs={{0,16},{4,20},{8,24},{12,28},{16,0},{20,4},{24,8},{28,12},{1,17},{... | collective-permute-start | bytes 786440 | tf_op jit(solution)/shard_map/ppermute | solution.py:21
  43.6 8.1 %collective-permute-start.23 = (bf16[1024,128]{1,0:T(8,128)(2,1)S(1)}, bf16[1024,128]{1,0:T(8,128)(2,1)S(1)}, u32[]{:S(2)}, u32[]{:S(2)}) collective-permute-start(bf16[1024,128]{1,0:T(8,128)(2,1)S(1)} %collective-permute-done.21.refs_2_), channel_id=1, source_target_pairs={{0,4},{4,0},{8,12},{12,8},{16,20},{20,16},{24,28},{28,24},{1,5},{5... | collective-permute-start | bytes 786440 | tf_op jit(solution)/shard_map/ppermute | solution.py:21
  43.6 9.8 %collective-permute-start.24 = (bf16[1024,128]{1,0:T(8,128)(2,1)S(1)}, bf16[1024,128]{1,0:T(8,128)(2,1)S(1)}, u32[]{:S(2)}, u32[]{:S(2)}) collective-permute-start(bf16[1024,128]{1,0:T(8,128)(2,1)S(1)} %collective-permute-done.22.refs_3_), channel_id=1, source_target_pairs={{0,4},{4,0},{8,12},{12,8},{16,20},{20,16},{24,28},{28,24},{1,5},{5... | collective-permute-start | bytes 786440 | tf_op jit(solution)/shard_map/ppermute | solution.py:21
  47.3 16.5 %collective-permute-start.11 = (bf16[1024,128]{1,0:T(8,128)(2,1)S(1)}, bf16[1024,128]{1,0:T(8,128)(2,1)S(1)}, u32[]{:S(2)}, u32[]{:S(2)}) collective-permute-start(bf16[1024,128]{1,0:T(8,128)(2,1)S(1)} %collective-permute-done.9.refs_2_), channel_id=1, source_target_pairs={{0,4},{4,0},{8,12},{12,8},{16,20},{20,16},{24,28},{28,24},{1,5},{5... | collective-permute-start | bytes 786440 | tf_op jit(solution)/shard_map/ppermute | solution.py:21
  47.3 16.8 %collective-permute-start.12 = (bf16[1024,128]{1,0:T(8,128)(2,1)S(1)}, bf16[1024,128]{1,0:T(8,128)(2,1)S(1)}, u32[]{:S(2)}, u32[]{:S(2)}) collective-permute-start(bf16[1024,128]{1,0:T(8,128)(2,1)S(1)} %collective-permute-done.10.refs_3_), channel_id=1, source_target_pairs={{0,4},{4,0},{8,12},{12,8},{16,20},{20,16},{24,28},{28,24},{1,5},{5... | collective-permute-start | bytes 786440 | tf_op jit(solution)/shard_map/ppermute | solution.py:21
  51.7 6.9 %collective-permute-start.20 = (bf16[3,128,128]{2,1,0:T(8,128)(2,1)S(1)}, bf16[3,128,128]{2,1,0:T(8,128)(2,1)S(1)}, u32[]{:S(2)}, u32[]{:S(2)}) collective-permute-start(bf16[3,128,128]{2,1,0:T(8,128)(2,1)S(1)} %get-tuple-element.39), channel_id=1, source_target_pairs={{0,4},{4,0},{8,12},{12,8},{16,20},{20,16},{24,28},{28,24},{1,5},{5... | collective-permute-start | bytes 294920 | tf_op jit(solution)/shard_map/ppermute | solution.py:21
  51.7 6.3 %copy-start.2 = (bf16[1024,128]{1,0:T(8,128)(2,1)}, bf16[1024,128]{1,0:T(8,128)(2,1)S(1)}, u32[]{:S(2)}) copy-start(bf16[1024,128]{1,0:T(8,128)(2,1)S(1)} %collective-permute-done.23.refs_4_) | copy-start | bytes 786436
  51.7 16.7 %collective-permute-start = (bf16[2,512,128]{2,1,0:T(8,128)(2,1)}, bf16[2,512,128]{2,1,0:T(8,128)(2,1)S(1)}, u32[]{:S(2)}, u32[]{:S(2)}) collective-permute-start(bf16[2,512,128]{2,1,0:T(8,128)(2,1)} %get-tuple-element.28), channel_id=1, source_target_pairs={{0,1},{1,0},{2,3},{3,2},{4,5},{5,4},{6,7},{7,6},{8,9},{9,8},{10,11... | collective-permute-start | bytes 786440 | tf_op jit(solution)/shard_map/ppermute | solution.py:21
  53.3 0.7 copy-start.4
  54.0 35.7 %collective-permute-start.1 = (bf16[2,512,128]{2,1,0:T(8,128)(2,1)}, bf16[2,512,128]{2,1,0:T(8,128)(2,1)S(1)}, u32[]{:S(2)}, u32[]{:S(2)}) collective-permute-start(bf16[2,512,128]{2,1,0:T(8,128)(2,1)} %get-tuple-element.29), channel_id=1, source_target_pairs={{0,2},{1,3},{2,0},{3,1},{4,6},{5,7},{6,4},{7,5},{8,10},{9,11},{10,... | collective-permute-start | bytes 786440 | tf_op jit(solution)/shard_map/ppermute | solution.py:21
  58.0 0.6 copy-start.6
  58.6 0.6 copy-start.8
  59.2 6.6 %collective-permute-start.8 = (bf16[3,128,128]{2,1,0:T(8,128)(2,1)}, bf16[3,128,128]{2,1,0:T(8,128)(2,1)}, u32[]{:S(2)}, u32[]{:S(2)}) collective-permute-start(bf16[3,128,128]{2,1,0:T(8,128)(2,1)} %get-tuple-element.35), channel_id=1, source_target_pairs={{0,4},{4,0},{8,12},{12,8},{16,20},{20,16},{24,28},{28,24},{1,5},{5... | collective-permute-start | bytes 294920 | tf_op jit(solution)/shard_map/ppermute | solution.py:21
  59.2 0.7 copy-start.12
  60.1 1.0 copy-start.3
  61.1 0.9 copy-start.5
  62.0 0.9 copy-start.9
  62.9 0.9 copy-start.11
  62.9 2.9 %copy-start.7 = (bf16[3,128,128]{2,1,0:T(8,128)(2,1)S(1)}, bf16[3,128,128]{2,1,0:T(8,128)(2,1)}, u32[]{:S(2)}) copy-start(bf16[3,128,128]{2,1,0:T(8,128)(2,1)} %copy-done.6) | copy-start | bytes 294916
  63.9 27.9 %collective-permute-start.2 = (bf16[2,512,128]{2,1,0:T(8,128)(2,1)S(1)}, bf16[2,512,128]{2,1,0:T(8,128)(2,1)S(1)}, u32[]{:S(2)}, u32[]{:S(2)}) collective-permute-start(bf16[2,512,128]{2,1,0:T(8,128)(2,1)S(1)} %copy-done.11), channel_id=1, source_target_pairs={{0,3},{1,2},{2,1},{3,0},{4,7},{5,6},{6,5},{7,4},{8,11},{9,10},{10,... | collective-permute-start | bytes 786440 | tf_op jit(solution)/shard_map/ppermute | solution.py:21
  64.1 25.6 %collective-permute-start.26 = (bf16[128,512]{1,0:T(8,128)(2,1)S(1)}, bf16[128,512]{1,0:T(8,128)(2,1)S(1)}, u32[]{:S(2)}, u32[]{:S(2)}) collective-permute-start(bf16[128,512]{1,0:T(8,128)(2,1)S(1)} %shard_map.64.refs_4_), channel_id=1, source_target_pairs={{0,2},{1,3},{2,0},{3,1},{4,6},{5,7},{6,4},{7,5},{8,10},{9,11},{10,... | collective-permute-start | bytes 393224 | tf_op jit(solution)/shard_map/ppermute | solution.py:21
  67.0 24.8 %collective-permute-start.14 = (bf16[128,512]{1,0:T(8,128)(2,1)S(1)}, bf16[128,512]{1,0:T(8,128)(2,1)S(1)}, u32[]{:S(2)}, u32[]{:S(2)}) collective-permute-start(bf16[128,512]{1,0:T(8,128)(2,1)S(1)} %shard_map.62.refs_4_), channel_id=1, source_target_pairs={{0,2},{1,3},{2,0},{3,1},{4,6},{5,7},{6,4},{7,5},{8,10},{9,11},{10,... | collective-permute-start | bytes 393224 | tf_op jit(solution)/shard_map/ppermute | solution.py:21
  68.4 23.4 %collective-permute-start.25 = (bf16[128,512]{1,0:T(8,128)(2,1)S(1)}, bf16[128,512]{1,0:T(8,128)(2,1)S(1)}, u32[]{:S(2)}, u32[]{:S(2)}) collective-permute-start(bf16[128,512]{1,0:T(8,128)(2,1)S(1)} %shard_map.64.refs_4_), channel_id=1, source_target_pairs={{0,1},{1,0},{2,3},{3,2},{4,5},{5,4},{6,7},{7,6},{8,9},{9,8},{10,11... | collective-permute-start | bytes 393224 | tf_op jit(solution)/shard_map/ppermute | solution.py:21
  89.7 6.4 %collective-permute-start.27 = (bf16[128,512]{1,0:T(8,128)(2,1)S(1)}, bf16[128,512]{1,0:T(8,128)(2,1)S(1)}, u32[]{:S(2)}, u32[]{:S(2)}) collective-permute-start(bf16[128,512]{1,0:T(8,128)(2,1)S(1)} %collective-permute-done.26.refs_6_), channel_id=1, source_target_pairs={{0,1},{1,0},{2,3},{3,2},{4,5},{5,4},{6,7},{7,6},{8,9},{9,8},{10,11... | collective-permute-start | bytes 393224 | tf_op jit(solution)/shard_map/ppermute | solution.py:21
  89.7 9.0 %collective-permute-start.13 = (bf16[128,512]{1,0:T(8,128)(2,1)S(1)}, bf16[128,512]{1,0:T(8,128)(2,1)S(1)}, u32[]{:S(2)}, u32[]{:S(2)}) collective-permute-start(bf16[128,512]{1,0:T(8,128)(2,1)S(1)} %shard_map.62.refs_4_), channel_id=1, source_target_pairs={{0,1},{1,0},{2,3},{3,2},{4,5},{5,4},{6,7},{7,6},{8,9},{9,8},{10,11... | collective-permute-start | bytes 393224 | tf_op jit(solution)/shard_map/ppermute | solution.py:21
  91.8 8.3 %collective-permute-start.15 = (bf16[128,512]{1,0:T(8,128)(2,1)S(1)}, bf16[128,512]{1,0:T(8,128)(2,1)S(1)}, u32[]{:S(2)}, u32[]{:S(2)}) collective-permute-start(bf16[128,512]{1,0:T(8,128)(2,1)S(1)} %collective-permute-done.14.refs_6_), channel_id=1, source_target_pairs={{0,1},{1,0},{2,3},{3,2},{4,5},{5,4},{6,7},{7,6},{8,9},{9,8},{10,11... | collective-permute-start | bytes 393224 | tf_op jit(solution)/shard_map/ppermute | solution.py:21
  101.7 5.2 %collective-permute-start.28 = (f32[4,72,128]{2,1,0:T(8,128)S(1)}, f32[4,72,128]{2,1,0:T(8,128)S(1)}, u32[]{:S(2)}, u32[]{:S(2)}) collective-permute-start(f32[4,72,128]{2,1,0:T(8,128)S(1)} %get-tuple-element.40), channel_id=1, source_target_pairs={{0,1},{1,0},{2,3},{3,2},{4,5},{5,4},{6,7},{7,6},{8,9},{9,8},{10,11... | collective-permute-start | bytes 442376 | tf_op jit(solution)/shard_map/ppermute | solution.py:21
  106.9 7.2 %collective-permute-start.29 = (f32[4,72,128]{2,1,0:T(8,128)S(1)}, f32[4,72,128]{2,1,0:T(8,128)S(1)}, u32[]{:S(2)}, u32[]{:S(2)}) collective-permute-start(f32[4,72,128]{2,1,0:T(8,128)S(1)} %add.8.own_ref), channel_id=1, source_target_pairs={{0,2},{1,3},{2,0},{3,1},{4,6},{5,7},{6,4},{7,5},{8,10},{9,11},{10,... | collective-permute-start | bytes 442376 | tf_op jit(solution)/shard_map/ppermute | solution.py:21
